TPU v7x, 32 devices: a whole 2x2x4 slice. The times are simulated.
32 devices in a mesh: groups: 2 (over y), ctx: 8 (over z, x), tp: 2 (over core).
Axes of the slice: x: 2, y: 2, z: 4, core: 2. Of those that a mesh axis runs over, the one named last changes fastest.
Arguments:
- normed_input: bfloat16 [4096, 2688], P(('groups', 'ctx')), parts along dimension 0, may hold values from -6 to 6
- attn_queries: bfloat16 [4096, 2048], P(('groups', 'ctx'), 'tp'), parts along dimension 0, may hold values from -45 to 45
- attn_keys: bfloat16 [4096, 1024], P(('groups', 'ctx'), 'tp'), parts along dimension 0, may hold values from -9 to 9
- attn_values: bfloat16 [4096, 1024], P(('groups', 'ctx'), 'tp'), parts along dimension 0, may hold values from -6 to 6
- out_grad: bfloat16 [4096, 2048], P(('groups', 'ctx'), 'tp'), parts along dimension 0, may hold values from -6 to 6
Outputs:
- query_grad: bfloat16 [4096, 2048], P(('groups', 'ctx'), 'tp'), parts along dimension 0
- key_weight_grad: float32 [5376, 1024], P(('groups', 'ctx'), 'tp'), parts along dimension 0
- value_grad: bfloat16 [4096, 1024], P(('groups', 'ctx'), 'tp'), parts along dimension 0
There are 2 independent parts, one for each index of `groups`. A program takes and returns all parts, laid end to end along the dimension named above; each array names one. Nothing has to cross between parts.
All inputs are finite; a program needn't handle non-finite values.
Results may differ from a plain program's by a relative error of at most 0.0053.
Values may be sent and summed in bfloat16 or wider, within the bound.
No kernel may reach another device: no remote copies, remote signals or barrier semaphores. Data moves between devices by JAX's collectives and lax.ppermute only.
A program may use at most 128 MiB of HBM per device.

v0:
```python
import jax
import jax.numpy as jnp
from jax import lax
from jax.sharding import PartitionSpec as P

HD = 128
HQ = 16
HK = 8
W = 1024


attn_scale = 168.0 ** (-0.5)


def shifted(value, axis, steps):
    count = lax.axis_size(axis)
    first, last = (max(0, -steps), min(count, count - steps))
    return lax.ppermute(value, axis, [(source, source + steps) for source in range(first, last)])


def head_block(query_head, grad_head, key_head, value_head, allowed):
    scores = attn_scale * jnp.einsum(
        "qgd,kd->gqk", query_head, key_head, preferred_element_type=jnp.float32
    )
    scores = jnp.where(allowed, scores, -jnp.inf)
    row_max = jnp.max(scores, axis=-1, keepdims=True)
    raised = jnp.exp(scores - row_max)
    soft_weights = raised / jnp.sum(raised, axis=-1, keepdims=True)
    soft_low = soft_weights.astype(jnp.bfloat16)
    grad_probs = jnp.einsum(
        "qgd,kd->gqk", grad_head, value_head, preferred_element_type=jnp.float32
    )
    row_delta = jnp.sum(soft_weights * grad_probs, axis=-1, keepdims=True)
    grad_scores = (soft_weights * (grad_probs - row_delta)).astype(jnp.bfloat16)
    grad_query = attn_scale * jnp.einsum(
        "gqk,kd->qgd", grad_scores, key_head, preferred_element_type=jnp.float32
    )
    grad_key = attn_scale * jnp.einsum(
        "gqk,qgd->kd", grad_scores, query_head, preferred_element_type=jnp.float32
    )
    grad_value = jnp.einsum("gqk,qgd->kd", soft_low, grad_head, preferred_element_type=jnp.float32)
    return (grad_query.astype(jnp.bfloat16), grad_key, grad_value)


def shards(normed_input, attn_queries, attn_keys, attn_values, out_grad):
    tokens_here = attn_queries.shape[0]
    kv_width = attn_keys.shape[1]
    heads_here = kv_width // HD
    group_size = HQ // HK
    reach_count = max(1, W // tokens_here)
    edge_rows = min(W, tokens_here)
    block_rows = min(512, tokens_here)
    window_rows = block_rows + W
    halo_keys = []
    halo_values = []
    for distance in range(reach_count, 0, -1):
        far_keys, far_values = shifted((attn_keys, attn_values), "ctx", distance)
        halo_keys.append(far_keys)
        halo_values.append(far_values)
    every_key = jnp.concatenate(halo_keys + [attn_keys], axis=0)
    every_value = jnp.concatenate(halo_values + [attn_values], axis=0)
    first_row = lax.axis_index("ctx") * tokens_here
    query_offsets = jnp.arange(block_rows, dtype=jnp.int32)
    key_offsets = jnp.arange(window_rows, dtype=jnp.int32)
    key_grads = [jnp.zeros((W + tokens_here, HD), jnp.float32) for head_index in range(heads_here)]
    value_grads = [
        jnp.zeros((W + tokens_here, HD), jnp.float32) for head_index in range(heads_here)
    ]
    query_pos = first_row + 0 + query_offsets
    key_pos = first_row + 0 - W + key_offsets
    distance_back = query_pos[:, None] - key_pos[None, :]
    allowed = (distance_back >= 0) & (distance_back < W) & (key_pos[None, :] >= 0)
    columns = []
    for head_index in range(heads_here):
        query_cols = slice(head_index * group_size * HD, (head_index + 1) * group_size * HD)
        kv_cols = slice(head_index * HD, (head_index + 1) * HD)
        query_head = attn_queries[0:block_rows, query_cols].reshape(block_rows, group_size, HD)
        grad_head = out_grad[0:block_rows, query_cols].reshape(block_rows, group_size, HD)
        key_head = every_key[0:window_rows, kv_cols]
        value_head = every_value[0:window_rows, kv_cols]
        grad_query, grad_key, grad_value = head_block(
            query_head, grad_head, key_head, value_head, allowed
        )
        columns.append(grad_query.reshape(block_rows, group_size * HD))
        key_grads[head_index] = key_grads[head_index].at[0:window_rows].add(grad_key)
        value_grads[head_index] = value_grads[head_index].at[0:window_rows].add(grad_value)
    query_rows = jnp.concatenate(columns, axis=1)
    key_total = jnp.concatenate(key_grads, axis=1)
    value_total = jnp.concatenate(value_grads, axis=1)
    own_keys = key_total[W:]
    own_values = value_total[W:]
    for distance in range(1, reach_count + 1):
        slot_index = reach_count - distance
        back_keys, back_values = shifted(
            (
                key_total[slot_index * edge_rows : (slot_index + 1) * edge_rows],
                value_total[slot_index * edge_rows : (slot_index + 1) * edge_rows],
            ),
            "ctx",
            -distance,
        )
        own_keys = own_keys.at[tokens_here - edge_rows :].add(back_keys)
        own_values = own_values.at[tokens_here - edge_rows :].add(back_values)
    key_low = own_keys.astype(jnp.bfloat16)
    value_low = own_values.astype(jnp.bfloat16)
    contract = (((0,), (0,)), ((), ()))
    partial_term = lax.dot_general(
        normed_input, key_low, contract, preferred_element_type=jnp.float32
    )
    summed = lax.psum_scatter(partial_term, "ctx", scatter_dimension=0, tiled=True)
    return (query_rows, summed, value_low)


def solution(mesh):
    return jax.shard_map(
        shards,
        mesh=mesh,
        in_specs=(
            P(("groups", "ctx"), None),
            P(("groups", "ctx"), "tp"),
            P(("groups", "ctx"), "tp"),
            P(("groups", "ctx"), "tp"),
            P(("groups", "ctx"), "tp"),
        ),
        out_specs=(
            P(("groups", "ctx"), "tp"),
            P(("groups", "ctx"), "tp"),
            P(("groups", "ctx"), "tp"),
        ),
        check_vma=False,
    )
```

profile of v0, /device:TPU:0, one launch (start us, length us, event | category | flops | bytes accessed | tf_op | source)
XLA Modules:
  0.0 363.5 jit_solution(14561726327072352522)
XLA Ops:
  7.2 5.8 %collective-permute-start.2 = (bf16[256,512]{1,0:T(8,128)(2,1)}, bf16[256,512]{1,0:T(8,128)(2,1)}, u32[]{:S(2)}, u32[]{:S(2)}) collective-permute-start(bf16[256,512]{1,0:T(8,128)(2,1)} %param.71), channel_id=1, source_target_pairs={{0,4},{2,6},{4,8},{6,10},{8,12},{10,14},{1,5},{3,7},{5,9},{7,11},{... | collective-permute-start | bytes 786440 | tf_op jit(solution)/shard_map/ppermute | solution.py:18
  13.0 4.4 %collective-permute-start.1 = (bf16[256,512]{1,0:T(8,128)(2,1)}, bf16[256,512]{1,0:T(8,128)(2,1)}, u32[]{:S(2)}, u32[]{:S(2)}) collective-permute-start(bf16[256,512]{1,0:T(8,128)(2,1)} %param.71), channel_id=1, source_target_pairs={{0,6},{2,8},{4,10},{6,12},{8,14},{1,7},{3,9},{5,11},{7,13},{9,15},... | collective-permute-start | bytes 786440 | tf_op jit(solution)/shard_map/ppermute | solution.py:18
  17.5 3.5 collective-permute-start.6
  33.0 7.7 %collective-permute-done.4 = bf16[256,512]{1,0:T(8,128)(2,1)} collective-permute-done((bf16[256,512]{1,0:T(8,128)(2,1)}, bf16[256,512]{1,0:T(8,128)(2,1)}, u32[]{:S(2)}, u32[]{:S(2)}) %collective-permute-start.4) | collective-permute-done | bytes 262176 | tf_op jit(solution)/shard_map/ppermute | solution.py:18
  40.7 3.4 collective-permute-start.7
  45.2 5.3 %collective-permute-start = (bf16[256,512]{1,0:T(8,128)(2,1)}, bf16[256,512]{1,0:T(8,128)(2,1)S(1)}, u32[]{:S(2)}, u32[]{:S(2)}) collective-permute-start(bf16[256,512]{1,0:T(8,128)(2,1)} %param.71), channel_id=1, source_target_pairs={{0,8},{2,10},{4,12},{6,14},{1,9},{3,11},{5,13},{7,15},{16,24},{18,... | collective-permute-start | bytes 786440 | tf_op jit(solution)/shard_map/ppermute | solution.py:18
  50.5 8.9 %collective-permute-start.3 = (bf16[256,512]{1,0:T(8,128)(2,1)}, bf16[256,512]{1,0:T(8,128)(2,1)S(1)}, u32[]{:S(2)}, u32[]{:S(2)}) collective-permute-start(bf16[256,512]{1,0:T(8,128)(2,1)} %param.71), channel_id=1, source_target_pairs={{0,2},{2,4},{4,6},{6,8},{8,10},{10,12},{12,14},{1,3},{3,5},{5,7},{... | collective-permute-start | bytes 786440 | tf_op jit(solution)/shard_map/ppermute | solution.py:18
  71.5 3.5 fusion.61
  75.0 2.6 multiply_reduce_fusion.2
  80.7 3.5 fusion.60
  84.2 2.6 multiply_reduce_fusion.1
  89.7 3.5 fusion.59
  93.3 2.6 multiply_reduce_fusion
  103.8 35.6 %collective-permute-done.8 = f32[256,512]{0,1:T(8,128)S(1)} collective-permute-done((f32[256,512]{0,1:T(8,128)S(1)}, f32[256,512]{0,1:T(8,128)S(1)}, u32[]{:S(2)}, u32[]{:S(2)}) %collective-permute-start.8) | collective-permute-done | bytes 524320 | tf_op jit(solution)/shard_map/ppermute | solution.py:18
  139.4 29.3 %collective-permute-done.11 = f32[256,512]{0,1:T(8,128)S(1)} collective-permute-done((f32[256,512]{0,1:T(8,128)S(1)}, f32[256,512]{0,1:T(8,128)S(1)}, u32[]{:S(2)}, u32[]{:S(2)}) %collective-permute-start.11) | collective-permute-done | bytes 524320 | tf_op jit(solution)/shard_map/ppermute | solution.py:18
  168.7 3.5 convolution_bitcast_fusion
  172.1 6.2 %copy.142 = f32[2688,512]{1,0:T(8,128)} copy(f32[2688,512]{0,1:T(8,128)} %convolution_bitcast_fusion) | data formatting | bytes 11010048
  179.3 2.6 convolution_bitcast_fusion.8
  181.9 2.6 convolution_bitcast_fusion.7
  184.5 2.6 convolution_bitcast_fusion.6
  187.1 3.5 convolution_bitcast_fusion.5
  203.1 20.9 %collective-permute-done.12 = f32[256,512]{0,1:T(8,128)S(1)} collective-permute-done((f32[256,512]{0,1:T(8,128)}, f32[256,512]{0,1:T(8,128)S(1)}, u32[]{:S(2)}, u32[]{:S(2)}) %collective-permute-start.12) | collective-permute-done | bytes 524320 | tf_op jit(solution)/shard_map/ppermute | solution.py:18
  224.0 71.5 %collective-permute-done.15 = f32[256,512]{0,1:T(8,128)} collective-permute-done((f32[256,512]{0,1:T(8,128)}, f32[256,512]{0,1:T(8,128)}, u32[]{:S(2)}, u32[]{:S(2)}) %collective-permute-start.15) | collective-permute-done | bytes 524320 | tf_op jit(solution)/shard_map/ppermute | solution.py:18
  298.0 58.6 %reduce-scatter.4.cloned.1.call-done = f32[336,512]{1,0:T(8,128)} async-done(((f32[2688,512]{1,0:T(8,128)}), f32[336,512]{1,0:T(8,128)}) %reduce-scatter.4.cloned.1.call-update) | async-done | bytes 688144
  (128 shorter events, 54.6 us)
Async XLA Ops:
  7.2 161.5 %copy-start = (bf16[256,2688]{1,0:T(8,128)(2,1)S(1)}, bf16[256,2688]{1,0:T(8,128)(2,1)}, u32[]{:S(2)}) copy-start(bf16[256,2688]{1,0:T(8,128)(2,1)} %param.69) | copy-start | bytes 4128772
  7.2 33.5 %copy-start.23 = (bf16[256,512]{1,0:T(8,128)(2,1)S(1)}, bf16[256,512]{1,0:T(8,128)(2,1)}, u32[]{:S(2)}) copy-start(bf16[256,512]{1,0:T(8,128)(2,1)} %param.72) | copy-start | bytes 786436
  7.2 349.5 %reduce-scatter.4.cloned.1.call-start = ((), (), s32[]{:S(2)}) async-start(), calls=%async_computation.1 | async-start | bytes 6193152
  7.2 53.6 %collective-permute-start.2 = (bf16[256,512]{1,0:T(8,128)(2,1)}, bf16[256,512]{1,0:T(8,128)(2,1)}, u32[]{:S(2)}, u32[]{:S(2)}) collective-permute-start(bf16[256,512]{1,0:T(8,128)(2,1)} %param.71), channel_id=1, source_target_pairs={{0,4},{2,6},{4,8},{6,10},{8,12},{10,14},{1,5},{3,7},{5,9},{7,11},{... | collective-permute-start | bytes 786440 | tf_op jit(solution)/shard_map/ppermute | solution.py:18
  13.0 46.6 %collective-permute-start.1 = (bf16[256,512]{1,0:T(8,128)(2,1)}, bf16[256,512]{1,0:T(8,128)(2,1)}, u32[]{:S(2)}, u32[]{:S(2)}) collective-permute-start(bf16[256,512]{1,0:T(8,128)(2,1)} %param.71), channel_id=1, source_target_pairs={{0,6},{2,8},{4,10},{6,12},{8,14},{1,7},{3,9},{5,11},{7,13},{9,15},... | collective-permute-start | bytes 786440 | tf_op jit(solution)/shard_map/ppermute | solution.py:18
  17.5 33.1 %collective-permute-start.6 = (bf16[256,512]{1,0:T(8,128)(2,1)}, bf16[256,512]{1,0:T(8,128)(2,1)S(1)}, u32[]{:S(2)}, u32[]{:S(2)}) collective-permute-start(bf16[256,512]{1,0:T(8,128)(2,1)} %param.72), channel_id=1, source_target_pairs={{0,4},{2,6},{4,8},{6,10},{8,12},{10,14},{1,5},{3,7},{5,9},{7,11},{... | collective-permute-start | bytes 786440 | tf_op jit(solution)/shard_map/ppermute | solution.py:18
  21.0 24.2 %collective-permute-start.5 = (bf16[256,512]{1,0:T(8,128)(2,1)}, bf16[256,512]{1,0:T(8,128)(2,1)S(1)}, u32[]{:S(2)}, u32[]{:S(2)}) collective-permute-start(bf16[256,512]{1,0:T(8,128)(2,1)} %param.72), channel_id=1, source_target_pairs={{0,6},{2,8},{4,10},{6,12},{8,14},{1,7},{3,9},{5,11},{7,13},{9,15},... | collective-permute-start | bytes 786440 | tf_op jit(solution)/shard_map/ppermute | solution.py:18
  22.3 18.4 %collective-permute-start.4 = (bf16[256,512]{1,0:T(8,128)(2,1)}, bf16[256,512]{1,0:T(8,128)(2,1)}, u32[]{:S(2)}, u32[]{:S(2)}) collective-permute-start(bf16[256,512]{1,0:T(8,128)(2,1)} %param.72), channel_id=1, source_target_pairs={{0,8},{2,10},{4,12},{6,14},{1,9},{3,11},{5,13},{7,15},{16,24},{18,... | collective-permute-start | bytes 786440 | tf_op jit(solution)/shard_map/ppermute | solution.py:18
  28.3 36.6 %copy-start.17 = (bf16[256,256]{0,1:T(8,128)(2,1)}, bf16[256,256]{0,1:T(8,128)(2,1)S(1)}, u32[]{:S(2)}) copy-start(bf16[256,256]{0,1:T(8,128)(2,1)S(1)} %copy.144) | copy-start | bytes 393220
  33.0 32.0 %copy-start.22 = (pred[256,1280]{0,1:T(8,128)(4,1)S(1)}, pred[256,1280]{0,1:T(8,128)(4,1)}, u32[]{:S(2)}) copy-start(pred[256,1280]{0,1:T(8,128)(4,1)} %fusion.29) | copy-start | bytes 983044
  40.7 18.8 %collective-permute-start.7 = (bf16[256,512]{1,0:T(8,128)(2,1)S(1)}, bf16[256,512]{1,0:T(8,128)(2,1)S(1)}, u32[]{:S(2)}, u32[]{:S(2)}) collective-permute-start(bf16[256,512]{1,0:T(8,128)(2,1)S(1)} %copy-done.23), channel_id=1, source_target_pairs={{0,2},{2,4},{4,6},{6,8},{8,10},{10,12},{12,14},{1,3},{3,5},{5,7},{... | collective-permute-start | bytes 786440 | tf_op jit(solution)/shard_map/ppermute | solution.py:18
  45.2 14.4 %collective-permute-start = (bf16[256,512]{1,0:T(8,128)(2,1)}, bf16[256,512]{1,0:T(8,128)(2,1)S(1)}, u32[]{:S(2)}, u32[]{:S(2)}) collective-permute-start(bf16[256,512]{1,0:T(8,128)(2,1)} %param.71), channel_id=1, source_target_pairs={{0,8},{2,10},{4,12},{6,14},{1,9},{3,11},{5,13},{7,15},{16,24},{18,... | collective-permute-start | bytes 786440 | tf_op jit(solution)/shard_map/ppermute | solution.py:18
  50.5 13.4 %collective-permute-start.3 = (bf16[256,512]{1,0:T(8,128)(2,1)}, bf16[256,512]{1,0:T(8,128)(2,1)S(1)}, u32[]{:S(2)}, u32[]{:S(2)}) collective-permute-start(bf16[256,512]{1,0:T(8,128)(2,1)} %param.71), channel_id=1, source_target_pairs={{0,2},{2,4},{4,6},{6,8},{8,10},{10,12},{12,14},{1,3},{3,5},{5,7},{... | collective-permute-start | bytes 786440 | tf_op jit(solution)/shard_map/ppermute | solution.py:18
  98.4 41.0 %collective-permute-start.8 = (f32[256,512]{0,1:T(8,128)S(1)}, f32[256,512]{0,1:T(8,128)S(1)}, u32[]{:S(2)}, u32[]{:S(2)}) collective-permute-start(f32[256,512]{0,1:T(8,128)S(1)} %get-tuple-element.336), channel_id=1, source_target_pairs={{2,0},{4,2},{6,4},{8,6},{10,8},{12,10},{14,12},{3,1},{5,3},{7,5},{... | collective-permute-start | bytes 1572872 | tf_op jit(solution)/shard_map/ppermute | solution.py:18
  99.7 69.0 %collective-permute-start.11 = (f32[256,512]{0,1:T(8,128)S(1)}, f32[256,512]{0,1:T(8,128)S(1)}, u32[]{:S(2)}, u32[]{:S(2)}) collective-permute-start(f32[256,512]{0,1:T(8,128)S(1)} %get-tuple-element.337), channel_id=1, source_target_pairs={{8,0},{10,2},{12,4},{14,6},{9,1},{11,3},{13,5},{15,7},{24,16},{26,... | collective-permute-start | bytes 1572872 | tf_op jit(solution)/shard_map/ppermute | solution.py:18
  101.0 67.7 %collective-permute-start.10 = (f32[256,512]{0,1:T(8,128)S(1)}, f32[256,512]{0,1:T(8,128)S(1)}, u32[]{:S(2)}, u32[]{:S(2)}) collective-permute-start(f32[256,512]{0,1:T(8,128)S(1)} %get-tuple-element.338), channel_id=1, source_target_pairs={{6,0},{8,2},{10,4},{12,6},{14,8},{7,1},{9,3},{11,5},{13,7},{15,9},... | collective-permute-start | bytes 1572872 | tf_op jit(solution)/shard_map/ppermute | solution.py:18
  102.3 66.4 %collective-permute-start.9 = (f32[256,512]{0,1:T(8,128)S(1)}, f32[256,512]{0,1:T(8,128)S(1)}, u32[]{:S(2)}, u32[]{:S(2)}) collective-permute-start(f32[256,512]{0,1:T(8,128)S(1)} %get-tuple-element.339), channel_id=1, source_target_pairs={{4,0},{6,2},{8,4},{10,6},{12,8},{14,10},{5,1},{7,3},{9,5},{11,7},{... | collective-permute-start | bytes 1572872 | tf_op jit(solution)/shard_map/ppermute | solution.py:18
  191.9 7.2 %copy-start.7 = (f32[1280,512]{0,1:T(8,128)}, f32[1280,512]{0,1:T(8,128)S(1)}, u32[]{:S(2)}) copy-start(f32[1280,512]{0,1:T(8,128)S(1)} %pad_maximum_fusion.1) | copy-start | bytes 7864324
  191.9 7.2 %copy-start.3 = (bf16[2,256,1280]{1,2,0:T(8,128)(2,1)S(1)}, bf16[2,256,1280]{1,2,0:T(8,128)(2,1)}, u32[]{:S(2)}) copy-start(bf16[2,256,1280]{1,2,0:T(8,128)(2,1)} %copy-done.2) | copy-start | bytes 3932164
  193.3 30.8 %collective-permute-start.12 = (f32[256,512]{0,1:T(8,128)}, f32[256,512]{0,1:T(8,128)S(1)}, u32[]{:S(2)}, u32[]{:S(2)}) collective-permute-start(f32[256,512]{0,1:T(8,128)} %get-tuple-element.332), channel_id=1, source_target_pairs={{2,0},{4,2},{6,4},{8,6},{10,8},{12,10},{14,12},{3,1},{5,3},{7,5},{... | collective-permute-start | bytes 1572872 | tf_op jit(solution)/shard_map/ppermute | solution.py:18
  194.8 100.7 %collective-permute-start.15 = (f32[256,512]{0,1:T(8,128)}, f32[256,512]{0,1:T(8,128)}, u32[]{:S(2)}, u32[]{:S(2)}) collective-permute-start(f32[256,512]{0,1:T(8,128)} %get-tuple-element.333), channel_id=1, source_target_pairs={{8,0},{10,2},{12,4},{14,6},{9,1},{11,3},{13,5},{15,7},{24,16},{26,... | collective-permute-start | bytes 1572872 | tf_op jit(solution)/shard_map/ppermute | solution.py:18
  196.1 99.4 %collective-permute-start.14 = (f32[256,512]{0,1:T(8,128)}, f32[256,512]{0,1:T(8,128)}, u32[]{:S(2)}, u32[]{:S(2)}) collective-permute-start(f32[256,512]{0,1:T(8,128)} %get-tuple-element.334), channel_id=1, source_target_pairs={{6,0},{8,2},{10,4},{12,6},{14,8},{7,1},{9,3},{11,5},{13,7},{15,9},... | collective-permute-start | bytes 1572872 | tf_op jit(solution)/shard_map/ppermute | solution.py:18
  197.4 98.1 %collective-permute-start.13 = (f32[256,512]{0,1:T(8,128)}, f32[256,512]{0,1:T(8,128)}, u32[]{:S(2)}, u32[]{:S(2)}) collective-permute-start(f32[256,512]{0,1:T(8,128)} %get-tuple-element.335), channel_id=1, source_target_pairs={{4,0},{6,2},{8,4},{10,6},{12,8},{14,10},{5,1},{7,3},{9,5},{11,7},{... | collective-permute-start | bytes 1572872 | tf_op jit(solution)/shard_map/ppermute | solution.py:18
  200.2 156.5 %copy-start.1 = (bf16[256,2688]{1,0:T(8,128)(2,1)S(1)}, bf16[256,2688]{1,0:T(8,128)(2,1)}, u32[]{:S(2)}) copy-start(bf16[256,2688]{1,0:T(8,128)(2,1)} %param.69) | copy-start | bytes 4128772
  (21 other events, 52.5 us)
Sparse Core Ops, SparseCore 0:
  178.5 178.1 reduce-scatter.3
where the time goes:
time: 365 us; the launch traced here: 364 us
  waiting for transfers between devices  226 us (62%)
  starting transfers between devices  45.6 us (12%)
  matrix products  44.8 us (12%)
  local copies, waits for them, and re-layouts  25.4 us (7%)
  between operations  14.6 us (4%)
  other arithmetic  7.22 us (2%)
    ppermute x16, waiting for transfers between devices, shifted(): lax.ppermute(value, axis, [(source, source + steps) for source in range(f...  167 us
    unnamed x2, waiting for transfers between devices  58.6 us
    ppermute x16, starting transfers between devices, shifted(): lax.ppermute(value, axis, [(source, source + steps) for source in range(f...  45.5 us
    unnamed x74, local copies, waits for them, and re-layouts  20.3 us
    sub x4, matrix products, head_block(): raised = jnp.exp(scores - row_max)  13 us
    dot_general x4, matrix products, head_block(): jnp.einsum('gqk,qgd->kd', soft_low, grad_head, preferred_element_type=jnp...  11.3 us
    dot_general x4, matrix products, head_block(): jnp.einsum('qgd,kd->gqk', grad_head, value_head, preferred_element_type=j...  10.2 us
  transfers between devices with their start and end apart: 17, of which 7 were waited for; matrix products, arithmetic and copies ran while one was open for 9% of the time, Pallas kernels for 0%

commit v1 on v0

v1 whole, which is shorter than its diff:
```python
import functools

import jax
import jax.numpy as jnp
from jax import lax
from jax.experimental import pallas as pl
from jax.experimental.pallas import tpu as pltpu
from jax.sharding import PartitionSpec as P

HD = 128
HQ = 16
HK = 8
W = 1024
GROUP = HQ // HK

attn_scale = 168.0 ** (-0.5)
log2_e = 1.4426950408889634

VMEM = pl.BlockSpec(memory_space=pltpu.VMEM)
SMEM = pl.BlockSpec(memory_space=pltpu.SMEM)
ANY = pl.BlockSpec(memory_space=pl.ANY)


def call(kernel, outs, in_specs, out_specs, scratch=(), flops=0, moved=0, name=None):
    return pl.pallas_call(
        kernel,
        out_shape=outs,
        in_specs=in_specs,
        out_specs=out_specs,
        scratch_shapes=list(scratch),
        cost_estimate=pl.CostEstimate(flops=flops, bytes_accessed=moved, transcendentals=0),
        compiler_params=pltpu.CompilerParams(vmem_limit_bytes=56 * 1024 * 1024),
        name=name,
    )


def shape(dims, kind=jnp.bfloat16):
    return jax.ShapeDtypeStruct(dims, kind)


def pack_kernel(parts, where, q_ref, k_ref, v_ref, d_ref, *outs):
    place = where[0]
    rows = q_ref.shape[0]
    full, cross = outs[:parts], outs[parts:]
    for slot in range(parts):
        head = place ^ slot
        pair = pl.ds(pl.multiple_of(head * GROUP * HD, HD), GROUP * HD)
        single = pl.ds(pl.multiple_of(head * HD, HD), HD)
        both = q_ref[:, pair]
        for g in range(GROUP):
            full[slot][g * rows : (g + 1) * rows, :] = both[:, g * HD : (g + 1) * HD]
        both = d_ref[:, pair]
        for g in range(GROUP):
            full[slot][(GROUP + g) * rows : (GROUP + g + 1) * rows, :] = both[:, g * HD : (g + 1) * HD]
        keys, values = k_ref[:, single], v_ref[:, single]
        full[slot][2 * GROUP * rows : (2 * GROUP + 1) * rows, :] = keys
        full[slot][(2 * GROUP + 1) * rows :, :] = values
        cross[slot][:rows, :] = keys
        cross[slot][rows:, :] = values


def attention_kernel(parts, rows, where, *refs):
    full, cross = refs[:parts], refs[parts : 2 * parts]
    dq_out = refs[2 * parts : 3 * parts]
    back_k, back_v, own_k, own_v = refs[3 * parts : 3 * parts + 4]
    q_s, d_s, k_s, v_s, dq_s, dk_s, dv_s, sems = refs[3 * parts + 4 :]
    place, first = where[0], where[1]
    span = parts * rows
    wide = GROUP * rows
    copies = []

    def move(source, target):
        copy = pltpu.make_async_copy(source, target, sems.at[len(copies)])
        copy.start()
        copies.append(copy)

    for slot in range(parts):
        spot = place ^ slot
        pair = pl.ds(pl.multiple_of(spot * wide, wide), wide)
        old = pl.ds(pl.multiple_of(spot * rows, rows), rows)
        new = pl.ds(pl.multiple_of(span + spot * rows, rows), rows)
        move(full[slot].at[0:wide], q_s.at[pair])
        move(full[slot].at[wide : 2 * wide], d_s.at[pair])
        move(full[slot].at[2 * wide : 2 * wide + rows], k_s.at[new])
        move(full[slot].at[2 * wide + rows : 2 * wide + 2 * rows], v_s.at[new])
        move(cross[slot].at[0:rows], k_s.at[old])
        move(cross[slot].at[rows : 2 * rows], v_s.at[old])
    dk_s[...] = jnp.zeros_like(dk_s)
    dv_s[...] = jnp.zeros_like(dv_s)
    for copy in copies:
        copy.wait()

    key_at = lax.broadcasted_iota(jnp.int32, (rows, wide), 0)
    query_at = lax.broadcasted_iota(jnp.int32, (rows, wide), 1) % rows
    older = key_at > query_at
    nt = (((1,), (1,)), ((), ()))
    chunks = parts + 1
    hidden = jnp.float32(-jnp.inf)

    def one_block(block, carry):
        pair = pl.ds(pl.multiple_of(block * wide, wide), wide)
        queries = q_s[pair, :]
        grads = d_s[pair, :]

        def keys_of(chunk):
            return pl.ds(pl.multiple_of((block + chunk) * rows, rows), rows)

        scores = []
        for chunk in range(chunks):
            s = lax.dot_general(k_s[keys_of(chunk), :], queries, nt, preferred_element_type=jnp.float32)
            s = s * (attn_scale * log2_e)
            if chunk == 0:
                s = jnp.where(older, s, hidden)
            if chunk == chunks - 1:
                s = jnp.where(older, hidden, s)
            else:
                s = s + jnp.where((first == 1) & (block + chunk < parts), hidden, 0.0)
            scores.append(s)
        top = functools.reduce(jnp.maximum, [jnp.max(s, axis=0, keepdims=True) for s in scores])
        total = jnp.zeros((1, wide), jnp.float32)
        delta = jnp.zeros((1, wide), jnp.float32)
        raised, probs = [], []
        for chunk in range(chunks):
            e = jnp.exp2(scores[chunk] - top)
            dp = lax.dot_general(v_s[keys_of(chunk), :], grads, nt, preferred_element_type=jnp.float32)
            total = total + jnp.sum(e, axis=0, keepdims=True)
            delta = delta + jnp.sum(e * dp, axis=0, keepdims=True)
            raised.append(e)
            probs.append(dp)
        inverse = 1.0 / total
        delta = delta * inverse
        dq = jnp.zeros((HD, wide), jnp.float32)
        for chunk in range(chunks):
            soft = raised[chunk] * inverse
            ds = (soft * (probs[chunk] - delta)).astype(jnp.bfloat16)
            low = soft.astype(jnp.bfloat16)
            here = keys_of(chunk)
            dv_s[here, :] += jnp.dot(low, grads, preferred_element_type=jnp.float32)
            dk_s[here, :] += jnp.dot(ds, queries, preferred_element_type=jnp.float32)
            dq += lax.dot_general(
                k_s[here, :], ds, (((0,), (0,)), ((), ())), preferred_element_type=jnp.float32
            )
        dq_s[pair, :] = (attn_scale * dq).T.astype(jnp.bfloat16)
        return carry

    lax.fori_loop(0, parts, one_block, 0)
    out_copies = []
    for slot in range(parts):
        spot = place ^ slot
        pair = pl.ds(pl.multiple_of(spot * wide, wide), wide)
        copy = pltpu.make_async_copy(dq_s.at[pair], dq_out[slot], sems.at[slot])
        copy.start()
        out_copies.append(copy)
    back_k[...] = (attn_scale * dk_s[:span, :]).astype(jnp.bfloat16)
    own_k[...] = attn_scale * dk_s[span:, :]
    back_v[...] = dv_s[:span, :].astype(jnp.bfloat16)
    own_v[...] = dv_s[span:, :]
    for copy in out_copies:
        copy.wait()


def weight_kernel(parts, rows, where, own_k, back_k, x_own, *refs):
    near, far, out = refs[: parts - 1], refs[parts - 1 : 2 * parts - 2], refs[2 * parts - 2]
    dk_s = refs[2 * parts - 1]
    place, core = where[0], where[2]
    half = rows // 2
    dk_s[...] = (own_k[...] + back_k[...].astype(jnp.float32)).astype(jnp.bfloat16)
    tt = (((0,), (0,)), ((), ()))
    spot = pl.multiple_of(place * rows, rows)
    total = lax.dot_general(dk_s[pl.ds(spot, rows), :], x_own[...], tt, preferred_element_type=jnp.float32)
    for slot in range(1, parts):
        spot = (place ^ slot) * rows
        mine = pl.ds(pl.multiple_of(spot + core * half, half), half)
        other = pl.ds(pl.multiple_of(spot + (1 - core) * half, half), half)
        total += lax.dot_general(dk_s[mine, :], near[slot - 1][...], tt, preferred_element_type=jnp.float32)
        total += lax.dot_general(dk_s[other, :], far[slot - 1][...], tt, preferred_element_type=jnp.float32)
    out[...] = total.T.astype(jnp.bfloat16)


def value_kernel(parts, rows, where, own_v, back_v, *refs):
    outs, keep = refs[:parts], refs[parts]
    keep[...] = own_v[...] + back_v[...].astype(jnp.float32)
    for slot in range(parts):
        spot = pl.multiple_of((where[0] ^ slot) * rows, rows)
        outs[slot][...] = keep[pl.ds(spot, rows), :].astype(jnp.bfloat16)


def spread_kernel(parts, width, where, *refs):
    ins, out = refs[:parts], refs[parts]
    rows = out.shape[0]
    for slot in range(parts):
        head = where[0] ^ slot
        for g in range(width):
            at = pl.ds(pl.multiple_of((head * width + g) * HD, HD), HD)
            out[:, at] = ins[slot][g * rows : (g + 1) * rows, :]


def shards(normed_input, attn_queries, attn_keys, attn_values, out_grad):
    rows, features = normed_input.shape
    heads = attn_keys.shape[1] // HD
    count = lax.axis_size("ctx")
    parts = W // rows
    assert parts == heads and count % parts == 0 and parts & (parts - 1) == 0
    blocks = count // parts
    me = lax.axis_index("ctx")
    place = me % parts
    core = lax.axis_index("tp")
    where = jnp.stack([place, (me < parts).astype(jnp.int32), core]).astype(jnp.int32)

    def within(value, slot):
        return lax.ppermute(value, "ctx", [(s, s ^ slot) for s in range(count)])

    def across(value, slot, step):
        perm = []
        for s in range(count):
            target = (s // parts + step) % blocks * parts + (s % parts ^ slot)
            perm.append((s, target))
        return lax.ppermute(value, "ctx", perm)

    wide = GROUP * rows
    span = parts * rows
    packed = call(
        functools.partial(pack_kernel, parts),
        [shape((2 * wide + 2 * rows, HD))] * parts + [shape((2 * rows, HD))] * parts,
        [SMEM] + [VMEM] * 4,
        [VMEM] * (2 * parts),
        moved=4 << 20,
        name="pack",
    )(where, attn_queries, attn_keys, attn_values, out_grad)
    full, cross = packed[:parts], packed[parts:]
    got_cross = [across(cross[slot], slot, 1) for slot in range(parts)]
    got_full = [full[0]] + [within(full[slot], slot) for slot in range(1, parts)]

    half = rows // 2
    x_half = lax.dynamic_slice_in_dim(normed_input, core * half, half, 0)
    near = [within(x_half, slot) for slot in range(1, parts)]
    far = [lax.ppermute(piece, "tp", [(0, 1), (1, 0)]) for piece in near]

    pairs = 2 * span * (parts + 1) * rows
    results = call(
        functools.partial(attention_kernel, parts, rows),
        [shape((wide, HD))] * parts
        + [shape((span, HD)), shape((span, HD)), shape((span, HD), jnp.float32), shape((span, HD), jnp.float32)],
        [SMEM] + [ANY] * (2 * parts),
        [ANY] * parts + [VMEM] * 4,
        scratch=[
            pltpu.VMEM((parts * wide, HD), jnp.bfloat16),
            pltpu.VMEM((parts * wide, HD), jnp.bfloat16),
            pltpu.VMEM((2 * span, HD), jnp.bfloat16),
            pltpu.VMEM((2 * span, HD), jnp.bfloat16),
            pltpu.VMEM((parts * wide, HD), jnp.bfloat16),
            pltpu.VMEM((2 * span, HD), jnp.float32),
            pltpu.VMEM((2 * span, HD), jnp.float32),
            pltpu.SemaphoreType.DMA((6 * parts,)),
        ],
        flops=10 * pairs * HD,
        moved=4 << 20,
        name="attention",
    )(where, *got_full, *got_cross)
    dq_parts = results[:parts]
    back_k, back_v, own_k, own_v = results[parts:]

    got_k = across(back_k, 0, -1)
    got_v = across(back_v, 0, -1)
    dq_got = [dq_parts[0]] + [within(dq_parts[slot], slot) for slot in range(1, parts)]

    partial_term = call(
        functools.partial(weight_kernel, parts, rows),
        shape((features, HD)),
        [SMEM] + [VMEM] * (2 * parts + 1),
        VMEM,
        scratch=[pltpu.VMEM((span, HD), jnp.bfloat16)],
        flops=2 * span * HD * features,
        moved=8 << 20,
        name="weight",
    )(where, own_k, got_k, normed_input, *near, *far)
    pieces = partial_term.reshape(count, features // count, HD)
    pieces = lax.all_to_all(pieces, "ctx", split_axis=0, concat_axis=0, tiled=True)
    pieces = pieces.reshape(blocks, parts, features // count, HD).astype(jnp.float32)
    weight_grad = pieces.sum(axis=0).transpose(1, 0, 2).reshape(features // count, parts * HD)

    dv_parts = call(
        functools.partial(value_kernel, parts, rows),
        [shape((rows, HD))] * parts,
        [SMEM, VMEM, VMEM],
        [VMEM] * parts,
        scratch=[pltpu.VMEM((span, HD), jnp.float32)],
        moved=1 << 20,
        name="value",
    )(where, own_v, got_v)
    dv_got = [dv_parts[0]] + [within(dv_parts[slot], slot) for slot in range(1, parts)]

    query_grad = call(
        functools.partial(spread_kernel, parts, GROUP),
        shape((rows, parts * GROUP * HD)),
        [SMEM] + [VMEM] * parts,
        VMEM,
        moved=1 << 20,
        name="spread_q",
    )(where, *dq_got)
    value_grad = call(
        functools.partial(spread_kernel, parts, 1),
        shape((rows, parts * HD)),
        [SMEM] + [VMEM] * parts,
        VMEM,
        moved=1 << 19,
        name="spread_v",
    )(where, *dv_got)
    return (query_grad, weight_grad, value_grad)


def solution(mesh):
    wide = P(("groups", "ctx"), "tp")
    return jax.shard_map(
        shards,
        mesh=mesh,
        in_specs=(P(("groups", "ctx"), None), wide, wide, wide, wide),
        out_specs=(wide, wide, wide),
        check_vma=False,
    )
```

time: 365 us -> 160 us (0.44)
  waiting for transfers between devices: 226 us -> 89.2 us
  matrix products: 44.8 us -> 0 us
  Pallas kernels: 0 us -> 28.6 us
  local copies, waits for them, and re-layouts: 25.4 us -> 5.11 us
  between operations: 14.6 us -> 0.88 us
  starting transfers between devices: 45.6 us -> 35.1 us
  other arithmetic: 7.22 us -> 0.75 us
    ppermute x16 -> x21, waiting for transfers between devices: 167 us -> 89.2 us  [the longest x6 72.9 us: across(): return lax.ppermute(value, 'ctx', perm)]
    unnamed x2 -> x0, waiting for transfers between devices: 58.6 us -> none
    dot_general x17 -> x0, matrix products: 31.8 us -> none  [the longest x4 11.3 us: head_block(): jnp.einsum('gqk,qgd->kd', soft_low, grad_head, preferred_element_type=jnp...]
    pallas_call x0 -> x6, Pallas kernels: none -> 28.6 us  [the longest x1 14.7 us: shards(): call(functools.partial(attention_kernel, parts, rows), [shape((wide, HD))...]
    unnamed x74 -> x60, local copies, waits for them, and re-layouts: 20.3 us -> 4.12 us
    ppermute x16 -> x21, starting transfers between devices: 45.5 us -> 30.2 us  [the longest x12 15.7 us: within(): return lax.ppermute(value, 'ctx', [(s, s ^ slot) for s in range(count)])]
    sub x4 -> x0, matrix products: 13 us -> none  [head_block(): raised = jnp.exp(scores - row_max)]
    all_to_all x0 -> x1, starting transfers between devices: none -> 4.86 us  [shards(): lax.all_to_all(pieces, 'ctx', split_axis=0, concat_axis=0, tiled=True)]
  transfers between devices with their start and end apart: 17 -> 22, of which waited for: 7 -> 9; matrix products, arithmetic and copies ran while one was open for 9% -> 0% of each run, Pallas kernels for 0% -> 13%
where the time goes in v1:
time: 160 us
  waiting for transfers between devices  89.2 us (56%)
  starting transfers between devices  35.1 us (22%)
  Pallas kernels  28.6 us (18%)
  local copies, waits for them, and re-layouts  5.11 us (3%)
    ppermute x6, waiting for transfers between devices, across(): return lax.ppermute(value, 'ctx', perm)  72.9 us
    ppermute x12, waiting for transfers between devices, within(): return lax.ppermute(value, 'ctx', [(s, s ^ slot) for s in range(count)])  16.3 us
    ppermute x12, starting transfers between devices, within(): return lax.ppermute(value, 'ctx', [(s, s ^ slot) for s in range(count)])  15.7 us
    pallas_call x1, Pallas kernels, shards(): call(functools.partial(attention_kernel, parts, rows), [shape((wide, HD))...  14.7 us
    ppermute x6, starting transfers between devices, across(): return lax.ppermute(value, 'ctx', perm)  14 us
    pallas_call x1, Pallas kernels, shards(): call(functools.partial(weight_kernel, parts, rows), shape((features, HD))...  5.32 us
    all_to_all x1, starting transfers between devices, shards(): lax.all_to_all(pieces, 'ctx', split_axis=0, concat_axis=0, tiled=True)  4.86 us
    unnamed x60, local copies, waits for them, and re-layouts  4.12 us
  transfers between devices with their start and end apart: 22, of which 9 were waited for; matrix products, arithmetic and copies ran while one was open for 0% of the time, Pallas kernels for 13%

profile of v1, /device:TPU:0, one launch (start us, length us, event | category | flops | bytes accessed | tf_op | source)
XLA Modules:
  0.0 159.7 jit_solution(5192307807238616970)
XLA Ops:
  1.3 2.9 %pack.1 = (bf16[1536,128]{1,0:T(8,128)(2,1)}, bf16[1536,128]{1,0:T(8,128)(2,1)}, bf16[1536,128]{1,0:T(8,128)(2,1)}, bf16[1536,128]{1,0:T(8,128)(2,1)}, bf16[512,...) custom-call(s32[3]{0:T(128)} %pad_add_fusion.where, ...), custom_call_target="tpu_custom_call" | custom-call | bytes 4194304 | tf_op jit(solution)/shard_map/pack/pallas_call | solution.py:222
  4.3 4.1 %collective-permute-start.3 = (bf16[512,128]{1,0:T(8,128)(2,1)}, bf16[512,128]{1,0:T(8,128)(2,1)S(1)}, u32[]{:S(2)}, u32[]{:S(2)}) collective-permute-start(bf16[512,128]{1,0:T(8,128)(2,1)} %get-tuple-element.27), channel_id=1, source_target_pairs={{0,8},{2,10},{4,12},{6,14},{8,0},{10,2},{12,4},{14,6},{1,9},{3,11}... | collective-permute-start | bytes 393224 | tf_op jit(solution)/shard_map/ppermute | solution.py:218
  8.5 1.6 collective-permute-start.11
  10.0 1.6 collective-permute-start.12
  13.3 1.7 %collective-permute-done.3.refs_4_ = bf16[512,128]{1,0:T(8,128)(2,1)S(1)} collective-permute-done((bf16[512,128]{1,0:T(8,128)(2,1)}, bf16[512,128]{1,0:T(8,128)(2,1)S(1)}, u32[]{:S(2)}, u32[]{:S(2)}) %collective-permute-start.3) | collective-permute-done | bytes 131104 | tf_op jit(solution)/shard_map/ppermute | solution.py:218
  15.0 2.1 %collective-permute-start = (bf16[1536,128]{1,0:T(8,128)(2,1)S(1)}, bf16[1536,128]{1,0:T(8,128)(2,1)S(1)}, u32[]{:S(2)}, u32[]{:S(2)}) collective-permute-start(bf16[1536,128]{1,0:T(8,128)(2,1)S(1)} %copy-done.18), channel_id=1, source_target_pairs={{0,2},{2,0},{4,6},{6,4},{8,10},{10,8},{12,14},{14,12},{1,3},{3,1},... | collective-permute-start | bytes 1179656 | tf_op jit(solution)/shard_map/ppermute | solution.py:211
  17.1 26.7 %collective-permute-done.4.refs_5_ = bf16[512,128]{1,0:T(8,128)(2,1)S(1)} collective-permute-done((bf16[512,128]{1,0:T(8,128)(2,1)}, bf16[512,128]{1,0:T(8,128)(2,1)S(1)}, u32[]{:S(2)}, u32[]{:S(2)}) %collective-permute-start.4) | collective-permute-done | bytes 131104 | tf_op jit(solution)/shard_map/ppermute | solution.py:218
  45.2 5.7 %collective-permute-done.5.refs_6_ = bf16[512,128]{1,0:T(8,128)(2,1)S(1)} collective-permute-done((bf16[512,128]{1,0:T(8,128)(2,1)}, bf16[512,128]{1,0:T(8,128)(2,1)S(1)}, u32[]{:S(2)}, u32[]{:S(2)}) %collective-permute-start.5) | collective-permute-done | bytes 131104 | tf_op jit(solution)/shard_map/ppermute | solution.py:218
  51.0 2.3 %collective-permute-start.6 = (bf16[512,128]{1,0:T(8,128)(2,1)S(1)}, bf16[512,128]{1,0:T(8,128)(2,1)S(1)}, u32[]{:S(2)}, u32[]{:S(2)}) collective-permute-start(bf16[512,128]{1,0:T(8,128)(2,1)S(1)} %copy-done.28), channel_id=1, source_target_pairs={{0,14},{2,12},{4,10},{6,8},{8,6},{10,4},{12,2},{14,0},{1,15},{3,13... | collective-permute-start | bytes 393224 | tf_op jit(solution)/shard_map/ppermute | solution.py:218
  53.2 5.5 %collective-permute-done.6.refs_7_ = bf16[512,128]{1,0:T(8,128)(2,1)S(1)} collective-permute-done((bf16[512,128]{1,0:T(8,128)(2,1)S(1)}, bf16[512,128]{1,0:T(8,128)(2,1)S(1)}, u32[]{:S(2)}, u32[]{:S(2)}) %collective-permute-start.6) | collective-permute-done | bytes 131104 | tf_op jit(solution)/shard_map/ppermute | solution.py:218
  58.7 1.9 %collective-permute-start.1 = (bf16[1536,128]{1,0:T(8,128)(2,1)S(1)}, bf16[1536,128]{1,0:T(8,128)(2,1)S(1)}, u32[]{:S(2)}, u32[]{:S(2)}) collective-permute-start(bf16[1536,128]{1,0:T(8,128)(2,1)S(1)} %copy-done.16), channel_id=1, source_target_pairs={{0,4},{2,6},{4,0},{6,2},{8,12},{10,14},{12,8},{14,10},{1,5},{3,7},... | collective-permute-start | bytes 1179656 | tf_op jit(solution)/shard_map/ppermute | solution.py:211
  62.4 8.3 %collective-permute-done.1.refs_2_ = bf16[1536,128]{1,0:T(8,128)(2,1)S(1)} collective-permute-done((bf16[1536,128]{1,0:T(8,128)(2,1)S(1)}, bf16[1536,128]{1,0:T(8,128)(2,1)S(1)}, u32[]{:S(2)}, u32[]{:S(2)}) %collective-permute-start.1) | collective-permute-done | bytes 393248 | tf_op jit(solution)/shard_map/ppermute | solution.py:211
  70.7 7.3 %collective-permute-done.2.refs_3_ = bf16[1536,128]{1,0:T(8,128)(2,1)S(1)} collective-permute-done((bf16[1536,128]{1,0:T(8,128)(2,1)S(1)}, bf16[1536,128]{1,0:T(8,128)(2,1)S(1)}, u32[]{:S(2)}, u32[]{:S(2)}) %collective-permute-start.2) | collective-permute-done | bytes 393248 | tf_op jit(solution)/shard_map/ppermute | solution.py:211
  78.8 14.7 %attention.1 = (bf16[512,128]{1,0:T(8,128)(2,1)}, bf16[512,128]{1,0:T(8,128)(2,1)}, bf16[512,128]{1,0:T(8,128)(2,1)}, bf16[512,128]{1,0:T(8,128)(2,1)}, bf16[102...) custom-call(s32[3]{0:T(128)} %pad_add_fusion.where, ...), custom_call_target="tpu_custom_call" | custom-call | flops 3355443200 | bytes 4194304 | tf_op jit(solution)/shard_map/attention/pallas_call | solution.py:240
  93.5 2.0 %collective-permute-start.10 = (bf16[1024,128]{1,0:T(8,128)(2,1)}, bf16[1024,128]{1,0:T(8,128)(2,1)S(1)}, u32[]{:S(2)}, u32[]{:S(2)}) collective-permute-start(bf16[1024,128]{1,0:T(8,128)(2,1)} %get-tuple-element.36), channel_id=1, source_target_pairs={{0,8},{2,10},{4,12},{6,14},{8,0},{10,2},{12,4},{14,6},{1,9},{3,11}... | collective-permute-start | bytes 786440 | tf_op jit(solution)/shard_map/ppermute | solution.py:218
  95.6 11.1 %collective-permute-done.10.back_k = bf16[1024,128]{1,0:T(8,128)(2,1)S(1)} collective-permute-done((bf16[1024,128]{1,0:T(8,128)(2,1)}, bf16[1024,128]{1,0:T(8,128)(2,1)S(1)}, u32[]{:S(2)}, u32[]{:S(2)}) %collective-permute-start.10) | collective-permute-done | bytes 262176 | tf_op jit(solution)/shard_map/ppermute | solution.py:218
  108.0 5.3 %weight.1 = bf16[2688,128]{1,0:T(8,128)(2,1)} custom-call(s32[3]{0:T(128)} %pad_add_fusion.where, f32[1024,128]{1,0:T(8,128)} %get-tuple-element.35.own_k, bf16[1024,128]{1,0:T(8,128)(2,1)} %copy-done.7, bf16[256,2688]{1,0:T(8,128)(2,1)} %x_own.1, bf16[128,2688]{1,0:T(8,128)(2,1)} %copy-done.1, bf16[128,2688]{1,0:T(8,128)(2,1)} %copy-done.2, ...), custom_call_target="tpu_custom_call" | custom-call | flops 704643072 | bytes 8388608 | tf_op jit(solution)/shard_map/weight/pallas_call | solution.py:267
  113.4 4.9 %all-to-all-start = ((bf16[8,336,128]{2,1,0:T(8,128)(2,1)}), bf16[8,336,128]{2,1,0:T(8,128)(2,1)S(1)}, u32[]{:S(2)}, u32[]{:S(2)}) async-start(bf16[8,336,128]{2,1,0:T(8,128)(2,1)} %bitcast.13), calls=%async_computation | async-start | bytes 1376256 | tf_op jit(solution)/shard_map/all_to_all | solution.py:278
  118.2 2.9 %collective-permute-start.17 = (bf16[1024,128]{1,0:T(8,128)(2,1)S(1)}, bf16[1024,128]{1,0:T(8,128)(2,1)S(1)}, u32[]{:S(2)}, u32[]{:S(2)}) collective-permute-start(bf16[1024,128]{1,0:T(8,128)(2,1)S(1)} %copy-done.21), channel_id=1, source_target_pairs={{0,8},{2,10},{4,12},{6,14},{8,0},{10,2},{12,4},{14,6},{1,9},{3,11}... | collective-permute-start | bytes 786440 | tf_op jit(solution)/shard_map/ppermute | solution.py:218
  124.7 22.1 %collective-permute-done.17.back_v = bf16[1024,128]{1,0:T(8,128)(2,1)S(1)} collective-permute-done((bf16[1024,128]{1,0:T(8,128)(2,1)S(1)}, bf16[1024,128]{1,0:T(8,128)(2,1)S(1)}, u32[]{:S(2)}, u32[]{:S(2)}) %collective-permute-start.17) | collective-permute-done | bytes 262176 | tf_op jit(solution)/shard_map/ppermute | solution.py:218
  147.5 1.9 %value.1 = (bf16[256,128]{1,0:T(8,128)(2,1)}, bf16[256,128]{1,0:T(8,128)(2,1)}, bf16[256,128]{1,0:T(8,128)(2,1)}, bf16[256,128]{1,0:T(8,128)(2,1)}) custom-call(s32[3]{0:T(128)} %pad_add_fusion.where, f32[1024,128]{1,0:T(8,128)} %get-tuple-element.37.own_v, bf16[1024,128]{1,0:T(8,128)(2,1)} %copy-done.8), custom_call_target="tpu_custom_call" | custom-call | bytes 1048576 | tf_op jit(solution)/shard_map/value/pallas_call | solution.py:282
  150.9 2.0 %collective-permute-start.20 = (bf16[256,128]{1,0:T(8,128)(2,1)}, bf16[256,128]{1,0:T(8,128)(2,1)S(1)}, u32[]{:S(2)}, u32[]{:S(2)}) collective-permute-start(bf16[256,128]{1,0:T(8,128)(2,1)} %get-tuple-element.42), channel_id=1, source_target_pairs={{0,6},{2,4},{4,2},{6,0},{8,14},{10,12},{12,10},{14,8},{1,7},{3,5},... | collective-permute-start | bytes 196616 | tf_op jit(solution)/shard_map/ppermute | solution.py:211
  153.6 2.0 %spread_q.1 = bf16[256,1024]{1,0:T(8,128)(2,1)} custom-call(s32[3]{0:T(128)} %pad_add_fusion.where, bf16[512,128]{1,0:T(8,128)(2,1)} %get-tuple-element.31.refs_0_, bf16[512,128]{1,0:T(8,128)(2,1)} %copy-done.9, bf16[512,128]{1,0:T(8,128)(2,1)} %copy-done.10, bf16[512,128]{1,0:T(8,128)(2,1)} %copy-done.11), custom_call_target="tpu_custom_call" | custom-call | bytes 1048576 | tf_op jit(solution)/shard_map/spread_q/pallas_call | solution.py:293
  156.9 1.7 %spread_v.1 = bf16[256,512]{1,0:T(8,128)(2,1)} custom-call(s32[3]{0:T(128)} %pad_add_fusion.where, bf16[256,128]{1,0:T(8,128)(2,1)} %get-tuple-element.39.refs_0_, bf16[256,128]{1,0:T(8,128)(2,1)} %copy-done.12, bf16[256,128]{1,0:T(8,128)(2,1)} %copy-done.13, bf16[256,128]{1,0:T(8,128)(2,1)} %copy-done.14), custom_call_target="tpu_custom_call" | custom-call | bytes 524288 | tf_op jit(solution)/shard_map/spread_v/pallas_call | solution.py:301
  (90 shorter events, 16.2 us)
Async XLA Ops:
  4.3 56.3 %copy-start.15 = (bf16[1536,128]{1,0:T(8,128)(2,1)S(1)}, bf16[1536,128]{1,0:T(8,128)(2,1)}, u32[]{:S(2)}) copy-start(bf16[1536,128]{1,0:T(8,128)(2,1)} %get-tuple-element.26) | copy-start | bytes 1179652
  4.3 10.7 %collective-permute-start.3 = (bf16[512,128]{1,0:T(8,128)(2,1)}, bf16[512,128]{1,0:T(8,128)(2,1)S(1)}, u32[]{:S(2)}, u32[]{:S(2)}) collective-permute-start(bf16[512,128]{1,0:T(8,128)(2,1)} %get-tuple-element.27), channel_id=1, source_target_pairs={{0,8},{2,10},{4,12},{6,14},{8,0},{10,2},{12,4},{14,6},{1,9},{3,11}... | collective-permute-start | bytes 393224 | tf_op jit(solution)/shard_map/ppermute | solution.py:218
  8.5 53.3 %collective-permute-start.11 = (bf16[128,2688]{1,0:T(8,128)(2,1)S(1)}, bf16[128,2688]{1,0:T(8,128)(2,1)S(1)}, u32[]{:S(2)}, u32[]{:S(2)}) collective-permute-start(bf16[128,2688]{1,0:T(8,128)(2,1)S(1)} %constant_dynamic-slice_fusion), channel_id=1, source_target_pairs={{0,2},{2,0},{4,6},{6,4},{8,10},{10,8},{12,14},{14,12},{1,3},{3,1},... | collective-permute-start | bytes 2064392 | tf_op jit(solution)/shard_map/ppermute | solution.py:211
  10.0 51.7 %collective-permute-start.12 = (bf16[128,2688]{1,0:T(8,128)(2,1)S(1)}, bf16[128,2688]{1,0:T(8,128)(2,1)S(1)}, u32[]{:S(2)}, u32[]{:S(2)}) collective-permute-start(bf16[128,2688]{1,0:T(8,128)(2,1)S(1)} %constant_dynamic-slice_fusion), channel_id=1, source_target_pairs={{0,4},{2,6},{4,0},{6,2},{8,12},{10,14},{12,8},{14,10},{1,5},{3,7},... | collective-permute-start | bytes 2064392 | tf_op jit(solution)/shard_map/ppermute | solution.py:211
  11.6 50.7 %collective-permute-start.13 = (bf16[128,2688]{1,0:T(8,128)(2,1)S(1)}, bf16[128,2688]{1,0:T(8,128)(2,1)S(1)}, u32[]{:S(2)}, u32[]{:S(2)}) collective-permute-start(bf16[128,2688]{1,0:T(8,128)(2,1)S(1)} %constant_dynamic-slice_fusion), channel_id=1, source_target_pairs={{0,6},{2,4},{4,2},{6,0},{8,14},{10,12},{12,10},{14,8},{1,7},{3,5},... | collective-permute-start | bytes 2064392 | tf_op jit(solution)/shard_map/ppermute | solution.py:211
  12.0 31.9 %collective-permute-start.4 = (bf16[512,128]{1,0:T(8,128)(2,1)}, bf16[512,128]{1,0:T(8,128)(2,1)S(1)}, u32[]{:S(2)}, u32[]{:S(2)}) collective-permute-start(bf16[512,128]{1,0:T(8,128)(2,1)} %get-tuple-element.28), channel_id=1, source_target_pairs={{0,10},{2,8},{4,14},{6,12},{8,2},{10,0},{12,6},{14,4},{1,11},{3,9}... | collective-permute-start | bytes 393224 | tf_op jit(solution)/shard_map/ppermute | solution.py:218
  15.0 63.0 %copy-start.22 = (bf16[512,128]{1,0:T(8,128)(2,1)}, bf16[512,128]{1,0:T(8,128)(2,1)S(1)}, u32[]{:S(2)}) copy-start(bf16[512,128]{1,0:T(8,128)(2,1)S(1)} %collective-permute-done.3.refs_4_) | copy-start | bytes 393220
  15.0 45.6 %collective-permute-start = (bf16[1536,128]{1,0:T(8,128)(2,1)S(1)}, bf16[1536,128]{1,0:T(8,128)(2,1)S(1)}, u32[]{:S(2)}, u32[]{:S(2)}) collective-permute-start(bf16[1536,128]{1,0:T(8,128)(2,1)S(1)} %copy-done.18), channel_id=1, source_target_pairs={{0,2},{2,0},{4,6},{6,4},{8,10},{10,8},{12,14},{14,12},{1,3},{3,1},... | collective-permute-start | bytes 1179656 | tf_op jit(solution)/shard_map/ppermute | solution.py:211
  43.9 7.1 %collective-permute-start.5 = (bf16[512,128]{1,0:T(8,128)(2,1)}, bf16[512,128]{1,0:T(8,128)(2,1)S(1)}, u32[]{:S(2)}, u32[]{:S(2)}) collective-permute-start(bf16[512,128]{1,0:T(8,128)(2,1)} %get-tuple-element.29), channel_id=1, source_target_pairs={{0,12},{2,14},{4,8},{6,10},{8,4},{10,6},{12,0},{14,2},{1,13},{3,15... | collective-permute-start | bytes 393224 | tf_op jit(solution)/shard_map/ppermute | solution.py:218
  51.0 7.8 %collective-permute-start.6 = (bf16[512,128]{1,0:T(8,128)(2,1)S(1)}, bf16[512,128]{1,0:T(8,128)(2,1)S(1)}, u32[]{:S(2)}, u32[]{:S(2)}) collective-permute-start(bf16[512,128]{1,0:T(8,128)(2,1)S(1)} %copy-done.28), channel_id=1, source_target_pairs={{0,14},{2,12},{4,10},{6,8},{8,6},{10,4},{12,2},{14,0},{1,15},{3,13... | collective-permute-start | bytes 393224 | tf_op jit(solution)/shard_map/ppermute | solution.py:218
  58.7 12.0 %collective-permute-start.1 = (bf16[1536,128]{1,0:T(8,128)(2,1)S(1)}, bf16[1536,128]{1,0:T(8,128)(2,1)S(1)}, u32[]{:S(2)}, u32[]{:S(2)}) collective-permute-start(bf16[1536,128]{1,0:T(8,128)(2,1)S(1)} %copy-done.16), channel_id=1, source_target_pairs={{0,4},{2,6},{4,0},{6,2},{8,12},{10,14},{12,8},{14,10},{1,5},{3,7},... | collective-permute-start | bytes 1179656 | tf_op jit(solution)/shard_map/ppermute | solution.py:211
  60.6 17.5 %collective-permute-start.2 = (bf16[1536,128]{1,0:T(8,128)(2,1)S(1)}, bf16[1536,128]{1,0:T(8,128)(2,1)S(1)}, u32[]{:S(2)}, u32[]{:S(2)}) collective-permute-start(bf16[1536,128]{1,0:T(8,128)(2,1)S(1)} %copy-done.15), channel_id=1, source_target_pairs={{0,6},{2,4},{4,2},{6,0},{8,14},{10,12},{12,10},{14,8},{1,7},{3,5},... | collective-permute-start | bytes 1179656 | tf_op jit(solution)/shard_map/ppermute | solution.py:211
  61.8 44.9 %collective-permute-start.14 = (bf16[128,2688]{1,0:T(8,128)(2,1)S(1)}, bf16[128,2688]{1,0:T(8,128)(2,1)S(1)}, u32[]{:S(2)}, u32[]{:S(2)}) collective-permute-start(bf16[128,2688]{1,0:T(8,128)(2,1)S(1)} %collective-permute-done.11.refs_0_), channel_id=1, source_target_pairs={{0,1},{1,0},{2,3},{3,2},{4,5},{5,4},{6,7},{7,6},{8,9},{9,8},{10,11... | collective-permute-start | bytes 2064392 | tf_op jit(solution)/shard_map/ppermute | solution.py:237
  61.8 44.9 %collective-permute-start.15 = (bf16[128,2688]{1,0:T(8,128)(2,1)S(1)}, bf16[128,2688]{1,0:T(8,128)(2,1)S(1)}, u32[]{:S(2)}, u32[]{:S(2)}) collective-permute-start(bf16[128,2688]{1,0:T(8,128)(2,1)S(1)} %collective-permute-done.12.refs_1_), channel_id=1, source_target_pairs={{0,1},{1,0},{2,3},{3,2},{4,5},{5,4},{6,7},{7,6},{8,9},{9,8},{10,11... | collective-permute-start | bytes 2064392 | tf_op jit(solution)/shard_map/ppermute | solution.py:237
  62.3 44.4 %collective-permute-start.16 = (bf16[128,2688]{1,0:T(8,128)(2,1)S(1)}, bf16[128,2688]{1,0:T(8,128)(2,1)S(1)}, u32[]{:S(2)}, u32[]{:S(2)}) collective-permute-start(bf16[128,2688]{1,0:T(8,128)(2,1)S(1)} %collective-permute-done.13.refs_2_), channel_id=1, source_target_pairs={{0,1},{1,0},{2,3},{3,2},{4,5},{5,4},{6,7},{7,6},{8,9},{9,8},{10,11... | collective-permute-start | bytes 2064392 | tf_op jit(solution)/shard_map/ppermute | solution.py:237
  93.5 13.1 %collective-permute-start.10 = (bf16[1024,128]{1,0:T(8,128)(2,1)}, bf16[1024,128]{1,0:T(8,128)(2,1)S(1)}, u32[]{:S(2)}, u32[]{:S(2)}) collective-permute-start(bf16[1024,128]{1,0:T(8,128)(2,1)} %get-tuple-element.36), channel_id=1, source_target_pairs={{0,8},{2,10},{4,12},{6,14},{8,0},{10,2},{12,4},{14,6},{1,9},{3,11}... | collective-permute-start | bytes 786440 | tf_op jit(solution)/shard_map/ppermute | solution.py:218
  113.4 45.2 %all-to-all-start = ((bf16[8,336,128]{2,1,0:T(8,128)(2,1)}), bf16[8,336,128]{2,1,0:T(8,128)(2,1)S(1)}, u32[]{:S(2)}, u32[]{:S(2)}) async-start(bf16[8,336,128]{2,1,0:T(8,128)(2,1)} %bitcast.13), calls=%async_computation | async-start | bytes 1376256 | tf_op jit(solution)/shard_map/all_to_all | solution.py:278
  118.2 28.5 %collective-permute-start.17 = (bf16[1024,128]{1,0:T(8,128)(2,1)S(1)}, bf16[1024,128]{1,0:T(8,128)(2,1)S(1)}, u32[]{:S(2)}, u32[]{:S(2)}) collective-permute-start(bf16[1024,128]{1,0:T(8,128)(2,1)S(1)} %copy-done.21), channel_id=1, source_target_pairs={{0,8},{2,10},{4,12},{6,14},{8,0},{10,2},{12,4},{14,6},{1,9},{3,11}... | collective-permute-start | bytes 786440 | tf_op jit(solution)/shard_map/ppermute | solution.py:218
  121.2 29.7 %collective-permute-start.7 = (bf16[512,128]{1,0:T(8,128)(2,1)S(1)}, bf16[512,128]{1,0:T(8,128)(2,1)S(1)}, u32[]{:S(2)}, u32[]{:S(2)}) collective-permute-start(bf16[512,128]{1,0:T(8,128)(2,1)S(1)} %copy-done.26), channel_id=1, source_target_pairs={{0,2},{2,0},{4,6},{6,4},{8,10},{10,8},{12,14},{14,12},{1,3},{3,1},... | collective-permute-start | bytes 393224 | tf_op jit(solution)/shard_map/ppermute | solution.py:211
  122.6 30.3 %collective-permute-start.8 = (bf16[512,128]{1,0:T(8,128)(2,1)S(1)}, bf16[512,128]{1,0:T(8,128)(2,1)S(1)}, u32[]{:S(2)}, u32[]{:S(2)}) collective-permute-start(bf16[512,128]{1,0:T(8,128)(2,1)S(1)} %copy-done.24), channel_id=1, source_target_pairs={{0,4},{2,6},{4,0},{6,2},{8,12},{10,14},{12,8},{14,10},{1,5},{3,7},... | collective-permute-start | bytes 393224 | tf_op jit(solution)/shard_map/ppermute | solution.py:211
  124.1 28.8 %collective-permute-start.9 = (bf16[512,128]{1,0:T(8,128)(2,1)S(1)}, bf16[512,128]{1,0:T(8,128)(2,1)S(1)}, u32[]{:S(2)}, u32[]{:S(2)}) collective-permute-start(bf16[512,128]{1,0:T(8,128)(2,1)S(1)} %copy-done.23), channel_id=1, source_target_pairs={{0,6},{2,4},{4,2},{6,0},{8,14},{10,12},{12,10},{14,8},{1,7},{3,5},... | collective-permute-start | bytes 393224 | tf_op jit(solution)/shard_map/ppermute | solution.py:211
  149.4 6.2 %collective-permute-start.18 = (bf16[256,128]{1,0:T(8,128)(2,1)}, bf16[256,128]{1,0:T(8,128)(2,1)S(1)}, u32[]{:S(2)}, u32[]{:S(2)}) collective-permute-start(bf16[256,128]{1,0:T(8,128)(2,1)} %get-tuple-element.40), channel_id=1, source_target_pairs={{0,2},{2,0},{4,6},{6,4},{8,10},{10,8},{12,14},{14,12},{1,3},{3,1},... | collective-permute-start | bytes 196616 | tf_op jit(solution)/shard_map/ppermute | solution.py:211
  150.8 4.8 %collective-permute-start.19 = (bf16[256,128]{1,0:T(8,128)(2,1)}, bf16[256,128]{1,0:T(8,128)(2,1)S(1)}, u32[]{:S(2)}, u32[]{:S(2)}) collective-permute-start(bf16[256,128]{1,0:T(8,128)(2,1)} %get-tuple-element.41), channel_id=1, source_target_pairs={{0,4},{2,6},{4,0},{6,2},{8,12},{10,14},{12,8},{14,10},{1,5},{3,7},... | collective-permute-start | bytes 196616 | tf_op jit(solution)/shard_map/ppermute | solution.py:211
  150.9 5.4 %collective-permute-start.20 = (bf16[256,128]{1,0:T(8,128)(2,1)}, bf16[256,128]{1,0:T(8,128)(2,1)S(1)}, u32[]{:S(2)}, u32[]{:S(2)}) collective-permute-start(bf16[256,128]{1,0:T(8,128)(2,1)} %get-tuple-element.42), channel_id=1, source_target_pairs={{0,6},{2,4},{4,2},{6,0},{8,14},{10,12},{12,10},{14,8},{1,7},{3,5},... | collective-permute-start | bytes 196616 | tf_op jit(solution)/shard_map/ppermute | solution.py:211
  (28 other events, 363.7 us)

commit v2 on v1

v2 whole, which is shorter than its diff:
```python
import functools

import jax
import jax.numpy as jnp
from jax import lax
from jax.experimental import pallas as pl
from jax.experimental.pallas import tpu as pltpu
from jax.sharding import PartitionSpec as P


HD = 128
HQ = 16
HK = 8
W = 1024
GROUP = HQ // HK

attn_scale = 168.0 ** (-0.5)
log2_e = 1.4426950408889634

VMEM = pl.BlockSpec(memory_space=pltpu.VMEM)
ANY = pl.BlockSpec(memory_space=pl.ANY)


def call(kernel, outs, in_specs, out_specs, scratch=(), flops=0, moved=0, room=8):
    return pl.pallas_call(
        kernel,
        out_shape=outs,
        in_specs=in_specs,
        out_specs=out_specs,
        scratch_shapes=list(scratch),
        cost_estimate=pl.CostEstimate(flops=flops, bytes_accessed=moved, transcendentals=0),
        compiler_params=pltpu.CompilerParams(vmem_limit_bytes=room << 20),
    )


def shape(dims, kind=jnp.bfloat16):
    return jax.ShapeDtypeStruct(dims, kind)


def place_of(parts):
    return lax.axis_index("ctx") % parts


def pack_kernel(parts, q_ref, k_ref, v_ref, d_ref, *outs):
    place = place_of(parts)
    rows = q_ref.shape[0]
    full, cross = outs[:parts], outs[parts:]
    for slot in range(parts):
        head = place ^ slot
        pair = pl.ds(pl.multiple_of(head * GROUP * HD, HD), GROUP * HD)
        single = pl.ds(pl.multiple_of(head * HD, HD), HD)
        both = q_ref[:, pair]
        for g in range(GROUP):
            full[slot][g * rows : (g + 1) * rows, :] = both[:, g * HD : (g + 1) * HD]
        both = d_ref[:, pair]
        for g in range(GROUP):
            full[slot][(GROUP + g) * rows : (GROUP + g + 1) * rows, :] = both[:, g * HD : (g + 1) * HD]
        keys, values = k_ref[:, single], v_ref[:, single]
        full[slot][2 * GROUP * rows : (2 * GROUP + 1) * rows, :] = keys
        full[slot][(2 * GROUP + 1) * rows :, :] = values
        cross[slot][:rows, :] = keys
        cross[slot][rows:, :] = values


def attention_kernel(parts, rows, *refs):
    full, cross = refs[:parts], refs[parts : 2 * parts]
    dq_s, back_k, back_v, own_k, own_v = refs[2 * parts : 2 * parts + 5]
    q_s, d_s, k_s, v_s, dk_s, dv_s, sems = refs[2 * parts + 5 :]
    place = place_of(parts)
    first = lax.axis_index("ctx") < parts
    span = parts * rows
    wide = GROUP * rows
    copies = []

    def move(source, target):
        copy = pltpu.make_async_copy(source, target, sems.at[len(copies)])
        copy.start()
        copies.append(copy)

    for slot in range(parts):
        spot = place ^ slot
        pair = pl.ds(pl.multiple_of(spot * wide, wide), wide)
        old = pl.ds(pl.multiple_of(spot * rows, rows), rows)
        new = pl.ds(pl.multiple_of(span + spot * rows, rows), rows)
        move(full[slot].at[0:wide], q_s.at[pair])
        move(full[slot].at[wide : 2 * wide], d_s.at[pair])
        move(full[slot].at[2 * wide : 2 * wide + rows], k_s.at[new])
        move(full[slot].at[2 * wide + rows : 2 * wide + 2 * rows], v_s.at[new])
        move(cross[slot].at[0:rows], k_s.at[old])
        move(cross[slot].at[rows : 2 * rows], v_s.at[old])
    dk_s[...] = jnp.zeros_like(dk_s)
    dv_s[...] = jnp.zeros_like(dv_s)
    for copy in copies:
        copy.wait()

    key_at = lax.broadcasted_iota(jnp.int32, (rows, wide), 0)
    query_at = lax.broadcasted_iota(jnp.int32, (rows, wide), 1) % rows
    older = key_at > query_at
    nt = (((1,), (1,)), ((), ()))
    chunks = parts + 1
    hidden = jnp.float32(-jnp.inf)

    def one_block(block, carry):
        pair = pl.ds(pl.multiple_of(block * wide, wide), wide)
        queries = q_s[pair, :]
        grads = d_s[pair, :]

        def keys_of(chunk):
            return pl.ds(pl.multiple_of((block + chunk) * rows, rows), rows)

        scores = []
        for chunk in range(chunks):
            s = lax.dot_general(k_s[keys_of(chunk), :], queries, nt, preferred_element_type=jnp.float32)
            s = s * (attn_scale * log2_e)
            if chunk == 0:
                s = jnp.where(older, s, hidden)
            if chunk == chunks - 1:
                s = jnp.where(older, hidden, s)
            else:
                s = s + jnp.where(first & (block + chunk < parts), hidden, 0.0)
            scores.append(s)
        top = functools.reduce(jnp.maximum, [jnp.max(s, axis=0, keepdims=True) for s in scores])
        total = jnp.zeros((1, wide), jnp.float32)
        delta = jnp.zeros((1, wide), jnp.float32)
        raised, probs = [], []
        for chunk in range(chunks):
            e = jnp.exp2(scores[chunk] - top)
            dp = lax.dot_general(v_s[keys_of(chunk), :], grads, nt, preferred_element_type=jnp.float32)
            total = total + jnp.sum(e, axis=0, keepdims=True)
            delta = delta + jnp.sum(e * dp, axis=0, keepdims=True)
            raised.append(e)
            probs.append(dp)
        inverse = 1.0 / total
        delta = delta * inverse
        dq = jnp.zeros((HD, wide), jnp.float32)
        for chunk in range(chunks):
            soft = raised[chunk] * inverse
            ds = (soft * (probs[chunk] - delta)).astype(jnp.bfloat16)
            low = soft.astype(jnp.bfloat16)
            here = keys_of(chunk)
            dv_s[here, :] += jnp.dot(low, grads, preferred_element_type=jnp.float32)
            dk_s[here, :] += jnp.dot(ds, queries, preferred_element_type=jnp.float32)
            dq += lax.dot_general(
                k_s[here, :], ds, (((0,), (0,)), ((), ())), preferred_element_type=jnp.float32
            )
        dq_s[pair, :] = (attn_scale * dq).T.astype(jnp.bfloat16)
        return carry

    lax.fori_loop(0, parts, one_block, 0)
    back_k[...] = (attn_scale * dk_s[:span, :]).astype(jnp.bfloat16)
    own_k[...] = attn_scale * dk_s[span:, :]
    back_v[...] = dv_s[:span, :].astype(jnp.bfloat16)
    own_v[...] = dv_s[span:, :]


def weight_kernel(parts, count, rows, own_k, back_k, x_own, *refs):
    near, far = refs[: parts - 1], refs[parts - 1 : 2 * parts - 2]
    outs = refs[2 * parts - 2 : -4]
    dk_s, x_s, w_s, sems = refs[-4:]
    place, core = place_of(parts), lax.axis_index("tp")
    half = rows // 2
    copies = []

    def move(source, at, size):
        target = x_s.at[pl.ds(pl.multiple_of(at, half), size)]
        copy = pltpu.make_async_copy(source, target, sems.at[len(copies)])
        copy.start()
        copies.append(copy)

    move(x_own, place * rows, rows)
    for slot in range(1, parts):
        spot = (place ^ slot) * rows
        move(near[slot - 1], spot + core * half, half)
        move(far[slot - 1], spot + (1 - core) * half, half)
    dk_s[...] = (own_k[...] + back_k[...].astype(jnp.float32)).astype(jnp.bfloat16).T
    for copy in copies:
        copy.wait()
    total = jnp.dot(dk_s[...], x_s[...], preferred_element_type=jnp.float32)
    if len(outs) == 1:
        outs[0][...] = total.T.astype(jnp.bfloat16)
        return
    w_s[...] = total.T.astype(jnp.bfloat16)
    piece = w_s.shape[0] // count
    for slot in range(count):
        at = (lax.axis_index("ctx") ^ slot) * piece
        outs[slot][...] = w_s[pl.ds(pl.multiple_of(at, 16), piece), :]


def gather_kernel(parts, *refs):
    ins, out = refs[:-1], refs[-1]
    for slot in range(parts):
        at = pl.ds(pl.multiple_of((place_of(parts) ^ slot) * HD, HD), HD)
        out[:, at] = ins[slot][...].astype(jnp.float32) + ins[slot + parts][...].astype(jnp.float32)


def value_kernel(parts, rows, dq, own_v, back_v, *outs):
    wide = GROUP * rows
    for slot in range(parts):
        spot = place_of(parts) ^ slot
        outs[slot][:wide, :] = dq[pl.ds(pl.multiple_of(spot * wide, wide), wide), :]
        at = pl.ds(pl.multiple_of(spot * rows, rows), rows)
        outs[slot][wide:, :] = (own_v[at, :] + back_v[at, :].astype(jnp.float32)).astype(jnp.bfloat16)


def spread_kernel(parts, *refs):
    ins, dq_out, dv_out = refs[:parts], refs[-2], refs[-1]
    rows = dq_out.shape[0]
    for slot in range(parts):
        head = place_of(parts) ^ slot
        for g in range(GROUP):
            at = pl.ds(pl.multiple_of((head * GROUP + g) * HD, HD), HD)
            dq_out[:, at] = ins[slot][g * rows : (g + 1) * rows, :]
        dv_out[:, pl.ds(pl.multiple_of(head * HD, HD), HD)] = ins[slot][GROUP * rows :, :]


def shards(normed_input, attn_queries, attn_keys, attn_values, out_grad):
    rows, features = normed_input.shape
    heads = attn_keys.shape[1] // HD
    count = lax.axis_size("ctx")
    parts = W // rows
    assert parts == heads and count % parts == 0 and parts & (parts - 1) == 0
    blocks = count // parts
    core = lax.axis_index("tp")

    def within(value, slot):
        return lax.ppermute(value, "ctx", [(s, s ^ slot) for s in range(count)])

    def across(value, slot, step):
        perm = []
        for s in range(count):
            target = (s // parts + step) * parts + (s % parts ^ slot)
            if 0 <= target < count:
                perm.append((s, target))
        return lax.ppermute(value, "ctx", perm)

    def swapped(value):
        return lax.ppermute(value, "tp", [(0, 1), (1, 0)])

    wide = GROUP * rows
    span = parts * rows
    packed = call(
        functools.partial(pack_kernel, parts),
        [shape((2 * wide + 2 * rows, HD))] * parts + [shape((2 * rows, HD))] * parts,
        [VMEM] * 4,
        [VMEM] * (2 * parts),
        moved=4 << 20,
        room=56,
    )(attn_queries, attn_keys, attn_values, out_grad)
    full, cross = packed[:parts], packed[parts:]
    got_cross = [across(cross[slot], slot, 1) for slot in range(parts)]
    got_full = [full[0]] + [within(full[slot], slot) for slot in range(1, parts)]

    half = rows // 2
    x_half = lax.dynamic_slice_in_dim(normed_input, core * half, half, 0)
    near = [within(x_half, slot) for slot in range(1, parts)]
    far = [swapped(piece) for piece in near]

    pairs = 2 * span * (parts + 1) * rows
    results = call(
        functools.partial(attention_kernel, parts, rows),
        [shape((parts * wide, HD)), shape((span, HD)), shape((span, HD))]
        + [shape((span, HD), jnp.float32)] * 2,
        [ANY] * (2 * parts),
        [VMEM] * 5,
        scratch=[
            pltpu.VMEM((parts * wide, HD), jnp.bfloat16),
            pltpu.VMEM((parts * wide, HD), jnp.bfloat16),
            pltpu.VMEM((2 * span, HD), jnp.bfloat16),
            pltpu.VMEM((2 * span, HD), jnp.bfloat16),
            pltpu.VMEM((2 * span, HD), jnp.float32),
            pltpu.VMEM((2 * span, HD), jnp.float32),
            pltpu.SemaphoreType.DMA((6 * parts,)),
        ],
        flops=10 * pairs * HD,
        moved=4 << 20,
        room=32,
    )(*got_full, *got_cross)
    dq, back_k, back_v, own_k, own_v = results
    got_k = across(back_k, 0, -1)
    got_v = across(back_v, 0, -1)
    mine = call(
        functools.partial(value_kernel, parts, rows),
        [shape((wide + rows, HD))] * parts,
        [VMEM] * 3,
        [VMEM] * parts,
        moved=1 << 20,
    )(dq, own_v, got_v)
    got_mine = [mine[0]] + [within(mine[slot], slot) for slot in range(1, parts)]

    piece = features // count
    direct = blocks == 2
    terms = call(
        functools.partial(weight_kernel, parts, count, rows),
        [shape((piece, HD))] * count if direct else [shape((features, HD))],
        [VMEM] * 2 + [ANY] * (2 * parts - 1),
        [VMEM] * (count if direct else 1),
        scratch=[
            pltpu.VMEM((HD, span), jnp.bfloat16),
            pltpu.VMEM((span, features), jnp.bfloat16),
            pltpu.VMEM((features, HD), jnp.bfloat16),
            pltpu.SemaphoreType.DMA((2 * parts - 1,)),
        ],
        flops=2 * span * HD * features,
        moved=8 << 20,
        room=24,
    )(own_k, got_k, normed_input, *near, *far)
    if direct:
        got_w = [terms[0]] + [within(terms[slot], slot) for slot in range(1, count)]
        weight_grad = call(
            functools.partial(gather_kernel, parts),
            shape((piece, parts * HD), jnp.float32),
            [VMEM] * count,
            VMEM,
            moved=2 << 20,
        )(*got_w)
    else:
        pieces = terms[0].reshape(count, piece, HD)
        pieces = lax.all_to_all(pieces, "ctx", split_axis=0, concat_axis=0, tiled=True)
        pieces = pieces.reshape(blocks, parts, piece, HD).astype(jnp.float32)
        weight_grad = pieces.sum(axis=0).transpose(1, 0, 2).reshape(piece, parts * HD)

    query_grad, value_grad = call(
        functools.partial(spread_kernel, parts),
        [shape((rows, parts * GROUP * HD)), shape((rows, parts * HD))],
        [VMEM] * parts,
        [VMEM] * 2,
        moved=2 << 20,
    )(*got_mine)
    return (query_grad, weight_grad, value_grad)


def solution(mesh):
    wide = P(("groups", "ctx"), "tp")

    return jax.shard_map(
        shards,
        mesh=mesh,
        in_specs=(P(("groups", "ctx"), None), wide, wide, wide, wide),
        out_specs=(wide, wide, wide),
        check_vma=False,
    )
```

time: 160 us -> 137 us (0.86)
  waiting for transfers between devices: 89.2 us -> 63.8 us
  starting transfers between devices: 35.1 us -> 50.7 us
  Pallas kernels: 28.6 us -> 21.6 us
  local copies, waits for them, and re-layouts: 5.11 us -> 0.08 us
    ppermute x6, waiting for transfers between devices: 72.9 us -> 44 us  [across(): return lax.ppermute(value, 'ctx', perm)]
    ppermute x6, starting transfers between devices: 14 us -> 24.5 us  [across(): return lax.ppermute(value, 'ctx', perm)]
    ppermute x12 -> x16, starting transfers between devices: 15.7 us -> 25.7 us  [within(): return lax.ppermute(value, 'ctx', [(s, s ^ slot) for s in range(count)])]
    pallas_call x5, Pallas kernels: 25.7 us -> 18.6 us  [the longest x1 13.5 us: shards(): call(functools.partial(attention_kernel, parts, rows), [shape((parts * wi...]
    all_to_all x1 -> x0, starting transfers between devices: 4.86 us -> none  [shards(): lax.all_to_all(pieces, 'ctx', split_axis=0, concat_axis=0, tiled=True)]
    unnamed x60 -> x10, local copies, waits for them, and re-layouts: 4.12 us -> 0.02 us
    ppermute x12 -> x16, waiting for transfers between devices: 16.3 us -> 19.8 us  [within(): return lax.ppermute(value, 'ctx', [(s, s ^ slot) for s in range(count)])]
  transfers between devices with their start and end apart: 22 -> 25, of which waited for: 9 -> 11; matrix products, arithmetic and copies ran while one was open for 0% -> 0% of each run, Pallas kernels for 13% -> 13%
where the time goes in v2:
time: 137 us
  waiting for transfers between devices  63.8 us (47%)
  starting transfers between devices  50.7 us (37%)
  Pallas kernels  21.6 us (16%)
    ppermute x6, waiting for transfers between devices, across(): return lax.ppermute(value, 'ctx', perm)  44 us
    ppermute x16, starting transfers between devices, within(): return lax.ppermute(value, 'ctx', [(s, s ^ slot) for s in range(count)])  25.7 us
    ppermute x6, starting transfers between devices, across(): return lax.ppermute(value, 'ctx', perm)  24.5 us
    ppermute x16, waiting for transfers between devices, within(): return lax.ppermute(value, 'ctx', [(s, s ^ slot) for s in range(count)])  19.8 us
    pallas_call x1, Pallas kernels, shards(): call(functools.partial(attention_kernel, parts, rows), [shape((parts * wi...  13.5 us
    pallas_call x1, Pallas kernels, shards(): call(functools.partial(pack_kernel, parts), [shape((2 * wide + 2 * rows,...  3.04 us
    pallas_call x1, Pallas kernels, shards(): call(functools.partial(weight_kernel, parts, count, rows), [shape((piece,...  2.93 us
  transfers between devices with their start and end apart: 25, of which 11 were waited for; matrix products, arithmetic and copies ran while one was open for 0% of the time, Pallas kernels for 13%

profile of v2, /device:TPU:0, one launch (start us, length us, event | category | flops | bytes accessed | tf_op | source)
XLA Modules:
  0.0 137.0 jit_solution(15112343218213358956)
XLA Ops:
  0.6 3.0 %shard_map.76 = (bf16[1536,128]{1,0:T(8,128)(2,1)}, bf16[1536,128]{1,0:T(8,128)(2,1)}, bf16[1536,128]{1,0:T(8,128)(2,1)}, bf16[1536,128]{1,0:T(8,128)(2,1)}, bf1...) custom-call(bf16[256,1024]{1,0:T(8,128)(2,1)} %q_ref.1, ...), custom_call_target="tpu_custom_call" | custom-call | bytes 4194304 | tf_op jit(solution)/shard_map/pallas_call | solution.py:241
  3.7 6.1 %collective-permute-start.3 = (bf16[512,128]{1,0:T(8,128)(2,1)}, bf16[512,128]{1,0:T(8,128)(2,1)S(1)}, u32[]{:S(2)}, u32[]{:S(2)}) collective-permute-start(bf16[512,128]{1,0:T(8,128)(2,1)} %get-tuple-element.34), channel_id=1, source_target_pairs={{0,8},{2,10},{4,12},{6,14},{1,9},{3,11},{5,13},{7,15},{16,24},{18,... | collective-permute-start | bytes 393224 | tf_op jit(solution)/shard_map/ppermute | solution.py:234
  14.3 1.6 %collective-permute-start.13 = (bf16[128,2688]{1,0:T(8,128)(2,1)S(1)}, bf16[128,2688]{1,0:T(8,128)(2,1)S(1)}, u32[]{:S(2)}, u32[]{:S(2)}) collective-permute-start(bf16[128,2688]{1,0:T(8,128)(2,1)S(1)} %constant_dynamic-slice_fusion), channel_id=1, source_target_pairs={{0,4},{2,6},{4,0},{6,2},{8,12},{10,14},{12,8},{14,10},{1,5},{3,7},... | collective-permute-start | bytes 2064392 | tf_op jit(solution)/shard_map/ppermute | solution.py:226
  15.8 5.1 %collective-permute-start.14 = (bf16[128,2688]{1,0:T(8,128)(2,1)S(1)}, bf16[128,2688]{1,0:T(8,128)(2,1)S(1)}, u32[]{:S(2)}, u32[]{:S(2)}) collective-permute-start(bf16[128,2688]{1,0:T(8,128)(2,1)S(1)} %constant_dynamic-slice_fusion), channel_id=1, source_target_pairs={{0,6},{2,4},{4,2},{6,0},{8,14},{10,12},{12,10},{14,8},{1,7},{3,5},... | collective-permute-start | bytes 2064392 | tf_op jit(solution)/shard_map/ppermute | solution.py:226
  21.0 7.4 %collective-permute-start.5 = (bf16[512,128]{1,0:T(8,128)(2,1)}, bf16[512,128]{1,0:T(8,128)(2,1)S(1)}, u32[]{:S(2)}, u32[]{:S(2)}) collective-permute-start(bf16[512,128]{1,0:T(8,128)(2,1)} %get-tuple-element.36), channel_id=1, source_target_pairs={{0,12},{2,14},{4,8},{6,10},{1,13},{3,15},{5,9},{7,11},{16,28},{18,... | collective-permute-start | bytes 393224 | tf_op jit(solution)/shard_map/ppermute | solution.py:234
  28.4 19.7 %collective-permute-done.5.refs_6_ = bf16[512,128]{1,0:T(8,128)(2,1)S(1)} collective-permute-done((bf16[512,128]{1,0:T(8,128)(2,1)}, bf16[512,128]{1,0:T(8,128)(2,1)S(1)}, u32[]{:S(2)}, u32[]{:S(2)}) %collective-permute-start.5) | collective-permute-done | bytes 131104 | tf_op jit(solution)/shard_map/ppermute | solution.py:234
  48.1 7.1 %collective-permute-start.6 = (bf16[512,128]{1,0:T(8,128)(2,1)S(1)}, bf16[512,128]{1,0:T(8,128)(2,1)S(1)}, u32[]{:S(2)}, u32[]{:S(2)}) collective-permute-start(bf16[512,128]{1,0:T(8,128)(2,1)S(1)} %copy-done.4), channel_id=1, source_target_pairs={{0,14},{2,12},{4,10},{6,8},{1,15},{3,13},{5,11},{7,9},{16,30},{18,... | collective-permute-start | bytes 393224 | tf_op jit(solution)/shard_map/ppermute | solution.py:234
  55.2 3.9 %collective-permute-done.6.refs_7_ = bf16[512,128]{1,0:T(8,128)(2,1)S(1)} collective-permute-done((bf16[512,128]{1,0:T(8,128)(2,1)S(1)}, bf16[512,128]{1,0:T(8,128)(2,1)S(1)}, u32[]{:S(2)}, u32[]{:S(2)}) %collective-permute-start.6) | collective-permute-done | bytes 131104 | tf_op jit(solution)/shard_map/ppermute | solution.py:234
  59.1 2.0 %collective-permute-start.2 = (bf16[1536,128]{1,0:T(8,128)(2,1)S(1)}, bf16[1536,128]{1,0:T(8,128)(2,1)S(1)}, u32[]{:S(2)}, u32[]{:S(2)}) collective-permute-start(bf16[1536,128]{1,0:T(8,128)(2,1)S(1)} %copy-done.2), channel_id=1, source_target_pairs={{0,6},{2,4},{4,2},{6,0},{8,14},{10,12},{12,10},{14,8},{1,7},{3,5},... | collective-permute-start | bytes 1179656 | tf_op jit(solution)/shard_map/ppermute | solution.py:226
  61.7 9.2 %collective-permute-done.1.refs_2_ = bf16[1536,128]{1,0:T(8,128)(2,1)S(1)} collective-permute-done((bf16[1536,128]{1,0:T(8,128)(2,1)S(1)}, bf16[1536,128]{1,0:T(8,128)(2,1)S(1)}, u32[]{:S(2)}, u32[]{:S(2)}) %collective-permute-start.1) | collective-permute-done | bytes 393248 | tf_op jit(solution)/shard_map/ppermute | solution.py:226
  70.9 4.1 %collective-permute-done.2.refs_3_ = bf16[1536,128]{1,0:T(8,128)(2,1)S(1)} collective-permute-done((bf16[1536,128]{1,0:T(8,128)(2,1)S(1)}, bf16[1536,128]{1,0:T(8,128)(2,1)S(1)}, u32[]{:S(2)}, u32[]{:S(2)}) %collective-permute-start.2) | collective-permute-done | bytes 393248 | tf_op jit(solution)/shard_map/ppermute | solution.py:226
  75.0 13.5 %shard_map.77 = (bf16[2048,128]{1,0:T(8,128)(2,1)S(1)}, bf16[1024,128]{1,0:T(8,128)(2,1)S(1)}, bf16[1024,128]{1,0:T(8,128)(2,1)S(1)}, f32[1024,128]{1,0:T(8,128)S(1)}, f32[1024,128]{1,0:T(8,128)S(1)}) custom-call(bf16[1536,128]{1,0:T(8,128)(2,1)S(1)} %copy-done.1, bf16[1536,128]{1,0:T(8,128)(2,1)S(1)} %collective-permute-done.refs_1_, ...), custom_call_target="tpu_custom_call" | custom-call | flops 3355443200 | bytes 4194304 | tf_op jit(solution)/shard_map/pallas_call | solution.py:259
  91.2 18.2 %collective-permute-done.7.back_v = bf16[1024,128]{1,0:T(8,128)(2,1)S(1)} collective-permute-done((bf16[1024,128]{1,0:T(8,128)(2,1)S(1)}, bf16[1024,128]{1,0:T(8,128)(2,1)S(1)}, u32[]{:S(2)}, u32[]{:S(2)}) %collective-permute-start.7) | collective-permute-done | bytes 262176 | tf_op jit(solution)/shard_map/ppermute | solution.py:234
  110.8 2.3 %collective-permute-done.11.back_k = bf16[1024,128]{1,0:T(8,128)(2,1)S(1)} collective-permute-done((bf16[1024,128]{1,0:T(8,128)(2,1)S(1)}, bf16[1024,128]{1,0:T(8,128)(2,1)S(1)}, u32[]{:S(2)}, u32[]{:S(2)}) %collective-permute-start.11) | collective-permute-done | bytes 262176 | tf_op jit(solution)/shard_map/ppermute | solution.py:234
  113.2 1.9 %collective-permute-start.10 = (bf16[768,128]{1,0:T(8,128)(2,1)S(1)}, bf16[768,128]{1,0:T(8,128)(2,1)S(1)}, u32[]{:S(2)}, u32[]{:S(2)}) collective-permute-start(bf16[768,128]{1,0:T(8,128)(2,1)S(1)} %get-tuple-element.44), channel_id=1, source_target_pairs={{0,6},{2,4},{4,2},{6,0},{8,14},{10,12},{12,10},{14,8},{1,7},{3,5},... | collective-permute-start | bytes 589832 | tf_op jit(solution)/shard_map/ppermute | solution.py:226
  115.0 2.9 %shard_map.80 = (bf16[336,128]{1,0:T(8,128)(2,1)S(1)}, bf16[336,128]{1,0:T(8,128)(2,1)S(1)}, bf16[336,128]{1,0:T(8,128)(2,1)S(1)}, bf16[336,128]{1,0:T(8,128)(2,...) custom-call(f32[1024,128]{1,0:T(8,128)S(1)} %get-tuple-element.46.ow, ...), custom_call_target="tpu_custom_call" | custom-call | flops 704643072 | bytes 8388608 | tf_op jit(solution)/shard_map/pallas_call | solution.py:292
  118.0 1.7 %collective-permute-start.18 = (bf16[336,128]{1,0:T(8,128)(2,1)S(1)}, bf16[336,128]{1,0:T(8,128)(2,1)S(1)}, u32[]{:S(2)}, u32[]{:S(2)}) collective-permute-start(bf16[336,128]{1,0:T(8,128)(2,1)S(1)} %get-tuple-element.49), channel_id=1, source_target_pairs={{0,2},{2,0},{4,6},{6,4},{8,10},{10,8},{12,14},{14,12},{1,3},{3,1},... | collective-permute-start | bytes 258056 | tf_op jit(solution)/shard_map/ppermute | solution.py:226
  119.6 1.9 %collective-permute-start.20 = (bf16[336,128]{1,0:T(8,128)(2,1)S(1)}, bf16[336,128]{1,0:T(8,128)(2,1)S(1)}, u32[]{:S(2)}, u32[]{:S(2)}) collective-permute-start(bf16[336,128]{1,0:T(8,128)(2,1)S(1)} %get-tuple-element.51), channel_id=1, source_target_pairs={{0,6},{2,4},{4,2},{6,0},{8,14},{10,12},{12,10},{14,8},{1,7},{3,5},... | collective-permute-start | bytes 258056 | tf_op jit(solution)/shard_map/ppermute | solution.py:226
  121.5 2.0 %collective-permute-done.10.refs_3_ = bf16[768,128]{1,0:T(8,128)(2,1)S(1)} collective-permute-done((bf16[768,128]{1,0:T(8,128)(2,1)S(1)}, bf16[768,128]{1,0:T(8,128)(2,1)S(1)}, u32[]{:S(2)}, u32[]{:S(2)}) %collective-permute-start.10) | collective-permute-done | bytes 196640 | tf_op jit(solution)/shard_map/ppermute | solution.py:226
  123.5 2.1 %collective-permute-start.22 = (bf16[336,128]{1,0:T(8,128)(2,1)S(1)}, bf16[336,128]{1,0:T(8,128)(2,1)S(1)}, u32[]{:S(2)}, u32[]{:S(2)}) collective-permute-start(bf16[336,128]{1,0:T(8,128)(2,1)S(1)} %get-tuple-element.53), channel_id=1, source_target_pairs={{0,10},{2,8},{4,14},{6,12},{8,2},{10,0},{12,6},{14,4},{1,11},{3,9}... | collective-permute-start | bytes 258056 | tf_op jit(solution)/shard_map/ppermute | solution.py:226
  125.6 2.8 %collective-permute-start.23 = (bf16[336,128]{1,0:T(8,128)(2,1)S(1)}, bf16[336,128]{1,0:T(8,128)(2,1)S(1)}, u32[]{:S(2)}, u32[]{:S(2)}) collective-permute-start(bf16[336,128]{1,0:T(8,128)(2,1)S(1)} %get-tuple-element.54), channel_id=1, source_target_pairs={{0,12},{2,14},{4,8},{6,10},{8,4},{10,6},{12,0},{14,2},{1,13},{3,15... | collective-permute-start | bytes 258056 | tf_op jit(solution)/shard_map/ppermute | solution.py:226
  128.8 2.2 %collective-permute-start.24 = (bf16[336,128]{1,0:T(8,128)(2,1)S(1)}, bf16[336,128]{1,0:T(8,128)(2,1)S(1)}, u32[]{:S(2)}, u32[]{:S(2)}) collective-permute-start(bf16[336,128]{1,0:T(8,128)(2,1)S(1)} %get-tuple-element.55), channel_id=1, source_target_pairs={{0,14},{2,12},{4,10},{6,8},{8,6},{10,4},{12,2},{14,0},{1,15},{3,13... | collective-permute-start | bytes 258056 | tf_op jit(solution)/shard_map/ppermute | solution.py:226
  132.5 1.8 %collective-permute-done.22.refs_5_ = bf16[336,128]{1,0:T(8,128)(2,1)S(1)} collective-permute-done((bf16[336,128]{1,0:T(8,128)(2,1)S(1)}, bf16[336,128]{1,0:T(8,128)(2,1)S(1)}, u32[]{:S(2)}, u32[]{:S(2)}) %collective-permute-start.22) | collective-permute-done | bytes 86048 | tf_op jit(solution)/shard_map/ppermute | solution.py:226
  134.3 1.8 %collective-permute-done.24.refs_7_ = bf16[336,128]{1,0:T(8,128)(2,1)S(1)} collective-permute-done((bf16[336,128]{1,0:T(8,128)(2,1)S(1)}, bf16[336,128]{1,0:T(8,128)(2,1)S(1)}, u32[]{:S(2)}, u32[]{:S(2)}) %collective-permute-start.24) | collective-permute-done | bytes 86048 | tf_op jit(solution)/shard_map/ppermute | solution.py:226
  (43 shorter events, 12.0 us)
Async XLA Ops:
  3.7 12.1 %collective-permute-start.3 = (bf16[512,128]{1,0:T(8,128)(2,1)}, bf16[512,128]{1,0:T(8,128)(2,1)S(1)}, u32[]{:S(2)}, u32[]{:S(2)}) collective-permute-start(bf16[512,128]{1,0:T(8,128)(2,1)} %get-tuple-element.34), channel_id=1, source_target_pairs={{0,8},{2,10},{4,12},{6,14},{1,9},{3,11},{5,13},{7,15},{16,24},{18,... | collective-permute-start | bytes 393224 | tf_op jit(solution)/shard_map/ppermute | solution.py:234
  9.9 51.2 %collective-permute-start.12 = (bf16[128,2688]{1,0:T(8,128)(2,1)S(1)}, bf16[128,2688]{1,0:T(8,128)(2,1)S(1)}, u32[]{:S(2)}, u32[]{:S(2)}) collective-permute-start(bf16[128,2688]{1,0:T(8,128)(2,1)S(1)} %constant_dynamic-slice_fusion), channel_id=1, source_target_pairs={{0,2},{2,0},{4,6},{6,4},{8,10},{10,8},{12,14},{14,12},{1,3},{3,1},... | collective-permute-start | bytes 2064392 | tf_op jit(solution)/shard_map/ppermute | solution.py:226
  11.5 9.5 %collective-permute-start.4 = (bf16[512,128]{1,0:T(8,128)(2,1)}, bf16[512,128]{1,0:T(8,128)(2,1)S(1)}, u32[]{:S(2)}, u32[]{:S(2)}) collective-permute-start(bf16[512,128]{1,0:T(8,128)(2,1)} %get-tuple-element.35), channel_id=1, source_target_pairs={{0,10},{2,8},{4,14},{6,12},{1,11},{3,9},{5,15},{7,13},{16,26},{18,... | collective-permute-start | bytes 393224 | tf_op jit(solution)/shard_map/ppermute | solution.py:234
  12.7 46.3 %collective-permute-start = (bf16[1536,128]{1,0:T(8,128)(2,1)}, bf16[1536,128]{1,0:T(8,128)(2,1)S(1)}, u32[]{:S(2)}, u32[]{:S(2)}) collective-permute-start(bf16[1536,128]{1,0:T(8,128)(2,1)} %get-tuple-element.31), channel_id=1, source_target_pairs={{0,2},{2,0},{4,6},{6,4},{8,10},{10,8},{12,14},{14,12},{1,3},{3,1},... | collective-permute-start | bytes 1179656 | tf_op jit(solution)/shard_map/ppermute | solution.py:226
  14.3 46.8 %collective-permute-start.13 = (bf16[128,2688]{1,0:T(8,128)(2,1)S(1)}, bf16[128,2688]{1,0:T(8,128)(2,1)S(1)}, u32[]{:S(2)}, u32[]{:S(2)}) collective-permute-start(bf16[128,2688]{1,0:T(8,128)(2,1)S(1)} %constant_dynamic-slice_fusion), channel_id=1, source_target_pairs={{0,4},{2,6},{4,0},{6,2},{8,12},{10,14},{12,8},{14,10},{1,5},{3,7},... | collective-permute-start | bytes 2064392 | tf_op jit(solution)/shard_map/ppermute | solution.py:226
  15.8 45.8 %collective-permute-start.14 = (bf16[128,2688]{1,0:T(8,128)(2,1)S(1)}, bf16[128,2688]{1,0:T(8,128)(2,1)S(1)}, u32[]{:S(2)}, u32[]{:S(2)}) collective-permute-start(bf16[128,2688]{1,0:T(8,128)(2,1)S(1)} %constant_dynamic-slice_fusion), channel_id=1, source_target_pairs={{0,6},{2,4},{4,2},{6,0},{8,14},{10,12},{12,10},{14,8},{1,7},{3,5},... | collective-permute-start | bytes 2064392 | tf_op jit(solution)/shard_map/ppermute | solution.py:226
  21.0 27.1 %collective-permute-start.5 = (bf16[512,128]{1,0:T(8,128)(2,1)}, bf16[512,128]{1,0:T(8,128)(2,1)S(1)}, u32[]{:S(2)}, u32[]{:S(2)}) collective-permute-start(bf16[512,128]{1,0:T(8,128)(2,1)} %get-tuple-element.36), channel_id=1, source_target_pairs={{0,12},{2,14},{4,8},{6,10},{1,13},{3,15},{5,9},{7,11},{16,28},{18,... | collective-permute-start | bytes 393224 | tf_op jit(solution)/shard_map/ppermute | solution.py:234
  48.1 10.9 %collective-permute-start.6 = (bf16[512,128]{1,0:T(8,128)(2,1)S(1)}, bf16[512,128]{1,0:T(8,128)(2,1)S(1)}, u32[]{:S(2)}, u32[]{:S(2)}) collective-permute-start(bf16[512,128]{1,0:T(8,128)(2,1)S(1)} %copy-done.4), channel_id=1, source_target_pairs={{0,14},{2,12},{4,10},{6,8},{1,15},{3,13},{5,11},{7,9},{16,30},{18,... | collective-permute-start | bytes 393224 | tf_op jit(solution)/shard_map/ppermute | solution.py:234
  59.0 11.8 %collective-permute-start.1 = (bf16[1536,128]{1,0:T(8,128)(2,1)S(1)}, bf16[1536,128]{1,0:T(8,128)(2,1)S(1)}, u32[]{:S(2)}, u32[]{:S(2)}) collective-permute-start(bf16[1536,128]{1,0:T(8,128)(2,1)S(1)} %copy-done.3), channel_id=1, source_target_pairs={{0,4},{2,6},{4,0},{6,2},{8,12},{10,14},{12,8},{14,10},{1,5},{3,7},... | collective-permute-start | bytes 1179656 | tf_op jit(solution)/shard_map/ppermute | solution.py:226
  59.1 15.9 %collective-permute-start.2 = (bf16[1536,128]{1,0:T(8,128)(2,1)S(1)}, bf16[1536,128]{1,0:T(8,128)(2,1)S(1)}, u32[]{:S(2)}, u32[]{:S(2)}) collective-permute-start(bf16[1536,128]{1,0:T(8,128)(2,1)S(1)} %copy-done.2), channel_id=1, source_target_pairs={{0,6},{2,4},{4,2},{6,0},{8,14},{10,12},{12,10},{14,8},{1,7},{3,5},... | collective-permute-start | bytes 1179656 | tf_op jit(solution)/shard_map/ppermute | solution.py:226
  61.1 52.1 %collective-permute-start.15 = (bf16[128,2688]{1,0:T(8,128)(2,1)S(1)}, bf16[128,2688]{1,0:T(8,128)(2,1)S(1)}, u32[]{:S(2)}, u32[]{:S(2)}) collective-permute-start(bf16[128,2688]{1,0:T(8,128)(2,1)S(1)} %collective-permute-done.12.refs_0_), channel_id=1, source_target_pairs={{0,1},{1,0},{2,3},{3,2},{4,5},{5,4},{6,7},{7,6},{8,9},{9,8},{10,11... | collective-permute-start | bytes 2064392 | tf_op jit(solution)/shard_map/ppermute | solution.py:237
  61.1 53.9 %collective-permute-start.16 = (bf16[128,2688]{1,0:T(8,128)(2,1)S(1)}, bf16[128,2688]{1,0:T(8,128)(2,1)S(1)}, u32[]{:S(2)}, u32[]{:S(2)}) collective-permute-start(bf16[128,2688]{1,0:T(8,128)(2,1)S(1)} %collective-permute-done.13.refs_1_), channel_id=1, source_target_pairs={{0,1},{1,0},{2,3},{3,2},{4,5},{5,4},{6,7},{7,6},{8,9},{9,8},{10,11... | collective-permute-start | bytes 2064392 | tf_op jit(solution)/shard_map/ppermute | solution.py:237
  61.6 53.4 %collective-permute-start.17 = (bf16[128,2688]{1,0:T(8,128)(2,1)S(1)}, bf16[128,2688]{1,0:T(8,128)(2,1)S(1)}, u32[]{:S(2)}, u32[]{:S(2)}) collective-permute-start(bf16[128,2688]{1,0:T(8,128)(2,1)S(1)} %collective-permute-done.14.refs_2_), channel_id=1, source_target_pairs={{0,1},{1,0},{2,3},{3,2},{4,5},{5,4},{6,7},{7,6},{8,9},{9,8},{10,11... | collective-permute-start | bytes 2064392 | tf_op jit(solution)/shard_map/ppermute | solution.py:237
  88.6 20.8 %collective-permute-start.7 = (bf16[1024,128]{1,0:T(8,128)(2,1)S(1)}, bf16[1024,128]{1,0:T(8,128)(2,1)S(1)}, u32[]{:S(2)}, u32[]{:S(2)}) collective-permute-start(bf16[1024,128]{1,0:T(8,128)(2,1)S(1)} %get-tuple-element.40), channel_id=1, source_target_pairs={{8,0},{10,2},{12,4},{14,6},{9,1},{11,3},{13,5},{15,7},{24,16},{26,... | collective-permute-start | bytes 786440 | tf_op jit(solution)/shard_map/ppermute | solution.py:234
  89.9 23.3 %collective-permute-start.11 = (bf16[1024,128]{1,0:T(8,128)(2,1)S(1)}, bf16[1024,128]{1,0:T(8,128)(2,1)S(1)}, u32[]{:S(2)}, u32[]{:S(2)}) collective-permute-start(bf16[1024,128]{1,0:T(8,128)(2,1)S(1)} %get-tuple-element.47), channel_id=1, source_target_pairs={{8,0},{10,2},{12,4},{14,6},{9,1},{11,3},{13,5},{15,7},{24,16},{26,... | collective-permute-start | bytes 786440 | tf_op jit(solution)/shard_map/ppermute | solution.py:234
  109.4 10.2 %collective-permute-start.8 = (bf16[768,128]{1,0:T(8,128)(2,1)S(1)}, bf16[768,128]{1,0:T(8,128)(2,1)S(1)}, u32[]{:S(2)}, u32[]{:S(2)}) collective-permute-start(bf16[768,128]{1,0:T(8,128)(2,1)S(1)} %get-tuple-element.42), channel_id=1, source_target_pairs={{0,2},{2,0},{4,6},{6,4},{8,10},{10,8},{12,14},{14,12},{1,3},{3,1},... | collective-permute-start | bytes 589832 | tf_op jit(solution)/shard_map/ppermute | solution.py:226
  113.1 8.4 %collective-permute-start.9 = (bf16[768,128]{1,0:T(8,128)(2,1)S(1)}, bf16[768,128]{1,0:T(8,128)(2,1)S(1)}, u32[]{:S(2)}, u32[]{:S(2)}) collective-permute-start(bf16[768,128]{1,0:T(8,128)(2,1)S(1)} %get-tuple-element.43), channel_id=1, source_target_pairs={{0,4},{2,6},{4,0},{6,2},{8,12},{10,14},{12,8},{14,10},{1,5},{3,7},... | collective-permute-start | bytes 589832 | tf_op jit(solution)/shard_map/ppermute | solution.py:226
  113.2 10.4 %collective-permute-start.10 = (bf16[768,128]{1,0:T(8,128)(2,1)S(1)}, bf16[768,128]{1,0:T(8,128)(2,1)S(1)}, u32[]{:S(2)}, u32[]{:S(2)}) collective-permute-start(bf16[768,128]{1,0:T(8,128)(2,1)S(1)} %get-tuple-element.44), channel_id=1, source_target_pairs={{0,6},{2,4},{4,2},{6,0},{8,14},{10,12},{12,10},{14,8},{1,7},{3,5},... | collective-permute-start | bytes 589832 | tf_op jit(solution)/shard_map/ppermute | solution.py:226
  118.0 7.7 %collective-permute-start.18 = (bf16[336,128]{1,0:T(8,128)(2,1)S(1)}, bf16[336,128]{1,0:T(8,128)(2,1)S(1)}, u32[]{:S(2)}, u32[]{:S(2)}) collective-permute-start(bf16[336,128]{1,0:T(8,128)(2,1)S(1)} %get-tuple-element.49), channel_id=1, source_target_pairs={{0,2},{2,0},{4,6},{6,4},{8,10},{10,8},{12,14},{14,12},{1,3},{3,1},... | collective-permute-start | bytes 258056 | tf_op jit(solution)/shard_map/ppermute | solution.py:226
  119.6 9.2 %collective-permute-start.19 = (bf16[336,128]{1,0:T(8,128)(2,1)S(1)}, bf16[336,128]{1,0:T(8,128)(2,1)S(1)}, u32[]{:S(2)}, u32[]{:S(2)}) collective-permute-start(bf16[336,128]{1,0:T(8,128)(2,1)S(1)} %get-tuple-element.50), channel_id=1, source_target_pairs={{0,4},{2,6},{4,0},{6,2},{8,12},{10,14},{12,8},{14,10},{1,5},{3,7},... | collective-permute-start | bytes 258056 | tf_op jit(solution)/shard_map/ppermute | solution.py:226
  119.6 12.4 %collective-permute-start.20 = (bf16[336,128]{1,0:T(8,128)(2,1)S(1)}, bf16[336,128]{1,0:T(8,128)(2,1)S(1)}, u32[]{:S(2)}, u32[]{:S(2)}) collective-permute-start(bf16[336,128]{1,0:T(8,128)(2,1)S(1)} %get-tuple-element.51), channel_id=1, source_target_pairs={{0,6},{2,4},{4,2},{6,0},{8,14},{10,12},{12,10},{14,8},{1,7},{3,5},... | collective-permute-start | bytes 258056 | tf_op jit(solution)/shard_map/ppermute | solution.py:226
  121.5 11.0 %collective-permute-start.21 = (bf16[336,128]{1,0:T(8,128)(2,1)S(1)}, bf16[336,128]{1,0:T(8,128)(2,1)S(1)}, u32[]{:S(2)}, u32[]{:S(2)}) collective-permute-start(bf16[336,128]{1,0:T(8,128)(2,1)S(1)} %get-tuple-element.52), channel_id=1, source_target_pairs={{0,8},{2,10},{4,12},{6,14},{8,0},{10,2},{12,4},{14,6},{1,9},{3,11}... | collective-permute-start | bytes 258056 | tf_op jit(solution)/shard_map/ppermute | solution.py:226
  123.5 10.8 %collective-permute-start.22 = (bf16[336,128]{1,0:T(8,128)(2,1)S(1)}, bf16[336,128]{1,0:T(8,128)(2,1)S(1)}, u32[]{:S(2)}, u32[]{:S(2)}) collective-permute-start(bf16[336,128]{1,0:T(8,128)(2,1)S(1)} %get-tuple-element.53), channel_id=1, source_target_pairs={{0,10},{2,8},{4,14},{6,12},{8,2},{10,0},{12,6},{14,4},{1,11},{3,9}... | collective-permute-start | bytes 258056 | tf_op jit(solution)/shard_map/ppermute | solution.py:226
  125.6 8.7 %collective-permute-start.23 = (bf16[336,128]{1,0:T(8,128)(2,1)S(1)}, bf16[336,128]{1,0:T(8,128)(2,1)S(1)}, u32[]{:S(2)}, u32[]{:S(2)}) collective-permute-start(bf16[336,128]{1,0:T(8,128)(2,1)S(1)} %get-tuple-element.54), channel_id=1, source_target_pairs={{0,12},{2,14},{4,8},{6,10},{8,4},{10,6},{12,0},{14,2},{1,13},{3,15... | collective-permute-start | bytes 258056 | tf_op jit(solution)/shard_map/ppermute | solution.py:226
  (6 other events, 243.0 us)

commit v3 on v2

v3 whole, which is shorter than its diff:
```python
import functools

import jax
import jax.numpy as jnp
from jax import lax
from jax.experimental import pallas as pl
from jax.experimental.pallas import tpu as pltpu
from jax.sharding import PartitionSpec as P


HD = 128
HQ = 16
HK = 8
W = 1024
GROUP = HQ // HK

attn_scale = 168.0 ** (-0.5)
log2_e = 1.4426950408889634

VMEM = pl.BlockSpec(memory_space=pltpu.VMEM)
ANY = pl.BlockSpec(memory_space=pl.ANY)


def call(kernel, outs, in_specs, out_specs, scratch=(), flops=0, moved=0, room=8):
    return pl.pallas_call(
        kernel,
        out_shape=outs,
        in_specs=in_specs,
        out_specs=out_specs,
        scratch_shapes=list(scratch),
        cost_estimate=pl.CostEstimate(flops=flops, bytes_accessed=moved, transcendentals=0),
        compiler_params=pltpu.CompilerParams(vmem_limit_bytes=room << 20),
    )


def shape(dims, kind=jnp.bfloat16):
    return jax.ShapeDtypeStruct(dims, kind)


def place_of(parts):
    return lax.axis_index("ctx") % parts


def pack_kernel(parts, slots, crosses, q_ref, k_ref, v_ref, d_ref, *refs):
    count = len(slots) + crosses
    outs, held, sems, out_sems = refs[:count], refs[count : 2 * count], refs[-2], refs[-1]
    rows = q_ref.shape[0]
    copies = []
    for at in range(count):
        cross = at >= len(slots)
        head = place_of(parts) ^ (at - len(slots) if cross else slots[at])
        sources = [(k_ref, head), (v_ref, head)]
        if not cross:
            sources = [(ref, head * GROUP + g) for ref in (q_ref, d_ref) for g in range(GROUP)] + sources
        mine = []
        for step, (ref, column) in enumerate(sources):
            source = ref.at[:, pl.ds(pl.multiple_of(column * HD, HD), HD)]
            target = held[at].at[step * rows : (step + 1) * rows]
            copy = pltpu.make_async_copy(source, target, sems.at[at, step])
            copy.start()
            mine.append(copy)
        copies.append(mine)
    sent = []
    for at, mine in enumerate(copies):
        for copy in mine:
            copy.wait()
        copy = pltpu.make_async_copy(held[at], outs[at], out_sems.at[at])
        copy.start()
        sent.append(copy)
    for copy in sent:
        copy.wait()


def attention_kernel(parts, rows, *refs):
    full, cross = refs[:parts], refs[parts : 2 * parts]
    dq_s, back_k, back_v, own_k, own_v = refs[2 * parts : 2 * parts + 5]
    q_s, d_s, k_s, v_s, dk_s, dv_s, sems = refs[2 * parts + 5 :]
    place = place_of(parts)
    first = lax.axis_index("ctx") < parts
    span = parts * rows
    wide = GROUP * rows
    copies = []

    def move(source, target):
        copy = pltpu.make_async_copy(source, target, sems.at[len(copies)])
        copy.start()
        copies.append(copy)

    for slot in range(parts):
        spot = place ^ slot
        pair = pl.ds(pl.multiple_of(spot * wide, wide), wide)
        old = pl.ds(pl.multiple_of(spot * rows, rows), rows)
        new = pl.ds(pl.multiple_of(span + spot * rows, rows), rows)
        move(full[slot].at[0:wide], q_s.at[pair])
        move(full[slot].at[wide : 2 * wide], d_s.at[pair])
        move(full[slot].at[2 * wide : 2 * wide + rows], k_s.at[new])
        move(full[slot].at[2 * wide + rows : 2 * wide + 2 * rows], v_s.at[new])
        move(cross[slot].at[0:rows], k_s.at[old])
        move(cross[slot].at[rows : 2 * rows], v_s.at[old])
    dk_s[...] = jnp.zeros_like(dk_s)
    dv_s[...] = jnp.zeros_like(dv_s)
    for copy in copies:
        copy.wait()

    key_at = lax.broadcasted_iota(jnp.int32, (rows, wide), 0)
    query_at = lax.broadcasted_iota(jnp.int32, (rows, wide), 1) % rows
    older = key_at > query_at
    nt = (((1,), (1,)), ((), ()))
    chunks = parts + 1
    hidden = jnp.float32(-jnp.inf)

    def one_block(block, skipped):
        pair = slice(block * wide, (block + 1) * wide)
        queries = q_s[pair, :]
        grads = d_s[pair, :]

        def keys_of(chunk):
            return slice((block + chunk) * rows, (block + chunk + 1) * rows)

        used = [chunk for chunk in range(chunks) if block + chunk >= skipped]
        scores = {}
        for chunk in used:
            s = lax.dot_general(k_s[keys_of(chunk), :], queries, nt, preferred_element_type=jnp.float32)
            s = s * (attn_scale * log2_e)
            if chunk == 0:
                s = jnp.where(older, s, hidden)
            if chunk == chunks - 1:
                s = jnp.where(older, hidden, s)
            scores[chunk] = s
        top = functools.reduce(jnp.maximum, [jnp.max(s, axis=0, keepdims=True) for s in scores.values()])
        total = jnp.zeros((1, wide), jnp.float32)
        delta = jnp.zeros((1, wide), jnp.float32)
        raised, probs = {}, {}
        for chunk in used:
            e = jnp.exp2(scores[chunk] - top)
            dp = lax.dot_general(v_s[keys_of(chunk), :], grads, nt, preferred_element_type=jnp.float32)
            total = total + jnp.sum(e, axis=0, keepdims=True)
            delta = delta + jnp.sum(e * dp, axis=0, keepdims=True)
            raised[chunk] = e
            probs[chunk] = dp
        inverse = 1.0 / total
        delta = delta * inverse
        dq = jnp.zeros((HD, wide), jnp.float32)
        for chunk in used:
            soft = raised[chunk] * inverse
            ds = (soft * (probs[chunk] - delta)).astype(jnp.bfloat16)
            low = soft.astype(jnp.bfloat16)
            here = keys_of(chunk)
            dv_s[here, :] += jnp.dot(low, grads, preferred_element_type=jnp.float32)
            dk_s[here, :] += jnp.dot(ds, queries, preferred_element_type=jnp.float32)
            dq += lax.dot_general(
                k_s[here, :], ds, (((0,), (0,)), ((), ())), preferred_element_type=jnp.float32
            )
        dq_s[pair, :] = (attn_scale * dq).T.astype(jnp.bfloat16)

    for skipped, here in ((parts, first), (0, jnp.logical_not(first))):

        @pl.when(here)
        def _(skipped=skipped):
            for block in range(parts):
                one_block(block, skipped)

    back_k[...] = (attn_scale * dk_s[:span, :]).astype(jnp.bfloat16)
    own_k[...] = attn_scale * dk_s[span:, :]
    back_v[...] = dv_s[:span, :].astype(jnp.bfloat16)
    own_v[...] = dv_s[span:, :]


def weight_kernel(parts, count, rows, spots, own_k, back_k, x_own, *refs):
    pieces, outs = refs[: 2 * len(spots)], refs[2 * len(spots) : -4]
    dk_s, x_s, w_s, sems = refs[-4:]
    place, core = place_of(parts), lax.axis_index("tp")
    half = rows // 2
    copies = []

    def move(source, at):
        target = x_s.at[pl.ds(pl.multiple_of(at, 64), source.shape[0])]
        copy = pltpu.make_async_copy(source, target, sems.at[len(copies)])
        copy.start()
        copies.append(copy)

    move(x_own, place * rows)
    for at, (slot, offset) in enumerate(spots):
        base = (place ^ slot) * rows + offset
        move(pieces[2 * at], base + core * half)
        move(pieces[2 * at + 1], base + (1 - core) * half)
    dk_s[...] = (own_k[...] + back_k[...].astype(jnp.float32)).astype(jnp.bfloat16).T
    for copy in copies:
        copy.wait()
    total = jnp.dot(dk_s[...], x_s[...], preferred_element_type=jnp.float32)
    if len(outs) == 1:
        outs[0][...] = total.T.astype(jnp.bfloat16)
        return
    w_s[...] = total.T.astype(jnp.bfloat16)
    piece = w_s.shape[0] // count
    for slot in range(count):
        at = (lax.axis_index("ctx") ^ slot) * piece
        outs[slot][...] = w_s[pl.ds(pl.multiple_of(at, 16), piece), :]


def split_kernel(parts, rows, value, *outs):
    for slot in range(parts):
        at = (place_of(parts) ^ slot) * rows
        outs[slot][...] = value[pl.ds(pl.multiple_of(at, rows), rows), :]


def value_kernel(parts, rows, own_v, back_v, *outs):
    for slot in range(parts):
        at = pl.ds(pl.multiple_of((place_of(parts) ^ slot) * rows, rows), rows)
        outs[slot][...] = (own_v[at, :] + back_v[at, :].astype(jnp.float32)).astype(jnp.bfloat16)


def spread_kernel(parts, *refs):
    dq, dv = refs[:parts], refs[parts : 2 * parts]
    outs = refs[-3:] if len(refs) > 2 * parts + 2 else refs[-2:]
    terms = refs[2 * parts : -len(outs)]
    rows = outs[0].shape[0]
    for slot in range(parts):
        head = place_of(parts) ^ slot
        for g in range(GROUP):
            at = pl.ds(pl.multiple_of((head * GROUP + g) * HD, HD), HD)
            outs[0][:, at] = dq[slot][g * rows : (g + 1) * rows, :]
        at = pl.ds(pl.multiple_of(head * HD, HD), HD)
        outs[1][:, at] = dv[slot][...]
        if terms:
            outs[2][:, at] = terms[slot][...].astype(jnp.float32) + terms[slot + parts][...].astype(jnp.float32)


def shards(normed_input, attn_queries, attn_keys, attn_values, out_grad):
    rows, features = normed_input.shape
    heads = attn_keys.shape[1] // HD
    count = lax.axis_size("ctx")
    parts = W // rows
    assert parts == heads and count % parts == 0 and parts & (parts - 1) == 0
    blocks = count // parts
    core = lax.axis_index("tp")

    def within(value, slot):
        return lax.ppermute(value, "ctx", [(s, s ^ slot) for s in range(count)])

    def across(value, slot, step):
        perm = []
        for s in range(count):
            target = (s // parts + step) * parts + (s % parts ^ slot)
            if 0 <= target < count:
                perm.append((s, target))
        return lax.ppermute(value, "ctx", perm)

    def swapped(value):
        return lax.ppermute(value, "tp", [(0, 1), (1, 0)])

    wide = GROUP * rows
    span = parts * rows

    def pack(slots, crosses):
        shapes = [(2 * wide + 2 * rows, HD)] * len(slots) + [(2 * rows, HD)] * crosses
        return call(
            functools.partial(pack_kernel, parts, slots, crosses),
            [shape(dims) for dims in shapes],
            [ANY] * 4,
            [ANY] * len(shapes),
            scratch=[pltpu.VMEM(dims, jnp.bfloat16) for dims in shapes]
            + [pltpu.SemaphoreType.DMA((len(shapes), 2 * GROUP + 2)), pltpu.SemaphoreType.DMA((len(shapes),))],
            moved=2 << 20,
            room=56,
        )(attn_queries, attn_keys, attn_values, out_grad)

    full_2, full_3, full_1, full_0, *cross = pack((2, 3, 1, 0), parts)
    full = (full_0, full_1, full_2, full_3)
    got_cross = [across(cross[slot], slot, 1) for slot in range(parts)]
    got_full = [full[0]] + [within(full[slot], slot) for slot in range(1, parts)]

    half = rows // 2
    x_half = lax.dynamic_slice_in_dim(normed_input, core * half, half, 0)
    quarter = half // 2
    near_2 = within(x_half, 2)
    near_3 = within(x_half[:quarter], 3)
    near_1 = within(x_half, 1)
    relay = within(near_2[quarter:], 1)
    spots = ((2, 0), (3, 0), (1, 0), (3, quarter))
    x_pieces = []
    for piece in (near_2, near_3, near_1, relay):
        x_pieces += [piece, swapped(piece)]

    pairs = 2 * span * (parts + 1) * rows
    results = call(
        functools.partial(attention_kernel, parts, rows),
        [shape((parts * wide, HD)), shape((span, HD)), shape((span, HD))]
        + [shape((span, HD), jnp.float32)] * 2,
        [ANY] * (2 * parts),
        [VMEM] * 5,
        scratch=[
            pltpu.VMEM((parts * wide, HD), jnp.bfloat16),
            pltpu.VMEM((parts * wide, HD), jnp.bfloat16),
            pltpu.VMEM((2 * span, HD), jnp.bfloat16),
            pltpu.VMEM((2 * span, HD), jnp.bfloat16),
            pltpu.VMEM((2 * span, HD), jnp.float32),
            pltpu.VMEM((2 * span, HD), jnp.float32),
            pltpu.SemaphoreType.DMA((6 * parts,)),
        ],
        flops=10 * pairs * HD,
        moved=4 << 20,
        room=32,
    )(*got_full, *got_cross)
    dq, back_k, back_v, own_k, own_v = results
    got_k = across(back_k, 0, -1)
    got_v = across(back_v, 0, -1)

    def exchanged(values):
        return [values[0]] + [within(values[slot], slot) for slot in range(1, parts)]

    dq_parts = call(
        functools.partial(split_kernel, parts, wide), [shape((wide, HD))] * parts, [VMEM], [VMEM] * parts, moved=1 << 20
    )(dq)
    got_dq = exchanged(dq_parts)
    dv_parts = call(
        functools.partial(value_kernel, parts, rows),
        [shape((rows, HD))] * parts,
        [VMEM] * 2,
        [VMEM] * parts,
        moved=1 << 20,
    )(own_v, got_v)
    got_dv = exchanged(dv_parts)

    piece = features // count
    direct = blocks == 2
    terms = call(
        functools.partial(weight_kernel, parts, count, rows, spots),
        [shape((piece, HD))] * count if direct else [shape((features, HD))],
        [VMEM] * 2 + [ANY] * (1 + len(x_pieces)),
        [VMEM] * (count if direct else 1),
        scratch=[
            pltpu.VMEM((HD, span), jnp.bfloat16),
            pltpu.VMEM((span, features), jnp.bfloat16),
            pltpu.VMEM((features, HD), jnp.bfloat16),
            pltpu.SemaphoreType.DMA((1 + len(x_pieces),)),
        ],
        flops=2 * span * HD * features,
        moved=8 << 20,
        room=24,
    )(own_k, got_k, normed_input, *x_pieces)
    got_terms = []
    if direct:
        got_terms = [terms[0]] + [within(terms[slot], slot) for slot in range(1, count)]

    outs = call(
        functools.partial(spread_kernel, parts),
        [shape((rows, parts * GROUP * HD)), shape((rows, parts * HD))]
        + ([shape((piece, parts * HD), jnp.float32)] if direct else []),
        [VMEM] * (2 * parts + len(got_terms)),
        [VMEM] * (3 if direct else 2),
        moved=3 << 20,
    )(*got_dq, *got_dv, *got_terms)
    query_grad, value_grad = outs[:2]
    if direct:
        weight_grad = outs[2]
    else:
        pieces = terms[0].reshape(count, piece, HD)
        pieces = lax.all_to_all(pieces, "ctx", split_axis=0, concat_axis=0, tiled=True)
        pieces = pieces.reshape(blocks, parts, piece, HD).astype(jnp.float32)
        weight_grad = pieces.sum(axis=0).transpose(1, 0, 2).reshape(piece, parts * HD)
    return (query_grad, weight_grad, value_grad)


def solution(mesh):
    wide = P(("groups", "ctx"), "tp")

    return jax.shard_map(
        shards,
        mesh=mesh,
        in_specs=(P(("groups", "ctx"), None), wide, wide, wide, wide),
        out_specs=(wide, wide, wide),
        check_vma=False,
    )
```

time: 137 us -> 124 us (0.905)
  starting transfers between devices: 50.7 us -> 41.8 us
  Pallas kernels: 21.6 us -> 15.7 us
    ppermute x6, starting transfers between devices: 24.5 us -> 16.6 us  [across(): return lax.ppermute(value, 'ctx', perm)]
    pallas_call x1, Pallas kernels: 13.5 us -> 8.43 us  [shards(): call(functools.partial(attention_kernel, parts, rows), [shape((parts * wi...]
    ppermute x16 -> x20, waiting for transfers between devices: 19.8 us -> 16.7 us  [within(): return lax.ppermute(value, 'ctx', [(s, s ^ slot) for s in range(count)])]
    ppermute x6, waiting for transfers between devices: 44 us -> 46.8 us  [across(): return lax.ppermute(value, 'ctx', perm)]
    ppermute x16 -> x20, starting transfers between devices: 25.7 us -> 24.6 us  [within(): return lax.ppermute(value, 'ctx', [(s, s ^ slot) for s in range(count)])]
  transfers between devices with their start and end apart: 25 -> 30, of which waited for: 11 -> 12; matrix products, arithmetic and copies ran while one was open for 0% -> 0% of each run, Pallas kernels for 13% -> 12%
where the time goes in v3:
time: 124 us; the launch traced here: 123 us
  waiting for transfers between devices  63.5 us (51%)
  starting transfers between devices  41.8 us (34%)
  Pallas kernels  15.7 us (13%)
  local copies, waits for them, and re-layouts  1.33 us (1%)
    ppermute x6, waiting for transfers between devices, across(): return lax.ppermute(value, 'ctx', perm)  46.8 us
    ppermute x20, starting transfers between devices, within(): return lax.ppermute(value, 'ctx', [(s, s ^ slot) for s in range(count)])  24.6 us
    ppermute x20, waiting for transfers between devices, within(): return lax.ppermute(value, 'ctx', [(s, s ^ slot) for s in range(count)])  16.7 us
    ppermute x6, starting transfers between devices, across(): return lax.ppermute(value, 'ctx', perm)  16.6 us
    pallas_call x1, Pallas kernels, shards(): call(functools.partial(attention_kernel, parts, rows), [shape((parts * wi...  8.43 us
    pallas_call x1, Pallas kernels, shards(): call(functools.partial(weight_kernel, parts, count, rows, spots), [shape(...  2.95 us
    pallas_call x1, Pallas kernels, pack(): call(functools.partial(pack_kernel, parts, slots, crosses), [shape(dims)...  2.84 us
  transfers between devices with their start and end apart: 30, of which 12 were waited for; matrix products, arithmetic and copies ran while one was open for 0% of the time, Pallas kernels for 12%

profile of v3, /device:TPU:0, one launch (start us, length us, event | category | flops | bytes accessed | tf_op | source)
XLA Modules:
  0.0 123.1 jit_solution(4379206535418123719)
XLA Ops:
  1.9 3.1 %collective-permute-start.15 = (bf16[128,2688]{1,0:T(8,128)(2,1)S(1)}, bf16[128,2688]{1,0:T(8,128)(2,1)S(1)}, u32[]{:S(2)}, u32[]{:S(2)}) collective-permute-start(bf16[128,2688]{1,0:T(8,128)(2,1)S(1)} %constant_dynamic-slice_fusion.1), channel_id=1, source_target_pairs={{0,4},{2,6},{4,0},{6,2},{8,12},{10,14},{12,8},{14,10},{1,5},{3,7},... | collective-permute-start | bytes 2064392 | tf_op jit(solution)/shard_map/ppermute | solution.py:239
  6.5 2.8 %shard_map.76 = (bf16[1536,128]{1,0:T(8,128)(2,1)}, bf16[1536,128]{1,0:T(8,128)(2,1)}, bf16[1536,128]{1,0:T(8,128)(2,1)}, bf16[1536,128]{1,0:T(8,128)(2,1)}, bf1...) custom-call(bf16[256,1024]{1,0:T(8,128)(2,1)} %q_ref.1, ...), custom_call_target="tpu_custom_call" | custom-call | bytes 2097152 | tf_op jit(solution)/shard_map/pallas_call | solution.py:257
  9.4 4.6 %collective-permute-start.3 = (bf16[512,128]{1,0:T(8,128)(2,1)}, bf16[512,128]{1,0:T(8,128)(2,1)S(1)}, u32[]{:S(2)}, u32[]{:S(2)}) collective-permute-start(bf16[512,128]{1,0:T(8,128)(2,1)} %get-tuple-element.39), channel_id=1, source_target_pairs={{0,8},{2,10},{4,12},{6,14},{1,9},{3,11},{5,13},{7,15},{16,24},{18,... | collective-permute-start | bytes 393224 | tf_op jit(solution)/shard_map/ppermute | solution.py:247
  16.6 7.2 %collective-permute-done.3.refs_4_ = bf16[512,128]{1,0:T(8,128)(2,1)S(1)} collective-permute-done((bf16[512,128]{1,0:T(8,128)(2,1)}, bf16[512,128]{1,0:T(8,128)(2,1)S(1)}, u32[]{:S(2)}, u32[]{:S(2)}) %collective-permute-start.3) | collective-permute-done | bytes 131104 | tf_op jit(solution)/shard_map/ppermute | solution.py:247
  26.6 2.8 %collective-permute-done.5.refs_6_ = bf16[512,128]{1,0:T(8,128)(2,1)S(1)} collective-permute-done((bf16[512,128]{1,0:T(8,128)(2,1)}, bf16[512,128]{1,0:T(8,128)(2,1)S(1)}, u32[]{:S(2)}, u32[]{:S(2)}) %collective-permute-start.5) | collective-permute-done | bytes 131104 | tf_op jit(solution)/shard_map/ppermute | solution.py:247
  30.5 6.6 %collective-permute-start.6 = (bf16[512,128]{1,0:T(8,128)(2,1)}, bf16[512,128]{1,0:T(8,128)(2,1)S(1)}, u32[]{:S(2)}, u32[]{:S(2)}) collective-permute-start(bf16[512,128]{1,0:T(8,128)(2,1)} %get-tuple-element.42), channel_id=1, source_target_pairs={{0,14},{2,12},{4,10},{6,8},{1,15},{3,13},{5,11},{7,9},{16,30},{18,... | collective-permute-start | bytes 393224 | tf_op jit(solution)/shard_map/ppermute | solution.py:247
  37.2 11.3 %collective-permute-done.6.refs_7_ = bf16[512,128]{1,0:T(8,128)(2,1)S(1)} collective-permute-done((bf16[512,128]{1,0:T(8,128)(2,1)}, bf16[512,128]{1,0:T(8,128)(2,1)S(1)}, u32[]{:S(2)}, u32[]{:S(2)}) %collective-permute-start.6) | collective-permute-done | bytes 131104 | tf_op jit(solution)/shard_map/ppermute | solution.py:247
  48.5 1.5 %collective-permute-start.21 = (bf16[64,2688]{1,0:T(8,128)(2,1)S(1)}, bf16[64,2688]{1,0:T(8,128)(2,1)S(1)}, u32[]{:S(2)}, u32[]{:S(2)}) collective-permute-start(bf16[64,2688]{1,0:T(8,128)(2,1)S(1)} %slice.8), channel_id=1, source_target_pairs={{0,2},{2,0},{4,6},{6,4},{8,10},{10,8},{12,14},{14,12},{1,3},{3,1},... | collective-permute-start | bytes 1032200 | tf_op jit(solution)/shard_map/ppermute | solution.py:239
  50.5 8.4 %shard_map.77 = (bf16[2048,128]{1,0:T(8,128)(2,1)S(1)}, bf16[1024,128]{1,0:T(8,128)(2,1)S(1)}, bf16[1024,128]{1,0:T(8,128)(2,1)S(1)}, f32[1024,128]{1,0:T(8,128)S(1)}, f32[1024,128]{1,0:T(8,128)S(1)}) custom-call(bf16[1536,128]{1,0:T(8,128)(2,1)S(1)} %copy-done.1, bf16[1536,128]{1,0:T(8,128)(2,1)S(1)} %collective-permute-done.refs_1_, ...), custom_call_target="tpu_custom_call" | custom-call | flops 3355443200 | bytes 4194304 | tf_op jit(solution)/shard_map/pallas_call | solution.py:286
  60.4 3.9 %collective-permute-done.21.refs_6_ = bf16[64,2688]{1,0:T(8,128)(2,1)S(1)} collective-permute-done((bf16[64,2688]{1,0:T(8,128)(2,1)S(1)}, bf16[64,2688]{1,0:T(8,128)(2,1)S(1)}, u32[]{:S(2)}, u32[]{:S(2)}) %collective-permute-start.21) | collective-permute-done | bytes 344096 | tf_op jit(solution)/shard_map/ppermute | solution.py:239
  64.3 22.7 %collective-permute-done.14.back_k = bf16[1024,128]{1,0:T(8,128)(2,1)S(1)} collective-permute-done((bf16[1024,128]{1,0:T(8,128)(2,1)S(1)}, bf16[1024,128]{1,0:T(8,128)(2,1)S(1)}, u32[]{:S(2)}, u32[]{:S(2)}) %collective-permute-start.14) | collective-permute-done | bytes 262176 | tf_op jit(solution)/shard_map/ppermute | solution.py:247
  87.0 1.5 %collective-permute-start.10 = (bf16[1024,128]{1,0:T(8,128)(2,1)S(1)}, bf16[1024,128]{1,0:T(8,128)(2,1)S(1)}, u32[]{:S(2)}, u32[]{:S(2)}) collective-permute-start(bf16[1024,128]{1,0:T(8,128)(2,1)S(1)} %get-tuple-element.49), channel_id=1, source_target_pairs={{8,0},{10,2},{12,4},{14,6},{9,1},{11,3},{13,5},{15,7},{24,16},{26,... | collective-permute-start | bytes 786440 | tf_op jit(solution)/shard_map/ppermute | solution.py:247
  88.6 1.6 %collective-permute-start.7 = (bf16[512,128]{1,0:T(8,128)(2,1)S(1)}, bf16[512,128]{1,0:T(8,128)(2,1)S(1)}, u32[]{:S(2)}, u32[]{:S(2)}) collective-permute-start(bf16[512,128]{1,0:T(8,128)(2,1)S(1)} %get-tuple-element.45), channel_id=1, source_target_pairs={{0,2},{2,0},{4,6},{6,4},{8,10},{10,8},{12,14},{14,12},{1,3},{3,1},... | collective-permute-start | bytes 393224 | tf_op jit(solution)/shard_map/ppermute | solution.py:239
  90.2 2.0 %collective-permute-start.9 = (bf16[512,128]{1,0:T(8,128)(2,1)S(1)}, bf16[512,128]{1,0:T(8,128)(2,1)S(1)}, u32[]{:S(2)}, u32[]{:S(2)}) collective-permute-start(bf16[512,128]{1,0:T(8,128)(2,1)S(1)} %get-tuple-element.47), channel_id=1, source_target_pairs={{0,6},{2,4},{4,2},{6,0},{8,14},{10,12},{12,10},{14,8},{1,7},{3,5},... | collective-permute-start | bytes 393224 | tf_op jit(solution)/shard_map/ppermute | solution.py:239
  92.2 3.0 %shard_map.80 = (bf16[336,128]{1,0:T(8,128)(2,1)S(1)}, bf16[336,128]{1,0:T(8,128)(2,1)S(1)}, bf16[336,128]{1,0:T(8,128)(2,1)S(1)}, bf16[336,128]{1,0:T(8,128)(2,...) custom-call(f32[1024,128]{1,0:T(8,128)S(1)} %get-tuple-element.54.ow, ...), custom_call_target="tpu_custom_call" | custom-call | flops 704643072 | bytes 8388608 | tf_op jit(solution)/shard_map/pallas_call | solution.py:327
  95.1 1.6 %collective-permute-start.23 = (bf16[336,128]{1,0:T(8,128)(2,1)S(1)}, bf16[336,128]{1,0:T(8,128)(2,1)S(1)}, u32[]{:S(2)}, u32[]{:S(2)}) collective-permute-start(bf16[336,128]{1,0:T(8,128)(2,1)S(1)} %get-tuple-element.57), channel_id=1, source_target_pairs={{0,2},{2,0},{4,6},{6,4},{8,10},{10,8},{12,14},{14,12},{1,3},{3,1},... | collective-permute-start | bytes 258056 | tf_op jit(solution)/shard_map/ppermute | solution.py:239
  98.2 1.6 %collective-permute-start.11 = (bf16[256,128]{1,0:T(8,128)(2,1)S(1)}, bf16[256,128]{1,0:T(8,128)(2,1)S(1)}, u32[]{:S(2)}, u32[]{:S(2)}) collective-permute-start(bf16[256,128]{1,0:T(8,128)(2,1)S(1)} %get-tuple-element.51), channel_id=1, source_target_pairs={{0,2},{2,0},{4,6},{6,4},{8,10},{10,8},{12,14},{14,12},{1,3},{3,1},... | collective-permute-start | bytes 196616 | tf_op jit(solution)/shard_map/ppermute | solution.py:239
  101.8 2.9 %collective-permute-done.9.refs_3_ = bf16[512,128]{1,0:T(8,128)(2,1)S(1)} collective-permute-done((bf16[512,128]{1,0:T(8,128)(2,1)S(1)}, bf16[512,128]{1,0:T(8,128)(2,1)S(1)}, u32[]{:S(2)}, u32[]{:S(2)}) %collective-permute-start.9) | collective-permute-done | bytes 131104 | tf_op jit(solution)/shard_map/ppermute | solution.py:239
  104.7 2.9 %collective-permute-start.25 = (bf16[336,128]{1,0:T(8,128)(2,1)S(1)}, bf16[336,128]{1,0:T(8,128)(2,1)S(1)}, u32[]{:S(2)}, u32[]{:S(2)}) collective-permute-start(bf16[336,128]{1,0:T(8,128)(2,1)S(1)} %get-tuple-element.59), channel_id=1, source_target_pairs={{0,6},{2,4},{4,2},{6,0},{8,14},{10,12},{12,10},{14,8},{1,7},{3,5},... | collective-permute-start | bytes 258056 | tf_op jit(solution)/shard_map/ppermute | solution.py:239
  107.6 2.2 %collective-permute-done.13.refs_7_ = bf16[256,128]{1,0:T(8,128)(2,1)S(1)} collective-permute-done((bf16[256,128]{1,0:T(8,128)(2,1)S(1)}, bf16[256,128]{1,0:T(8,128)(2,1)S(1)}, u32[]{:S(2)}, u32[]{:S(2)}) %collective-permute-start.13) | collective-permute-done | bytes 65568 | tf_op jit(solution)/shard_map/ppermute | solution.py:239
  110.6 2.4 %collective-permute-start.28 = (bf16[336,128]{1,0:T(8,128)(2,1)S(1)}, bf16[336,128]{1,0:T(8,128)(2,1)S(1)}, u32[]{:S(2)}, u32[]{:S(2)}) collective-permute-start(bf16[336,128]{1,0:T(8,128)(2,1)S(1)} %get-tuple-element.62), channel_id=1, source_target_pairs={{0,12},{2,14},{4,8},{6,10},{8,4},{10,6},{12,0},{14,2},{1,13},{3,15... | collective-permute-start | bytes 258056 | tf_op jit(solution)/shard_map/ppermute | solution.py:239
  112.9 2.4 %collective-permute-start.29 = (bf16[336,128]{1,0:T(8,128)(2,1)S(1)}, bf16[336,128]{1,0:T(8,128)(2,1)S(1)}, u32[]{:S(2)}, u32[]{:S(2)}) collective-permute-start(bf16[336,128]{1,0:T(8,128)(2,1)S(1)} %get-tuple-element.63), channel_id=1, source_target_pairs={{0,14},{2,12},{4,10},{6,8},{8,6},{10,4},{12,2},{14,0},{1,15},{3,13... | collective-permute-start | bytes 258056 | tf_op jit(solution)/shard_map/ppermute | solution.py:239
  115.3 3.9 %collective-permute-done.26.refs_12_ = bf16[336,128]{1,0:T(8,128)(2,1)S(1)} collective-permute-done((bf16[336,128]{1,0:T(8,128)(2,1)S(1)}, bf16[336,128]{1,0:T(8,128)(2,1)S(1)}, u32[]{:S(2)}, u32[]{:S(2)}) %collective-permute-start.26) | collective-permute-done | bytes 86048 | tf_op jit(solution)/shard_map/ppermute | solution.py:239
  119.2 2.6 %collective-permute-done.27.refs_13_ = bf16[336,128]{1,0:T(8,128)(2,1)S(1)} collective-permute-done((bf16[336,128]{1,0:T(8,128)(2,1)S(1)}, bf16[336,128]{1,0:T(8,128)(2,1)S(1)}, u32[]{:S(2)}, u32[]{:S(2)}) %collective-permute-start.27) | collective-permute-done | bytes 86048 | tf_op jit(solution)/shard_map/ppermute | solution.py:239
  (49 shorter events, 17.0 us)
Async XLA Ops:
  1.9 28.6 %collective-permute-start.15 = (bf16[128,2688]{1,0:T(8,128)(2,1)S(1)}, bf16[128,2688]{1,0:T(8,128)(2,1)S(1)}, u32[]{:S(2)}, u32[]{:S(2)}) collective-permute-start(bf16[128,2688]{1,0:T(8,128)(2,1)S(1)} %constant_dynamic-slice_fusion.1), channel_id=1, source_target_pairs={{0,4},{2,6},{4,0},{6,2},{8,12},{10,14},{12,8},{14,10},{1,5},{3,7},... | collective-permute-start | bytes 2064392 | tf_op jit(solution)/shard_map/ppermute | solution.py:239
  5.0 45.0 %collective-permute-start.19 = (bf16[128,2688]{1,0:T(8,128)(2,1)S(1)}, bf16[128,2688]{1,0:T(8,128)(2,1)S(1)}, u32[]{:S(2)}, u32[]{:S(2)}) collective-permute-start(bf16[128,2688]{1,0:T(8,128)(2,1)S(1)} %constant_dynamic-slice_fusion.1), channel_id=1, source_target_pairs={{0,2},{2,0},{4,6},{6,4},{8,10},{10,8},{12,14},{14,12},{1,3},{3,1},... | collective-permute-start | bytes 2064392 | tf_op jit(solution)/shard_map/ppermute | solution.py:239
  9.4 14.4 %collective-permute-start.3 = (bf16[512,128]{1,0:T(8,128)(2,1)}, bf16[512,128]{1,0:T(8,128)(2,1)S(1)}, u32[]{:S(2)}, u32[]{:S(2)}) collective-permute-start(bf16[512,128]{1,0:T(8,128)(2,1)} %get-tuple-element.39), channel_id=1, source_target_pairs={{0,8},{2,10},{4,12},{6,14},{1,9},{3,11},{5,13},{7,15},{16,24},{18,... | collective-permute-start | bytes 393224 | tf_op jit(solution)/shard_map/ppermute | solution.py:247
  14.0 12.6 %collective-permute-start.4 = (bf16[512,128]{1,0:T(8,128)(2,1)}, bf16[512,128]{1,0:T(8,128)(2,1)S(1)}, u32[]{:S(2)}, u32[]{:S(2)}) collective-permute-start(bf16[512,128]{1,0:T(8,128)(2,1)} %get-tuple-element.40), channel_id=1, source_target_pairs={{0,10},{2,8},{4,14},{6,12},{1,11},{3,9},{5,15},{7,13},{16,26},{18,... | collective-permute-start | bytes 393224 | tf_op jit(solution)/shard_map/ppermute | solution.py:247
  15.3 14.1 %collective-permute-start.5 = (bf16[512,128]{1,0:T(8,128)(2,1)}, bf16[512,128]{1,0:T(8,128)(2,1)S(1)}, u32[]{:S(2)}, u32[]{:S(2)}) collective-permute-start(bf16[512,128]{1,0:T(8,128)(2,1)} %get-tuple-element.41), channel_id=1, source_target_pairs={{0,12},{2,14},{4,8},{6,10},{1,13},{3,15},{5,9},{7,11},{16,28},{18,... | collective-permute-start | bytes 393224 | tf_op jit(solution)/shard_map/ppermute | solution.py:247
  23.8 24.7 %collective-permute-start = (bf16[1536,128]{1,0:T(8,128)(2,1)}, bf16[1536,128]{1,0:T(8,128)(2,1)S(1)}, u32[]{:S(2)}, u32[]{:S(2)}) collective-permute-start(bf16[1536,128]{1,0:T(8,128)(2,1)} %get-tuple-element.36), channel_id=1, source_target_pairs={{0,2},{2,0},{4,6},{6,4},{8,10},{10,8},{12,14},{14,12},{1,3},{3,1},... | collective-permute-start | bytes 1179656 | tf_op jit(solution)/shard_map/ppermute | solution.py:239
  26.6 23.4 %collective-permute-start.1 = (bf16[1536,128]{1,0:T(8,128)(2,1)}, bf16[1536,128]{1,0:T(8,128)(2,1)S(1)}, u32[]{:S(2)}, u32[]{:S(2)}) collective-permute-start(bf16[1536,128]{1,0:T(8,128)(2,1)} %get-tuple-element.37), channel_id=1, source_target_pairs={{0,4},{2,6},{4,0},{6,2},{8,12},{10,14},{12,8},{14,10},{1,5},{3,7},... | collective-permute-start | bytes 1179656 | tf_op jit(solution)/shard_map/ppermute | solution.py:239
  29.4 21.1 %collective-permute-start.2 = (bf16[1536,128]{1,0:T(8,128)(2,1)}, bf16[1536,128]{1,0:T(8,128)(2,1)S(1)}, u32[]{:S(2)}, u32[]{:S(2)}) collective-permute-start(bf16[1536,128]{1,0:T(8,128)(2,1)} %get-tuple-element.38), channel_id=1, source_target_pairs={{0,6},{2,4},{4,2},{6,0},{8,14},{10,12},{12,10},{14,8},{1,7},{3,5},... | collective-permute-start | bytes 1179656 | tf_op jit(solution)/shard_map/ppermute | solution.py:239
  30.5 17.9 %collective-permute-start.6 = (bf16[512,128]{1,0:T(8,128)(2,1)}, bf16[512,128]{1,0:T(8,128)(2,1)S(1)}, u32[]{:S(2)}, u32[]{:S(2)}) collective-permute-start(bf16[512,128]{1,0:T(8,128)(2,1)} %get-tuple-element.42), channel_id=1, source_target_pairs={{0,14},{2,12},{4,10},{6,8},{1,15},{3,13},{5,11},{7,9},{16,30},{18,... | collective-permute-start | bytes 393224 | tf_op jit(solution)/shard_map/ppermute | solution.py:247
  48.5 11.8 %collective-permute-start.17 = (bf16[64,2688]{1,0:T(8,128)(2,1)S(1)}, bf16[64,2688]{1,0:T(8,128)(2,1)S(1)}, u32[]{:S(2)}, u32[]{:S(2)}) collective-permute-start(bf16[64,2688]{1,0:T(8,128)(2,1)S(1)} %constant_dynamic-slice_fusion), channel_id=1, source_target_pairs={{0,6},{2,4},{4,2},{6,0},{8,14},{10,12},{12,10},{14,8},{1,7},{3,5},... | collective-permute-start | bytes 1032200 | tf_op jit(solution)/shard_map/ppermute | solution.py:239
  48.5 15.8 %collective-permute-start.21 = (bf16[64,2688]{1,0:T(8,128)(2,1)S(1)}, bf16[64,2688]{1,0:T(8,128)(2,1)S(1)}, u32[]{:S(2)}, u32[]{:S(2)}) collective-permute-start(bf16[64,2688]{1,0:T(8,128)(2,1)S(1)} %slice.8), channel_id=1, source_target_pairs={{0,2},{2,0},{4,6},{6,4},{8,10},{10,8},{12,14},{14,12},{1,3},{3,1},... | collective-permute-start | bytes 1032200 | tf_op jit(solution)/shard_map/ppermute | solution.py:239
  50.0 40.2 %collective-permute-start.16 = (bf16[128,2688]{1,0:T(8,128)(2,1)S(1)}, bf16[128,2688]{1,0:T(8,128)(2,1)S(1)}, u32[]{:S(2)}, u32[]{:S(2)}) collective-permute-start(bf16[128,2688]{1,0:T(8,128)(2,1)S(1)} %collective-permute-done.15.refs_0_), channel_id=1, source_target_pairs={{0,1},{1,0},{2,3},{3,2},{4,5},{5,4},{6,7},{7,6},{8,9},{9,8},{10,11... | collective-permute-start | bytes 2064392 | tf_op jit(solution)/shard_map/ppermute | solution.py:250
  50.0 40.2 %collective-permute-start.20 = (bf16[128,2688]{1,0:T(8,128)(2,1)S(1)}, bf16[128,2688]{1,0:T(8,128)(2,1)S(1)}, u32[]{:S(2)}, u32[]{:S(2)}) collective-permute-start(bf16[128,2688]{1,0:T(8,128)(2,1)S(1)} %collective-permute-done.19.refs_4_), channel_id=1, source_target_pairs={{0,1},{1,0},{2,3},{3,2},{4,5},{5,4},{6,7},{7,6},{8,9},{9,8},{10,11... | collective-permute-start | bytes 2064392 | tf_op jit(solution)/shard_map/ppermute | solution.py:250
  58.9 28.1 %collective-permute-start.14 = (bf16[1024,128]{1,0:T(8,128)(2,1)S(1)}, bf16[1024,128]{1,0:T(8,128)(2,1)S(1)}, u32[]{:S(2)}, u32[]{:S(2)}) collective-permute-start(bf16[1024,128]{1,0:T(8,128)(2,1)S(1)} %get-tuple-element.55), channel_id=1, source_target_pairs={{8,0},{10,2},{12,4},{14,6},{9,1},{11,3},{13,5},{15,7},{24,16},{26,... | collective-permute-start | bytes 786440 | tf_op jit(solution)/shard_map/ppermute | solution.py:247
  60.2 28.3 %collective-permute-start.18 = (bf16[64,2688]{1,0:T(8,128)(2,1)S(1)}, bf16[64,2688]{1,0:T(8,128)(2,1)S(1)}, u32[]{:S(2)}, u32[]{:S(2)}) collective-permute-start(bf16[64,2688]{1,0:T(8,128)(2,1)S(1)} %collective-permute-done.17.refs_2_), channel_id=1, source_target_pairs={{0,1},{1,0},{2,3},{3,2},{4,5},{5,4},{6,7},{7,6},{8,9},{9,8},{10,11... | collective-permute-start | bytes 1032200 | tf_op jit(solution)/shard_map/ppermute | solution.py:250
  64.3 27.9 %collective-permute-start.22 = (bf16[64,2688]{1,0:T(8,128)(2,1)S(1)}, bf16[64,2688]{1,0:T(8,128)(2,1)S(1)}, u32[]{:S(2)}, u32[]{:S(2)}) collective-permute-start(bf16[64,2688]{1,0:T(8,128)(2,1)S(1)} %collective-permute-done.21.refs_6_), channel_id=1, source_target_pairs={{0,1},{1,0},{2,3},{3,2},{4,5},{5,4},{6,7},{7,6},{8,9},{9,8},{10,11... | collective-permute-start | bytes 1032200 | tf_op jit(solution)/shard_map/ppermute | solution.py:250
  87.0 11.1 %collective-permute-start.10 = (bf16[1024,128]{1,0:T(8,128)(2,1)S(1)}, bf16[1024,128]{1,0:T(8,128)(2,1)S(1)}, u32[]{:S(2)}, u32[]{:S(2)}) collective-permute-start(bf16[1024,128]{1,0:T(8,128)(2,1)S(1)} %get-tuple-element.49), channel_id=1, source_target_pairs={{8,0},{10,2},{12,4},{14,6},{9,1},{11,3},{13,5},{15,7},{24,16},{26,... | collective-permute-start | bytes 786440 | tf_op jit(solution)/shard_map/ppermute | solution.py:247
  90.2 10.8 %collective-permute-start.8 = (bf16[512,128]{1,0:T(8,128)(2,1)S(1)}, bf16[512,128]{1,0:T(8,128)(2,1)S(1)}, u32[]{:S(2)}, u32[]{:S(2)}) collective-permute-start(bf16[512,128]{1,0:T(8,128)(2,1)S(1)} %get-tuple-element.46), channel_id=1, source_target_pairs={{0,4},{2,6},{4,0},{6,2},{8,12},{10,14},{12,8},{14,10},{1,5},{3,7},... | collective-permute-start | bytes 393224 | tf_op jit(solution)/shard_map/ppermute | solution.py:239
  90.2 14.5 %collective-permute-start.9 = (bf16[512,128]{1,0:T(8,128)(2,1)S(1)}, bf16[512,128]{1,0:T(8,128)(2,1)S(1)}, u32[]{:S(2)}, u32[]{:S(2)}) collective-permute-start(bf16[512,128]{1,0:T(8,128)(2,1)S(1)} %get-tuple-element.47), channel_id=1, source_target_pairs={{0,6},{2,4},{4,2},{6,0},{8,14},{10,12},{12,10},{14,8},{1,7},{3,5},... | collective-permute-start | bytes 393224 | tf_op jit(solution)/shard_map/ppermute | solution.py:239
  95.1 15.4 %collective-permute-start.23 = (bf16[336,128]{1,0:T(8,128)(2,1)S(1)}, bf16[336,128]{1,0:T(8,128)(2,1)S(1)}, u32[]{:S(2)}, u32[]{:S(2)}) collective-permute-start(bf16[336,128]{1,0:T(8,128)(2,1)S(1)} %get-tuple-element.57), channel_id=1, source_target_pairs={{0,2},{2,0},{4,6},{6,4},{8,10},{10,8},{12,14},{14,12},{1,3},{3,1},... | collective-permute-start | bytes 258056 | tf_op jit(solution)/shard_map/ppermute | solution.py:239
  98.2 14.8 %collective-permute-start.24 = (bf16[336,128]{1,0:T(8,128)(2,1)S(1)}, bf16[336,128]{1,0:T(8,128)(2,1)S(1)}, u32[]{:S(2)}, u32[]{:S(2)}) collective-permute-start(bf16[336,128]{1,0:T(8,128)(2,1)S(1)} %get-tuple-element.58), channel_id=1, source_target_pairs={{0,4},{2,6},{4,0},{6,2},{8,12},{10,14},{12,8},{14,10},{1,5},{3,7},... | collective-permute-start | bytes 258056 | tf_op jit(solution)/shard_map/ppermute | solution.py:239
  107.6 11.5 %collective-permute-start.26 = (bf16[336,128]{1,0:T(8,128)(2,1)S(1)}, bf16[336,128]{1,0:T(8,128)(2,1)S(1)}, u32[]{:S(2)}, u32[]{:S(2)}) collective-permute-start(bf16[336,128]{1,0:T(8,128)(2,1)S(1)} %get-tuple-element.60), channel_id=1, source_target_pairs={{0,8},{2,10},{4,12},{6,14},{8,0},{10,2},{12,4},{14,6},{1,9},{3,11}... | collective-permute-start | bytes 258056 | tf_op jit(solution)/shard_map/ppermute | solution.py:239
  109.9 11.9 %collective-permute-start.27 = (bf16[336,128]{1,0:T(8,128)(2,1)S(1)}, bf16[336,128]{1,0:T(8,128)(2,1)S(1)}, u32[]{:S(2)}, u32[]{:S(2)}) collective-permute-start(bf16[336,128]{1,0:T(8,128)(2,1)S(1)} %get-tuple-element.61), channel_id=1, source_target_pairs={{0,10},{2,8},{4,14},{6,12},{8,2},{10,0},{12,6},{14,4},{1,11},{3,9}... | collective-permute-start | bytes 258056 | tf_op jit(solution)/shard_map/ppermute | solution.py:239
  110.6 11.2 %collective-permute-start.28 = (bf16[336,128]{1,0:T(8,128)(2,1)S(1)}, bf16[336,128]{1,0:T(8,128)(2,1)S(1)}, u32[]{:S(2)}, u32[]{:S(2)}) collective-permute-start(bf16[336,128]{1,0:T(8,128)(2,1)S(1)} %get-tuple-element.62), channel_id=1, source_target_pairs={{0,12},{2,14},{4,8},{6,10},{8,4},{10,6},{12,0},{14,2},{1,13},{3,15... | collective-permute-start | bytes 258056 | tf_op jit(solution)/shard_map/ppermute | solution.py:239
  (8 other events, 125.0 us)

commit v4 on v3

--- a/solution.py
+++ b/solution.py
@@ -74,7 +74,7 @@
 def attention_kernel(parts, rows, *refs):
     full, cross = refs[:parts], refs[parts : 2 * parts]
     dq_s, back_k, back_v, own_k, own_v = refs[2 * parts : 2 * parts + 5]
-    q_s, d_s, k_s, v_s, dk_s, dv_s, sems = refs[2 * parts + 5 :]
+    q_s, d_s, k_s, v_s, dk_s, dv_s, s_s, p_s, sems = refs[2 * parts + 5 :]
     place = place_of(parts)
     first = lax.axis_index("ctx") < parts
     span = parts * rows
@@ -102,63 +102,83 @@
     for copy in copies:
         copy.wait()
 
-    key_at = lax.broadcasted_iota(jnp.int32, (rows, wide), 0)
-    query_at = lax.broadcasted_iota(jnp.int32, (rows, wide), 1) % rows
-    older = key_at > query_at
+    key_at = lax.broadcasted_iota(jnp.int32, (rows, rows), 0)
+    older = key_at > lax.broadcasted_iota(jnp.int32, (rows, rows), 1)
     nt = (((1,), (1,)), ((), ()))
     chunks = parts + 1
     hidden = jnp.float32(-jnp.inf)
 
-    def one_block(block, skipped):
-        pair = slice(block * wide, (block + 1) * wide)
-        queries = q_s[pair, :]
-        grads = d_s[pair, :]
-
-        def keys_of(chunk):
-            return slice((block + chunk) * rows, (block + chunk + 1) * rows)
-
-        used = [chunk for chunk in range(chunks) if block + chunk >= skipped]
-        scores = {}
-        for chunk in used:
-            s = lax.dot_general(k_s[keys_of(chunk), :], queries, nt, preferred_element_type=jnp.float32)
-            s = s * (attn_scale * log2_e)
-            if chunk == 0:
-                s = jnp.where(older, s, hidden)
-            if chunk == chunks - 1:
-                s = jnp.where(older, hidden, s)
-            scores[chunk] = s
-        top = functools.reduce(jnp.maximum, [jnp.max(s, axis=0, keepdims=True) for s in scores.values()])
-        total = jnp.zeros((1, wide), jnp.float32)
-        delta = jnp.zeros((1, wide), jnp.float32)
-        raised, probs = {}, {}
-        for chunk in used:
-            e = jnp.exp2(scores[chunk] - top)
-            dp = lax.dot_general(v_s[keys_of(chunk), :], grads, nt, preferred_element_type=jnp.float32)
-            total = total + jnp.sum(e, axis=0, keepdims=True)
-            delta = delta + jnp.sum(e * dp, axis=0, keepdims=True)
-            raised[chunk] = e
-            probs[chunk] = dp
-        inverse = 1.0 / total
-        delta = delta * inverse
-        dq = jnp.zeros((HD, wide), jnp.float32)
-        for chunk in used:
-            soft = raised[chunk] * inverse
-            ds = (soft * (probs[chunk] - delta)).astype(jnp.bfloat16)
-            low = soft.astype(jnp.bfloat16)
-            here = keys_of(chunk)
-            dv_s[here, :] += jnp.dot(low, grads, preferred_element_type=jnp.float32)
-            dk_s[here, :] += jnp.dot(ds, queries, preferred_element_type=jnp.float32)
-            dq += lax.dot_general(
-                k_s[here, :], ds, (((0,), (0,)), ((), ())), preferred_element_type=jnp.float32
-            )
-        dq_s[pair, :] = (attn_scale * dq).T.astype(jnp.bfloat16)
+    def queries_of(task):
+        at = (task // GROUP) * wide + (task % GROUP) * rows
+        return slice(at, at + rows)
+
+    def keys_of(task, chunk):
+        at = (task // GROUP + chunk) * rows
+        return slice(at, at + rows)
+
+    def held(chunk):
+        return slice(chunk * rows, (chunk + 1) * rows)
+
+    def scores(task, chunk):
+        keys, slot = keys_of(task, chunk), task % 2
+        s = lax.dot_general(k_s[keys, :], q_s[queries_of(task), :], nt, preferred_element_type=jnp.float32)
+        s = s * (attn_scale * log2_e)
+        if chunk == 0:
+            s = jnp.where(older, s, hidden)
+        if chunk == chunks - 1:
+            s = jnp.where(older, hidden, s)
+        s_s[slot, held(chunk), :] = s
+        p_s[slot, held(chunk), :] = lax.dot_general(
+            v_s[keys, :], d_s[queries_of(task), :], nt, preferred_element_type=jnp.float32
+        )
+        return jnp.max(s, axis=0, keepdims=True)
+
+    def all_tasks(skipped):
+        count = parts * GROUP
+
+        def used(task):
+            return [chunk for chunk in range(chunks) if task // GROUP + chunk >= skipped]
+
+        top = functools.reduce(jnp.maximum, [scores(0, chunk) for chunk in used(0)])
+        for task in range(count):
+            slot = task % 2
+            total = jnp.zeros((1, rows), jnp.float32)
+            delta = jnp.zeros((1, rows), jnp.float32)
+            tops = []
+            following = list(used(task + 1)) if task + 1 < count else []
+            for chunk in used(task):
+                e = jnp.exp2(s_s[slot, held(chunk), :] - top)
+                s_s[slot, held(chunk), :] = e
+                total = total + jnp.sum(e, axis=0, keepdims=True)
+                delta = delta + jnp.sum(e * p_s[slot, held(chunk), :], axis=0, keepdims=True)
+                if following:
+                    tops.append(scores(task + 1, following.pop(0)))
+            inverse = 1.0 / total
+            delta = delta * inverse
+            dq = jnp.zeros((HD, rows), jnp.float32)
+            for chunk in used(task):
+                soft = s_s[slot, held(chunk), :] * inverse
+                ds = (soft * (p_s[slot, held(chunk), :] - delta)).astype(jnp.bfloat16)
+                low = soft.astype(jnp.bfloat16)
+                here = keys_of(task, chunk)
+                dv_s[here, :] += jnp.dot(low, d_s[queries_of(task), :], preferred_element_type=jnp.float32)
+                dk_s[here, :] += jnp.dot(ds, q_s[queries_of(task), :], preferred_element_type=jnp.float32)
+                dq += lax.dot_general(
+                    k_s[here, :], ds, (((0,), (0,)), ((), ())), preferred_element_type=jnp.float32
+                )
+                if following:
+                    tops.append(scores(task + 1, following.pop(0)))
+            dq_s[queries_of(task), :] = (attn_scale * dq).T.astype(jnp.bfloat16)
+            while following:
+                tops.append(scores(task + 1, following.pop(0)))
+            if tops:
+                top = functools.reduce(jnp.maximum, tops)
 
     for skipped, here in ((parts, first), (0, jnp.logical_not(first))):
 
         @pl.when(here)
         def _(skipped=skipped):
-            for block in range(parts):
-                one_block(block, skipped)
+            all_tasks(skipped)
 
     back_k[...] = (attn_scale * dk_s[:span, :]).astype(jnp.bfloat16)
     own_k[...] = attn_scale * dk_s[span:, :]
@@ -204,10 +224,13 @@
         outs[slot][...] = value[pl.ds(pl.multiple_of(at, rows), rows), :]
 
 
-def value_kernel(parts, rows, own_v, back_v, *outs):
+def value_kernel(parts, rows, own_v, back_v, *refs):
+    terms, outs = refs[:-parts], refs[-parts:]
     for slot in range(parts):
         at = pl.ds(pl.multiple_of((place_of(parts) ^ slot) * rows, rows), rows)
-        outs[slot][...] = (own_v[at, :] + back_v[at, :].astype(jnp.float32)).astype(jnp.bfloat16)
+        outs[slot][:rows, :] = (own_v[at, :] + back_v[at, :].astype(jnp.float32)).astype(jnp.bfloat16)
+        if terms:
+            outs[slot][rows:, :] = terms[slot][...]
 
 
 def spread_kernel(parts, *refs):
@@ -221,9 +244,9 @@
             at = pl.ds(pl.multiple_of((head * GROUP + g) * HD, HD), HD)
             outs[0][:, at] = dq[slot][g * rows : (g + 1) * rows, :]
         at = pl.ds(pl.multiple_of(head * HD, HD), HD)
-        outs[1][:, at] = dv[slot][...]
+        outs[1][:, at] = dv[slot][:rows, :]
         if terms:
-            outs[2][:, at] = terms[slot][...].astype(jnp.float32) + terms[slot + parts][...].astype(jnp.float32)
+            outs[2][:, at] = dv[slot][rows:, :].astype(jnp.float32) + terms[slot][...].astype(jnp.float32)
 
 
 def shards(normed_input, attn_queries, attn_keys, attn_values, out_grad):
@@ -296,6 +319,8 @@
             pltpu.VMEM((2 * span, HD), jnp.bfloat16),
             pltpu.VMEM((2 * span, HD), jnp.float32),
             pltpu.VMEM((2 * span, HD), jnp.float32),
+            pltpu.VMEM((2, span + rows, rows), jnp.float32),
+            pltpu.VMEM((2, span + rows, rows), jnp.float32),
             pltpu.SemaphoreType.DMA((6 * parts,)),
         ],
         flops=10 * pairs * HD,
@@ -313,15 +338,6 @@
         functools.partial(split_kernel, parts, wide), [shape((wide, HD))] * parts, [VMEM], [VMEM] * parts, moved=1 << 20
     )(dq)
     got_dq = exchanged(dq_parts)
-    dv_parts = call(
-        functools.partial(value_kernel, parts, rows),
-        [shape((rows, HD))] * parts,
-        [VMEM] * 2,
-        [VMEM] * parts,
-        moved=1 << 20,
-    )(own_v, got_v)
-    got_dv = exchanged(dv_parts)
-
     piece = features // count
     direct = blocks == 2
     terms = call(
@@ -339,9 +355,16 @@
         moved=8 << 20,
         room=24,
     )(own_k, got_k, normed_input, *x_pieces)
-    got_terms = []
-    if direct:
-        got_terms = [terms[0]] + [within(terms[slot], slot) for slot in range(1, count)]
+    near_terms = terms[:parts] if direct else []
+    got_terms = [within(terms[slot], slot) for slot in range(parts, count)] if direct else []
+    dv_parts = call(
+        functools.partial(value_kernel, parts, rows),
+        [shape((rows + (piece if direct else 0), HD))] * parts,
+        [VMEM] * (2 + len(near_terms)),
+        [VMEM] * parts,
+        moved=1 << 20,
+    )(own_v, got_v, *near_terms)
+    got_dv = exchanged(dv_parts)
 
     outs = call(
         functools.partial(spread_kernel, parts),

time: 124 us -> 119 us (0.960)
  starting transfers between devices: 41.8 us -> 38.6 us
    ppermute x20 -> x17, starting transfers between devices: 24.6 us -> 21.3 us  [within(): return lax.ppermute(value, 'ctx', [(s, s ^ slot) for s in range(count)])]
    ppermute x6, waiting for transfers between devices: 46.8 us -> 44.6 us  [across(): return lax.ppermute(value, 'ctx', perm)]
    ppermute x20 -> x17, waiting for transfers between devices: 16.7 us -> 18.1 us  [within(): return lax.ppermute(value, 'ctx', [(s, s ^ slot) for s in range(count)])]
  transfers between devices with their start and end apart: 30 -> 27, of which waited for: 12 -> 11; matrix products, arithmetic and copies ran while one was open for 0% -> 0% of each run, Pallas kernels for 12% -> 12%
where the time goes in v4:
time: 119 us
  waiting for transfers between devices  62.7 us (53%)
  starting transfers between devices  38.6 us (32%)
  Pallas kernels  15.2 us (13%)
  local copies, waits for them, and re-layouts  1.33 us (1%)
    ppermute x6, waiting for transfers between devices, across(): return lax.ppermute(value, 'ctx', perm)  44.6 us
    ppermute x17, starting transfers between devices, within(): return lax.ppermute(value, 'ctx', [(s, s ^ slot) for s in range(count)])  21.3 us
    ppermute x17, waiting for transfers between devices, within(): return lax.ppermute(value, 'ctx', [(s, s ^ slot) for s in range(count)])  18.1 us
    ppermute x6, starting transfers between devices, across(): return lax.ppermute(value, 'ctx', perm)  16.6 us
    pallas_call x1, Pallas kernels, shards(): call(functools.partial(attention_kernel, parts, rows), [shape((parts * wi...  7.95 us
    pallas_call x1, Pallas kernels, shards(): call(functools.partial(weight_kernel, parts, count, rows, spots), [shape(...  2.95 us
    pallas_call x1, Pallas kernels, pack(): call(functools.partial(pack_kernel, parts, slots, crosses), [shape(dims)...  2.84 us
  transfers between devices with their start and end apart: 27, of which 11 were waited for; matrix products, arithmetic and copies ran while one was open for 0% of the time, Pallas kernels for 12%

profile of v4, /device:TPU:0, one launch (start us, length us, event | category | flops | bytes accessed | tf_op | source)
XLA Modules:
  0.0 118.7 jit_solution(12745717967111589875)
XLA Ops:
  1.9 3.1 %collective-permute-start.12 = (bf16[128,2688]{1,0:T(8,128)(2,1)S(1)}, bf16[128,2688]{1,0:T(8,128)(2,1)S(1)}, u32[]{:S(2)}, u32[]{:S(2)}) collective-permute-start(bf16[128,2688]{1,0:T(8,128)(2,1)S(1)} %constant_dynamic-slice_fusion.1), channel_id=1, source_target_pairs={{0,4},{2,6},{4,0},{6,2},{8,12},{10,14},{12,8},{14,10},{1,5},{3,7},... | collective-permute-start | bytes 2064392 | tf_op jit(solution)/shard_map/ppermute | solution.py:262
  5.0 1.5 %collective-permute-start.16 = (bf16[128,2688]{1,0:T(8,128)(2,1)S(1)}, bf16[128,2688]{1,0:T(8,128)(2,1)S(1)}, u32[]{:S(2)}, u32[]{:S(2)}) collective-permute-start(bf16[128,2688]{1,0:T(8,128)(2,1)S(1)} %constant_dynamic-slice_fusion.1), channel_id=1, source_target_pairs={{0,2},{2,0},{4,6},{6,4},{8,10},{10,8},{12,14},{14,12},{1,3},{3,1},... | collective-permute-start | bytes 2064392 | tf_op jit(solution)/shard_map/ppermute | solution.py:262
  6.5 2.8 %shard_map.76 = (bf16[1536,128]{1,0:T(8,128)(2,1)}, bf16[1536,128]{1,0:T(8,128)(2,1)}, bf16[1536,128]{1,0:T(8,128)(2,1)}, bf16[1536,128]{1,0:T(8,128)(2,1)}, bf1...) custom-call(bf16[256,1024]{1,0:T(8,128)(2,1)} %q_ref.1, ...), custom_call_target="tpu_custom_call" | custom-call | bytes 2097152 | tf_op jit(solution)/shard_map/pallas_call | solution.py:280
  9.4 4.6 %collective-permute-start.3 = (bf16[512,128]{1,0:T(8,128)(2,1)}, bf16[512,128]{1,0:T(8,128)(2,1)S(1)}, u32[]{:S(2)}, u32[]{:S(2)}) collective-permute-start(bf16[512,128]{1,0:T(8,128)(2,1)} %get-tuple-element.39), channel_id=1, source_target_pairs={{0,8},{2,10},{4,12},{6,14},{1,9},{3,11},{5,13},{7,15},{16,24},{18,... | collective-permute-start | bytes 393224 | tf_op jit(solution)/shard_map/ppermute | solution.py:270
  16.6 7.2 %collective-permute-done.3.refs_4_ = bf16[512,128]{1,0:T(8,128)(2,1)S(1)} collective-permute-done((bf16[512,128]{1,0:T(8,128)(2,1)}, bf16[512,128]{1,0:T(8,128)(2,1)S(1)}, u32[]{:S(2)}, u32[]{:S(2)}) %collective-permute-start.3) | collective-permute-done | bytes 131104 | tf_op jit(solution)/shard_map/ppermute | solution.py:270
  23.8 1.5 %collective-permute-start = (bf16[1536,128]{1,0:T(8,128)(2,1)}, bf16[1536,128]{1,0:T(8,128)(2,1)S(1)}, u32[]{:S(2)}, u32[]{:S(2)}) collective-permute-start(bf16[1536,128]{1,0:T(8,128)(2,1)} %get-tuple-element.36), channel_id=1, source_target_pairs={{0,2},{2,0},{4,6},{6,4},{8,10},{10,8},{12,14},{14,12},{1,3},{3,1},... | collective-permute-start | bytes 1179656 | tf_op jit(solution)/shard_map/ppermute | solution.py:262
  26.6 2.8 %collective-permute-done.5.refs_6_ = bf16[512,128]{1,0:T(8,128)(2,1)S(1)} collective-permute-done((bf16[512,128]{1,0:T(8,128)(2,1)}, bf16[512,128]{1,0:T(8,128)(2,1)S(1)}, u32[]{:S(2)}, u32[]{:S(2)}) %collective-permute-start.5) | collective-permute-done | bytes 131104 | tf_op jit(solution)/shard_map/ppermute | solution.py:270
  30.6 6.6 %collective-permute-start.6 = (bf16[512,128]{1,0:T(8,128)(2,1)}, bf16[512,128]{1,0:T(8,128)(2,1)S(1)}, u32[]{:S(2)}, u32[]{:S(2)}) collective-permute-start(bf16[512,128]{1,0:T(8,128)(2,1)} %get-tuple-element.42), channel_id=1, source_target_pairs={{0,14},{2,12},{4,10},{6,8},{1,15},{3,13},{5,11},{7,9},{16,30},{18,... | collective-permute-start | bytes 393224 | tf_op jit(solution)/shard_map/ppermute | solution.py:270
  37.2 11.3 %collective-permute-done.6.refs_7_ = bf16[512,128]{1,0:T(8,128)(2,1)S(1)} collective-permute-done((bf16[512,128]{1,0:T(8,128)(2,1)}, bf16[512,128]{1,0:T(8,128)(2,1)S(1)}, u32[]{:S(2)}, u32[]{:S(2)}) %collective-permute-start.6) | collective-permute-done | bytes 131104 | tf_op jit(solution)/shard_map/ppermute | solution.py:270
  48.5 1.5 %collective-permute-start.18 = (bf16[64,2688]{1,0:T(8,128)(2,1)S(1)}, bf16[64,2688]{1,0:T(8,128)(2,1)S(1)}, u32[]{:S(2)}, u32[]{:S(2)}) collective-permute-start(bf16[64,2688]{1,0:T(8,128)(2,1)S(1)} %slice.8), channel_id=1, source_target_pairs={{0,2},{2,0},{4,6},{6,4},{8,10},{10,8},{12,14},{14,12},{1,3},{3,1},... | collective-permute-start | bytes 1032200 | tf_op jit(solution)/shard_map/ppermute | solution.py:262
  50.5 8.0 %shard_map.77 = (bf16[2048,128]{1,0:T(8,128)(2,1)S(1)}, bf16[1024,128]{1,0:T(8,128)(2,1)S(1)}, bf16[1024,128]{1,0:T(8,128)(2,1)S(1)}, f32[1024,128]{1,0:T(8,128)S(1)}, f32[1024,128]{1,0:T(8,128)S(1)}) custom-call(bf16[1536,128]{1,0:T(8,128)(2,1)S(1)} %copy-done.1, bf16[1536,128]{1,0:T(8,128)(2,1)S(1)} %collective-permute-done.refs_1_, ...), custom_call_target="tpu_custom_call" | custom-call | flops 3355443200 | bytes 4194304 | tf_op jit(solution)/shard_map/pallas_call | solution.py:309
  59.9 4.4 %collective-permute-done.18.refs_6_ = bf16[64,2688]{1,0:T(8,128)(2,1)S(1)} collective-permute-done((bf16[64,2688]{1,0:T(8,128)(2,1)S(1)}, bf16[64,2688]{1,0:T(8,128)(2,1)S(1)}, u32[]{:S(2)}, u32[]{:S(2)}) %collective-permute-start.18) | collective-permute-done | bytes 344096 | tf_op jit(solution)/shard_map/ppermute | solution.py:262
  64.3 22.0 %collective-permute-done.11.back_k = bf16[1024,128]{1,0:T(8,128)(2,1)S(1)} collective-permute-done((bf16[1024,128]{1,0:T(8,128)(2,1)S(1)}, bf16[1024,128]{1,0:T(8,128)(2,1)S(1)}, u32[]{:S(2)}, u32[]{:S(2)}) %collective-permute-start.11) | collective-permute-done | bytes 262176 | tf_op jit(solution)/shard_map/ppermute | solution.py:270
  86.3 1.5 %collective-permute-start.10 = (bf16[1024,128]{1,0:T(8,128)(2,1)S(1)}, bf16[1024,128]{1,0:T(8,128)(2,1)S(1)}, u32[]{:S(2)}, u32[]{:S(2)}) collective-permute-start(bf16[1024,128]{1,0:T(8,128)(2,1)S(1)} %get-tuple-element.49), channel_id=1, source_target_pairs={{8,0},{10,2},{12,4},{14,6},{9,1},{11,3},{13,5},{15,7},{24,16},{26,... | collective-permute-start | bytes 786440 | tf_op jit(solution)/shard_map/ppermute | solution.py:270
  87.9 1.6 %collective-permute-start.7 = (bf16[512,128]{1,0:T(8,128)(2,1)S(1)}, bf16[512,128]{1,0:T(8,128)(2,1)S(1)}, u32[]{:S(2)}, u32[]{:S(2)}) collective-permute-start(bf16[512,128]{1,0:T(8,128)(2,1)S(1)} %get-tuple-element.45), channel_id=1, source_target_pairs={{0,2},{2,0},{4,6},{6,4},{8,10},{10,8},{12,14},{14,12},{1,3},{3,1},... | collective-permute-start | bytes 393224 | tf_op jit(solution)/shard_map/ppermute | solution.py:262
  89.4 2.0 %collective-permute-start.9 = (bf16[512,128]{1,0:T(8,128)(2,1)S(1)}, bf16[512,128]{1,0:T(8,128)(2,1)S(1)}, u32[]{:S(2)}, u32[]{:S(2)}) collective-permute-start(bf16[512,128]{1,0:T(8,128)(2,1)S(1)} %get-tuple-element.47), channel_id=1, source_target_pairs={{0,6},{2,4},{4,2},{6,0},{8,14},{10,12},{12,10},{14,8},{1,7},{3,5},... | collective-permute-start | bytes 393224 | tf_op jit(solution)/shard_map/ppermute | solution.py:262
  91.4 3.0 %shard_map.79 = (bf16[336,128]{1,0:T(8,128)(2,1)S(1)}, bf16[336,128]{1,0:T(8,128)(2,1)S(1)}, bf16[336,128]{1,0:T(8,128)(2,1)S(1)}, bf16[336,128]{1,0:T(8,128)(2,...) custom-call(f32[1024,128]{1,0:T(8,128)S(1)} %get-tuple-element.50.ow, ...), custom_call_target="tpu_custom_call" | custom-call | flops 704643072 | bytes 8388608 | tf_op jit(solution)/shard_map/pallas_call | solution.py:343
  94.4 3.6 %collective-permute-start.23 = (bf16[336,128]{1,0:T(8,128)(2,1)S(1)}, bf16[336,128]{1,0:T(8,128)(2,1)S(1)}, u32[]{:S(2)}, u32[]{:S(2)}) collective-permute-start(bf16[336,128]{1,0:T(8,128)(2,1)S(1)} %get-tuple-element.60), channel_id=1, source_target_pairs={{0,8},{2,10},{4,12},{6,14},{8,0},{10,2},{12,4},{14,6},{1,9},{3,11}... | collective-permute-start | bytes 258056 | tf_op jit(solution)/shard_map/ppermute | solution.py:262
  99.7 2.5 %collective-permute-done.8.refs_2_ = bf16[512,128]{1,0:T(8,128)(2,1)S(1)} collective-permute-done((bf16[512,128]{1,0:T(8,128)(2,1)S(1)}, bf16[512,128]{1,0:T(8,128)(2,1)S(1)}, u32[]{:S(2)}, u32[]{:S(2)}) %collective-permute-start.8) | collective-permute-done | bytes 131104 | tf_op jit(solution)/shard_map/ppermute | solution.py:262
  102.2 5.4 %collective-permute-done.9.refs_3_ = bf16[512,128]{1,0:T(8,128)(2,1)S(1)} collective-permute-done((bf16[512,128]{1,0:T(8,128)(2,1)S(1)}, bf16[512,128]{1,0:T(8,128)(2,1)S(1)}, u32[]{:S(2)}, u32[]{:S(2)}) %collective-permute-start.9) | collective-permute-done | bytes 131104 | tf_op jit(solution)/shard_map/ppermute | solution.py:262
  107.7 3.8 %collective-permute-start.26 = (bf16[336,128]{1,0:T(8,128)(2,1)S(1)}, bf16[336,128]{1,0:T(8,128)(2,1)S(1)}, u32[]{:S(2)}, u32[]{:S(2)}) collective-permute-start(bf16[336,128]{1,0:T(8,128)(2,1)S(1)} %get-tuple-element.63), channel_id=1, source_target_pairs={{0,14},{2,12},{4,10},{6,8},{8,6},{10,4},{12,2},{14,0},{1,15},{3,13... | collective-permute-start | bytes 258056 | tf_op jit(solution)/shard_map/ppermute | solution.py:262
  111.5 2.5 %collective-permute-done.25.refs_10_ = bf16[336,128]{1,0:T(8,128)(2,1)S(1)} collective-permute-done((bf16[336,128]{1,0:T(8,128)(2,1)S(1)}, bf16[336,128]{1,0:T(8,128)(2,1)S(1)}, u32[]{:S(2)}, u32[]{:S(2)}) %collective-permute-start.25) | collective-permute-done | bytes 86048 | tf_op jit(solution)/shard_map/ppermute | solution.py:262
  114.0 1.8 %collective-permute-done.26.refs_11_ = bf16[336,128]{1,0:T(8,128)(2,1)S(1)} collective-permute-done((bf16[336,128]{1,0:T(8,128)(2,1)S(1)}, bf16[336,128]{1,0:T(8,128)(2,1)S(1)}, u32[]{:S(2)}, u32[]{:S(2)}) %collective-permute-start.26) | collective-permute-done | bytes 86048 | tf_op jit(solution)/shard_map/ppermute | solution.py:262
  115.8 1.5 %collective-permute-done.22.refs_7_ = bf16[592,128]{1,0:T(8,128)(2,1)S(1)} collective-permute-done((bf16[592,128]{1,0:T(8,128)(2,1)S(1)}, bf16[592,128]{1,0:T(8,128)(2,1)S(1)}, u32[]{:S(2)}, u32[]{:S(2)}) %collective-permute-start.22) | collective-permute-done | bytes 151584 | tf_op jit(solution)/shard_map/ppermute | solution.py:262
  (43 shorter events, 11.5 us)
Async XLA Ops:
  1.9 28.6 %collective-permute-start.12 = (bf16[128,2688]{1,0:T(8,128)(2,1)S(1)}, bf16[128,2688]{1,0:T(8,128)(2,1)S(1)}, u32[]{:S(2)}, u32[]{:S(2)}) collective-permute-start(bf16[128,2688]{1,0:T(8,128)(2,1)S(1)} %constant_dynamic-slice_fusion.1), channel_id=1, source_target_pairs={{0,4},{2,6},{4,0},{6,2},{8,12},{10,14},{12,8},{14,10},{1,5},{3,7},... | collective-permute-start | bytes 2064392 | tf_op jit(solution)/shard_map/ppermute | solution.py:262
  5.0 45.0 %collective-permute-start.16 = (bf16[128,2688]{1,0:T(8,128)(2,1)S(1)}, bf16[128,2688]{1,0:T(8,128)(2,1)S(1)}, u32[]{:S(2)}, u32[]{:S(2)}) collective-permute-start(bf16[128,2688]{1,0:T(8,128)(2,1)S(1)} %constant_dynamic-slice_fusion.1), channel_id=1, source_target_pairs={{0,2},{2,0},{4,6},{6,4},{8,10},{10,8},{12,14},{14,12},{1,3},{3,1},... | collective-permute-start | bytes 2064392 | tf_op jit(solution)/shard_map/ppermute | solution.py:262
  9.4 14.4 %collective-permute-start.3 = (bf16[512,128]{1,0:T(8,128)(2,1)}, bf16[512,128]{1,0:T(8,128)(2,1)S(1)}, u32[]{:S(2)}, u32[]{:S(2)}) collective-permute-start(bf16[512,128]{1,0:T(8,128)(2,1)} %get-tuple-element.39), channel_id=1, source_target_pairs={{0,8},{2,10},{4,12},{6,14},{1,9},{3,11},{5,13},{7,15},{16,24},{18,... | collective-permute-start | bytes 393224 | tf_op jit(solution)/shard_map/ppermute | solution.py:270
  14.0 12.6 %collective-permute-start.4 = (bf16[512,128]{1,0:T(8,128)(2,1)}, bf16[512,128]{1,0:T(8,128)(2,1)S(1)}, u32[]{:S(2)}, u32[]{:S(2)}) collective-permute-start(bf16[512,128]{1,0:T(8,128)(2,1)} %get-tuple-element.40), channel_id=1, source_target_pairs={{0,10},{2,8},{4,14},{6,12},{1,11},{3,9},{5,15},{7,13},{16,26},{18,... | collective-permute-start | bytes 393224 | tf_op jit(solution)/shard_map/ppermute | solution.py:270
  15.3 14.1 %collective-permute-start.5 = (bf16[512,128]{1,0:T(8,128)(2,1)}, bf16[512,128]{1,0:T(8,128)(2,1)S(1)}, u32[]{:S(2)}, u32[]{:S(2)}) collective-permute-start(bf16[512,128]{1,0:T(8,128)(2,1)} %get-tuple-element.41), channel_id=1, source_target_pairs={{0,12},{2,14},{4,8},{6,10},{1,13},{3,15},{5,9},{7,11},{16,28},{18,... | collective-permute-start | bytes 393224 | tf_op jit(solution)/shard_map/ppermute | solution.py:270
  23.8 24.7 %collective-permute-start = (bf16[1536,128]{1,0:T(8,128)(2,1)}, bf16[1536,128]{1,0:T(8,128)(2,1)S(1)}, u32[]{:S(2)}, u32[]{:S(2)}) collective-permute-start(bf16[1536,128]{1,0:T(8,128)(2,1)} %get-tuple-element.36), channel_id=1, source_target_pairs={{0,2},{2,0},{4,6},{6,4},{8,10},{10,8},{12,14},{14,12},{1,3},{3,1},... | collective-permute-start | bytes 1179656 | tf_op jit(solution)/shard_map/ppermute | solution.py:262
  26.6 23.4 %collective-permute-start.1 = (bf16[1536,128]{1,0:T(8,128)(2,1)}, bf16[1536,128]{1,0:T(8,128)(2,1)S(1)}, u32[]{:S(2)}, u32[]{:S(2)}) collective-permute-start(bf16[1536,128]{1,0:T(8,128)(2,1)} %get-tuple-element.37), channel_id=1, source_target_pairs={{0,4},{2,6},{4,0},{6,2},{8,12},{10,14},{12,8},{14,10},{1,5},{3,7},... | collective-permute-start | bytes 1179656 | tf_op jit(solution)/shard_map/ppermute | solution.py:262
  29.4 21.1 %collective-permute-start.2 = (bf16[1536,128]{1,0:T(8,128)(2,1)}, bf16[1536,128]{1,0:T(8,128)(2,1)S(1)}, u32[]{:S(2)}, u32[]{:S(2)}) collective-permute-start(bf16[1536,128]{1,0:T(8,128)(2,1)} %get-tuple-element.38), channel_id=1, source_target_pairs={{0,6},{2,4},{4,2},{6,0},{8,14},{10,12},{12,10},{14,8},{1,7},{3,5},... | collective-permute-start | bytes 1179656 | tf_op jit(solution)/shard_map/ppermute | solution.py:262
  30.6 17.9 %collective-permute-start.6 = (bf16[512,128]{1,0:T(8,128)(2,1)}, bf16[512,128]{1,0:T(8,128)(2,1)S(1)}, u32[]{:S(2)}, u32[]{:S(2)}) collective-permute-start(bf16[512,128]{1,0:T(8,128)(2,1)} %get-tuple-element.42), channel_id=1, source_target_pairs={{0,14},{2,12},{4,10},{6,8},{1,15},{3,13},{5,11},{7,9},{16,30},{18,... | collective-permute-start | bytes 393224 | tf_op jit(solution)/shard_map/ppermute | solution.py:270
  48.5 11.3 %collective-permute-start.14 = (bf16[64,2688]{1,0:T(8,128)(2,1)S(1)}, bf16[64,2688]{1,0:T(8,128)(2,1)S(1)}, u32[]{:S(2)}, u32[]{:S(2)}) collective-permute-start(bf16[64,2688]{1,0:T(8,128)(2,1)S(1)} %constant_dynamic-slice_fusion), channel_id=1, source_target_pairs={{0,6},{2,4},{4,2},{6,0},{8,14},{10,12},{12,10},{14,8},{1,7},{3,5},... | collective-permute-start | bytes 1032200 | tf_op jit(solution)/shard_map/ppermute | solution.py:262
  48.5 15.8 %collective-permute-start.18 = (bf16[64,2688]{1,0:T(8,128)(2,1)S(1)}, bf16[64,2688]{1,0:T(8,128)(2,1)S(1)}, u32[]{:S(2)}, u32[]{:S(2)}) collective-permute-start(bf16[64,2688]{1,0:T(8,128)(2,1)S(1)} %slice.8), channel_id=1, source_target_pairs={{0,2},{2,0},{4,6},{6,4},{8,10},{10,8},{12,14},{14,12},{1,3},{3,1},... | collective-permute-start | bytes 1032200 | tf_op jit(solution)/shard_map/ppermute | solution.py:262
  50.0 39.5 %collective-permute-start.13 = (bf16[128,2688]{1,0:T(8,128)(2,1)S(1)}, bf16[128,2688]{1,0:T(8,128)(2,1)S(1)}, u32[]{:S(2)}, u32[]{:S(2)}) collective-permute-start(bf16[128,2688]{1,0:T(8,128)(2,1)S(1)} %collective-permute-done.12.refs_0_), channel_id=1, source_target_pairs={{0,1},{1,0},{2,3},{3,2},{4,5},{5,4},{6,7},{7,6},{8,9},{9,8},{10,11... | collective-permute-start | bytes 2064392 | tf_op jit(solution)/shard_map/ppermute | solution.py:273
  50.0 39.5 %collective-permute-start.17 = (bf16[128,2688]{1,0:T(8,128)(2,1)S(1)}, bf16[128,2688]{1,0:T(8,128)(2,1)S(1)}, u32[]{:S(2)}, u32[]{:S(2)}) collective-permute-start(bf16[128,2688]{1,0:T(8,128)(2,1)S(1)} %collective-permute-done.16.refs_4_), channel_id=1, source_target_pairs={{0,1},{1,0},{2,3},{3,2},{4,5},{5,4},{6,7},{7,6},{8,9},{9,8},{10,11... | collective-permute-start | bytes 2064392 | tf_op jit(solution)/shard_map/ppermute | solution.py:273
  58.5 27.8 %collective-permute-start.11 = (bf16[1024,128]{1,0:T(8,128)(2,1)S(1)}, bf16[1024,128]{1,0:T(8,128)(2,1)S(1)}, u32[]{:S(2)}, u32[]{:S(2)}) collective-permute-start(bf16[1024,128]{1,0:T(8,128)(2,1)S(1)} %get-tuple-element.51), channel_id=1, source_target_pairs={{8,0},{10,2},{12,4},{14,6},{9,1},{11,3},{13,5},{15,7},{24,16},{26,... | collective-permute-start | bytes 786440 | tf_op jit(solution)/shard_map/ppermute | solution.py:270
  59.8 28.1 %collective-permute-start.15 = (bf16[64,2688]{1,0:T(8,128)(2,1)S(1)}, bf16[64,2688]{1,0:T(8,128)(2,1)S(1)}, u32[]{:S(2)}, u32[]{:S(2)}) collective-permute-start(bf16[64,2688]{1,0:T(8,128)(2,1)S(1)} %collective-permute-done.14.refs_2_), channel_id=1, source_target_pairs={{0,1},{1,0},{2,3},{3,2},{4,5},{5,4},{6,7},{7,6},{8,9},{9,8},{10,11... | collective-permute-start | bytes 1032200 | tf_op jit(solution)/shard_map/ppermute | solution.py:273
  64.3 27.2 %collective-permute-start.19 = (bf16[64,2688]{1,0:T(8,128)(2,1)S(1)}, bf16[64,2688]{1,0:T(8,128)(2,1)S(1)}, u32[]{:S(2)}, u32[]{:S(2)}) collective-permute-start(bf16[64,2688]{1,0:T(8,128)(2,1)S(1)} %collective-permute-done.18.refs_6_), channel_id=1, source_target_pairs={{0,1},{1,0},{2,3},{3,2},{4,5},{5,4},{6,7},{7,6},{8,9},{9,8},{10,11... | collective-permute-start | bytes 1032200 | tf_op jit(solution)/shard_map/ppermute | solution.py:273
  86.3 11.7 %collective-permute-start.10 = (bf16[1024,128]{1,0:T(8,128)(2,1)S(1)}, bf16[1024,128]{1,0:T(8,128)(2,1)S(1)}, u32[]{:S(2)}, u32[]{:S(2)}) collective-permute-start(bf16[1024,128]{1,0:T(8,128)(2,1)S(1)} %get-tuple-element.49), channel_id=1, source_target_pairs={{8,0},{10,2},{12,4},{14,6},{9,1},{11,3},{13,5},{15,7},{24,16},{26,... | collective-permute-start | bytes 786440 | tf_op jit(solution)/shard_map/ppermute | solution.py:270
  87.9 11.2 %collective-permute-start.7 = (bf16[512,128]{1,0:T(8,128)(2,1)S(1)}, bf16[512,128]{1,0:T(8,128)(2,1)S(1)}, u32[]{:S(2)}, u32[]{:S(2)}) collective-permute-start(bf16[512,128]{1,0:T(8,128)(2,1)S(1)} %get-tuple-element.45), channel_id=1, source_target_pairs={{0,2},{2,0},{4,6},{6,4},{8,10},{10,8},{12,14},{14,12},{1,3},{3,1},... | collective-permute-start | bytes 393224 | tf_op jit(solution)/shard_map/ppermute | solution.py:262
  89.4 12.8 %collective-permute-start.8 = (bf16[512,128]{1,0:T(8,128)(2,1)S(1)}, bf16[512,128]{1,0:T(8,128)(2,1)S(1)}, u32[]{:S(2)}, u32[]{:S(2)}) collective-permute-start(bf16[512,128]{1,0:T(8,128)(2,1)S(1)} %get-tuple-element.46), channel_id=1, source_target_pairs={{0,4},{2,6},{4,0},{6,2},{8,12},{10,14},{12,8},{14,10},{1,5},{3,7},... | collective-permute-start | bytes 393224 | tf_op jit(solution)/shard_map/ppermute | solution.py:262
  89.4 18.2 %collective-permute-start.9 = (bf16[512,128]{1,0:T(8,128)(2,1)S(1)}, bf16[512,128]{1,0:T(8,128)(2,1)S(1)}, u32[]{:S(2)}, u32[]{:S(2)}) collective-permute-start(bf16[512,128]{1,0:T(8,128)(2,1)S(1)} %get-tuple-element.47), channel_id=1, source_target_pairs={{0,6},{2,4},{4,2},{6,0},{8,14},{10,12},{12,10},{14,8},{1,7},{3,5},... | collective-permute-start | bytes 393224 | tf_op jit(solution)/shard_map/ppermute | solution.py:262
  94.4 13.3 %collective-permute-start.23 = (bf16[336,128]{1,0:T(8,128)(2,1)S(1)}, bf16[336,128]{1,0:T(8,128)(2,1)S(1)}, u32[]{:S(2)}, u32[]{:S(2)}) collective-permute-start(bf16[336,128]{1,0:T(8,128)(2,1)S(1)} %get-tuple-element.60), channel_id=1, source_target_pairs={{0,8},{2,10},{4,12},{6,14},{8,0},{10,2},{12,4},{14,6},{1,9},{3,11}... | collective-permute-start | bytes 258056 | tf_op jit(solution)/shard_map/ppermute | solution.py:262
  98.0 9.7 %collective-permute-start.24 = (bf16[336,128]{1,0:T(8,128)(2,1)S(1)}, bf16[336,128]{1,0:T(8,128)(2,1)S(1)}, u32[]{:S(2)}, u32[]{:S(2)}) collective-permute-start(bf16[336,128]{1,0:T(8,128)(2,1)S(1)} %get-tuple-element.61), channel_id=1, source_target_pairs={{0,10},{2,8},{4,14},{6,12},{8,2},{10,0},{12,6},{14,4},{1,11},{3,9}... | collective-permute-start | bytes 258056 | tf_op jit(solution)/shard_map/ppermute | solution.py:262
  99.1 16.7 %collective-permute-start.20 = (bf16[592,128]{1,0:T(8,128)(2,1)S(1)}, bf16[592,128]{1,0:T(8,128)(2,1)S(1)}, u32[]{:S(2)}, u32[]{:S(2)}) collective-permute-start(bf16[592,128]{1,0:T(8,128)(2,1)S(1)} %get-tuple-element.57), channel_id=1, source_target_pairs={{0,2},{2,0},{4,6},{6,4},{8,10},{10,8},{12,14},{14,12},{1,3},{3,1},... | collective-permute-start | bytes 454664 | tf_op jit(solution)/shard_map/ppermute | solution.py:262
  102.2 13.6 %collective-permute-start.21 = (bf16[592,128]{1,0:T(8,128)(2,1)S(1)}, bf16[592,128]{1,0:T(8,128)(2,1)S(1)}, u32[]{:S(2)}, u32[]{:S(2)}) collective-permute-start(bf16[592,128]{1,0:T(8,128)(2,1)S(1)} %get-tuple-element.58), channel_id=1, source_target_pairs={{0,4},{2,6},{4,0},{6,2},{8,12},{10,14},{12,8},{14,10},{1,5},{3,7},... | collective-permute-start | bytes 454664 | tf_op jit(solution)/shard_map/ppermute | solution.py:262
  (5 other events, 101.7 us)

commit v5 on v4

--- a/solution.py
+++ b/solution.py
@@ -233,20 +233,26 @@
             outs[slot][rows:, :] = terms[slot][...]
 
 
-def spread_kernel(parts, *refs):
-    dq, dv = refs[:parts], refs[parts : 2 * parts]
-    outs = refs[-3:] if len(refs) > 2 * parts + 2 else refs[-2:]
-    terms = refs[2 * parts : -len(outs)]
-    rows = outs[0].shape[0]
+def query_kernel(parts, *refs):
+    out = refs[-1]
+    rows = out.shape[0]
     for slot in range(parts):
         head = place_of(parts) ^ slot
         for g in range(GROUP):
             at = pl.ds(pl.multiple_of((head * GROUP + g) * HD, HD), HD)
-            outs[0][:, at] = dq[slot][g * rows : (g + 1) * rows, :]
+            out[:, at] = refs[slot][g * rows : (g + 1) * rows, :]
+
+
+def spread_kernel(parts, rows, *refs):
+    dv = refs[:parts]
+    outs = refs[-2:] if len(refs) > parts + 1 else refs[-1:]
+    terms = refs[parts : -len(outs)]
+    for slot in range(parts):
+        head = place_of(parts) ^ slot
         at = pl.ds(pl.multiple_of(head * HD, HD), HD)
-        outs[1][:, at] = dv[slot][:rows, :]
+        outs[0][:, at] = dv[slot][:rows, :]
         if terms:
-            outs[2][:, at] = dv[slot][rows:, :].astype(jnp.float32) + terms[slot][...].astype(jnp.float32)
+            outs[1][:, at] = dv[slot][rows:, :].astype(jnp.float32) + terms[slot][...].astype(jnp.float32)
 
 
 def shards(normed_input, attn_queries, attn_keys, attn_values, out_grad):
@@ -366,17 +372,19 @@
     )(own_v, got_v, *near_terms)
     got_dv = exchanged(dv_parts)
 
+    query_grad = call(
+        functools.partial(query_kernel, parts), shape((rows, parts * GROUP * HD)), [VMEM] * parts, VMEM, moved=1 << 20
+    )(*got_dq)
     outs = call(
-        functools.partial(spread_kernel, parts),
-        [shape((rows, parts * GROUP * HD)), shape((rows, parts * HD))]
-        + ([shape((piece, parts * HD), jnp.float32)] if direct else []),
-        [VMEM] * (2 * parts + len(got_terms)),
-        [VMEM] * (3 if direct else 2),
-        moved=3 << 20,
-    )(*got_dq, *got_dv, *got_terms)
-    query_grad, value_grad = outs[:2]
+        functools.partial(spread_kernel, parts, rows),
+        [shape((rows, parts * HD))] + ([shape((piece, parts * HD), jnp.float32)] if direct else []),
+        [VMEM] * (parts + len(got_terms)),
+        [VMEM] * (2 if direct else 1),
+        moved=2 << 20,
+    )(*got_dv, *got_terms)
+    value_grad = outs[0]
     if direct:
-        weight_grad = outs[2]
+        weight_grad = outs[1]
     else:
         pieces = terms[0].reshape(count, piece, HD)
         pieces = lax.all_to_all(pieces, "ctx", split_axis=0, concat_axis=0, tiled=True)

time: 119 us -> 119 us (level)
  transfers between devices with their start and end apart: 27 -> 27, of which waited for: 11 -> 11; matrix products, arithmetic and copies ran while one was open for 0% -> 0% of each run, Pallas kernels for 12% -> 13%
where the time goes in v5:
time: 119 us; the launch traced here: 118 us
  waiting for transfers between devices  61.8 us (52%)
  starting transfers between devices  38.6 us (32%)
  Pallas kernels  15.9 us (13%)
  local copies, waits for them, and re-layouts  1.33 us (1%)
    ppermute x6, waiting for transfers between devices, across(): return lax.ppermute(value, 'ctx', perm)  44.6 us
    ppermute x17, starting transfers between devices, within(): return lax.ppermute(value, 'ctx', [(s, s ^ slot) for s in range(count)])  21.3 us
    ppermute x17, waiting for transfers between devices, within(): return lax.ppermute(value, 'ctx', [(s, s ^ slot) for s in range(count)])  17.2 us
    ppermute x6, starting transfers between devices, across(): return lax.ppermute(value, 'ctx', perm)  16.6 us
    pallas_call x1, Pallas kernels, shards(): call(functools.partial(attention_kernel, parts, rows), [shape((parts * wi...  7.95 us
    pallas_call x1, Pallas kernels, shards(): call(functools.partial(weight_kernel, parts, count, rows, spots), [shape(...  2.95 us
    pallas_call x1, Pallas kernels, pack(): call(functools.partial(pack_kernel, parts, slots, crosses), [shape(dims)...  2.84 us
  transfers between devices with their start and end apart: 27, of which 11 were waited for; matrix products, arithmetic and copies ran while one was open for 0% of the time, Pallas kernels for 13%

profile of v5, /device:TPU:0, one launch (start us, length us, event | category | flops | bytes accessed | tf_op | source)
XLA Modules:
  0.0 118.4 jit_solution(8708513180479978215)
XLA Ops:
  1.9 3.1 %collective-permute-start.12 = (bf16[128,2688]{1,0:T(8,128)(2,1)S(1)}, bf16[128,2688]{1,0:T(8,128)(2,1)S(1)}, u32[]{:S(2)}, u32[]{:S(2)}) collective-permute-start(bf16[128,2688]{1,0:T(8,128)(2,1)S(1)} %constant_dynamic-slice_fusion.1), channel_id=1, source_target_pairs={{0,4},{2,6},{4,0},{6,2},{8,12},{10,14},{12,8},{14,10},{1,5},{3,7},... | collective-permute-start | bytes 2064392 | tf_op jit(solution)/shard_map/ppermute | solution.py:268
  5.0 1.5 %collective-permute-start.16 = (bf16[128,2688]{1,0:T(8,128)(2,1)S(1)}, bf16[128,2688]{1,0:T(8,128)(2,1)S(1)}, u32[]{:S(2)}, u32[]{:S(2)}) collective-permute-start(bf16[128,2688]{1,0:T(8,128)(2,1)S(1)} %constant_dynamic-slice_fusion.1), channel_id=1, source_target_pairs={{0,2},{2,0},{4,6},{6,4},{8,10},{10,8},{12,14},{14,12},{1,3},{3,1},... | collective-permute-start | bytes 2064392 | tf_op jit(solution)/shard_map/ppermute | solution.py:268
  6.5 2.8 %shard_map.76 = (bf16[1536,128]{1,0:T(8,128)(2,1)}, bf16[1536,128]{1,0:T(8,128)(2,1)}, bf16[1536,128]{1,0:T(8,128)(2,1)}, bf16[1536,128]{1,0:T(8,128)(2,1)}, bf1...) custom-call(bf16[256,1024]{1,0:T(8,128)(2,1)} %q_ref.1, ...), custom_call_target="tpu_custom_call" | custom-call | bytes 2097152 | tf_op jit(solution)/shard_map/pallas_call | solution.py:286
  9.4 4.6 %collective-permute-start.3 = (bf16[512,128]{1,0:T(8,128)(2,1)}, bf16[512,128]{1,0:T(8,128)(2,1)S(1)}, u32[]{:S(2)}, u32[]{:S(2)}) collective-permute-start(bf16[512,128]{1,0:T(8,128)(2,1)} %get-tuple-element.38), channel_id=1, source_target_pairs={{0,8},{2,10},{4,12},{6,14},{1,9},{3,11},{5,13},{7,15},{16,24},{18,... | collective-permute-start | bytes 393224 | tf_op jit(solution)/shard_map/ppermute | solution.py:276
  16.6 7.2 %collective-permute-done.3.refs_4_ = bf16[512,128]{1,0:T(8,128)(2,1)S(1)} collective-permute-done((bf16[512,128]{1,0:T(8,128)(2,1)}, bf16[512,128]{1,0:T(8,128)(2,1)S(1)}, u32[]{:S(2)}, u32[]{:S(2)}) %collective-permute-start.3) | collective-permute-done | bytes 131104 | tf_op jit(solution)/shard_map/ppermute | solution.py:276
  23.8 1.5 %collective-permute-start = (bf16[1536,128]{1,0:T(8,128)(2,1)}, bf16[1536,128]{1,0:T(8,128)(2,1)S(1)}, u32[]{:S(2)}, u32[]{:S(2)}) collective-permute-start(bf16[1536,128]{1,0:T(8,128)(2,1)} %get-tuple-element.35), channel_id=1, source_target_pairs={{0,2},{2,0},{4,6},{6,4},{8,10},{10,8},{12,14},{14,12},{1,3},{3,1},... | collective-permute-start | bytes 1179656 | tf_op jit(solution)/shard_map/ppermute | solution.py:268
  26.6 2.8 %collective-permute-done.5.refs_6_ = bf16[512,128]{1,0:T(8,128)(2,1)S(1)} collective-permute-done((bf16[512,128]{1,0:T(8,128)(2,1)}, bf16[512,128]{1,0:T(8,128)(2,1)S(1)}, u32[]{:S(2)}, u32[]{:S(2)}) %collective-permute-start.5) | collective-permute-done | bytes 131104 | tf_op jit(solution)/shard_map/ppermute | solution.py:276
  30.6 6.6 %collective-permute-start.6 = (bf16[512,128]{1,0:T(8,128)(2,1)}, bf16[512,128]{1,0:T(8,128)(2,1)S(1)}, u32[]{:S(2)}, u32[]{:S(2)}) collective-permute-start(bf16[512,128]{1,0:T(8,128)(2,1)} %get-tuple-element.41), channel_id=1, source_target_pairs={{0,14},{2,12},{4,10},{6,8},{1,15},{3,13},{5,11},{7,9},{16,30},{18,... | collective-permute-start | bytes 393224 | tf_op jit(solution)/shard_map/ppermute | solution.py:276
  37.2 11.3 %collective-permute-done.6.refs_7_ = bf16[512,128]{1,0:T(8,128)(2,1)S(1)} collective-permute-done((bf16[512,128]{1,0:T(8,128)(2,1)}, bf16[512,128]{1,0:T(8,128)(2,1)S(1)}, u32[]{:S(2)}, u32[]{:S(2)}) %collective-permute-start.6) | collective-permute-done | bytes 131104 | tf_op jit(solution)/shard_map/ppermute | solution.py:276
  48.5 1.5 %collective-permute-start.18 = (bf16[64,2688]{1,0:T(8,128)(2,1)S(1)}, bf16[64,2688]{1,0:T(8,128)(2,1)S(1)}, u32[]{:S(2)}, u32[]{:S(2)}) collective-permute-start(bf16[64,2688]{1,0:T(8,128)(2,1)S(1)} %slice.8), channel_id=1, source_target_pairs={{0,2},{2,0},{4,6},{6,4},{8,10},{10,8},{12,14},{14,12},{1,3},{3,1},... | collective-permute-start | bytes 1032200 | tf_op jit(solution)/shard_map/ppermute | solution.py:268
  50.5 8.0 %shard_map.77 = (bf16[2048,128]{1,0:T(8,128)(2,1)S(1)}, bf16[1024,128]{1,0:T(8,128)(2,1)S(1)}, bf16[1024,128]{1,0:T(8,128)(2,1)S(1)}, f32[1024,128]{1,0:T(8,128)S(1)}, f32[1024,128]{1,0:T(8,128)S(1)}) custom-call(bf16[1536,128]{1,0:T(8,128)(2,1)S(1)} %copy-done.1, bf16[1536,128]{1,0:T(8,128)(2,1)S(1)} %collective-permute-done.refs_1_, ...), custom_call_target="tpu_custom_call" | custom-call | flops 3355443200 | bytes 4194304 | tf_op jit(solution)/shard_map/pallas_call | solution.py:315
  59.9 4.4 %collective-permute-done.18.refs_6_ = bf16[64,2688]{1,0:T(8,128)(2,1)S(1)} collective-permute-done((bf16[64,2688]{1,0:T(8,128)(2,1)S(1)}, bf16[64,2688]{1,0:T(8,128)(2,1)S(1)}, u32[]{:S(2)}, u32[]{:S(2)}) %collective-permute-start.18) | collective-permute-done | bytes 344096 | tf_op jit(solution)/shard_map/ppermute | solution.py:268
  64.3 22.0 %collective-permute-done.11.back_k = bf16[1024,128]{1,0:T(8,128)(2,1)S(1)} collective-permute-done((bf16[1024,128]{1,0:T(8,128)(2,1)S(1)}, bf16[1024,128]{1,0:T(8,128)(2,1)S(1)}, u32[]{:S(2)}, u32[]{:S(2)}) %collective-permute-start.11) | collective-permute-done | bytes 262176 | tf_op jit(solution)/shard_map/ppermute | solution.py:276
  86.3 1.5 %collective-permute-start.10 = (bf16[1024,128]{1,0:T(8,128)(2,1)S(1)}, bf16[1024,128]{1,0:T(8,128)(2,1)S(1)}, u32[]{:S(2)}, u32[]{:S(2)}) collective-permute-start(bf16[1024,128]{1,0:T(8,128)(2,1)S(1)} %get-tuple-element.48), channel_id=1, source_target_pairs={{8,0},{10,2},{12,4},{14,6},{9,1},{11,3},{13,5},{15,7},{24,16},{26,... | collective-permute-start | bytes 786440 | tf_op jit(solution)/shard_map/ppermute | solution.py:276
  87.9 1.6 %collective-permute-start.7 = (bf16[512,128]{1,0:T(8,128)(2,1)S(1)}, bf16[512,128]{1,0:T(8,128)(2,1)S(1)}, u32[]{:S(2)}, u32[]{:S(2)}) collective-permute-start(bf16[512,128]{1,0:T(8,128)(2,1)S(1)} %get-tuple-element.44), channel_id=1, source_target_pairs={{0,2},{2,0},{4,6},{6,4},{8,10},{10,8},{12,14},{14,12},{1,3},{3,1},... | collective-permute-start | bytes 393224 | tf_op jit(solution)/shard_map/ppermute | solution.py:268
  89.4 2.0 %collective-permute-start.9 = (bf16[512,128]{1,0:T(8,128)(2,1)S(1)}, bf16[512,128]{1,0:T(8,128)(2,1)S(1)}, u32[]{:S(2)}, u32[]{:S(2)}) collective-permute-start(bf16[512,128]{1,0:T(8,128)(2,1)S(1)} %get-tuple-element.46), channel_id=1, source_target_pairs={{0,6},{2,4},{4,2},{6,0},{8,14},{10,12},{12,10},{14,8},{1,7},{3,5},... | collective-permute-start | bytes 393224 | tf_op jit(solution)/shard_map/ppermute | solution.py:268
  91.4 3.0 %shard_map.80 = (bf16[336,128]{1,0:T(8,128)(2,1)S(1)}, bf16[336,128]{1,0:T(8,128)(2,1)S(1)}, bf16[336,128]{1,0:T(8,128)(2,1)S(1)}, bf16[336,128]{1,0:T(8,128)(2,...) custom-call(f32[1024,128]{1,0:T(8,128)S(1)} %get-tuple-element.49.ow, ...), custom_call_target="tpu_custom_call" | custom-call | flops 704643072 | bytes 8388608 | tf_op jit(solution)/shard_map/pallas_call | solution.py:349
  94.4 3.6 %collective-permute-start.23 = (bf16[336,128]{1,0:T(8,128)(2,1)S(1)}, bf16[336,128]{1,0:T(8,128)(2,1)S(1)}, u32[]{:S(2)}, u32[]{:S(2)}) collective-permute-start(bf16[336,128]{1,0:T(8,128)(2,1)S(1)} %get-tuple-element.59), channel_id=1, source_target_pairs={{0,8},{2,10},{4,12},{6,14},{8,0},{10,2},{12,4},{14,6},{1,9},{3,11}... | collective-permute-start | bytes 258056 | tf_op jit(solution)/shard_map/ppermute | solution.py:268
  99.7 2.5 %collective-permute-done.8.refs_2_ = bf16[512,128]{1,0:T(8,128)(2,1)S(1)} collective-permute-done((bf16[512,128]{1,0:T(8,128)(2,1)S(1)}, bf16[512,128]{1,0:T(8,128)(2,1)S(1)}, u32[]{:S(2)}, u32[]{:S(2)}) %collective-permute-start.8) | collective-permute-done | bytes 131104 | tf_op jit(solution)/shard_map/ppermute | solution.py:268
  102.2 5.4 %collective-permute-done.9.refs_3_ = bf16[512,128]{1,0:T(8,128)(2,1)S(1)} collective-permute-done((bf16[512,128]{1,0:T(8,128)(2,1)S(1)}, bf16[512,128]{1,0:T(8,128)(2,1)S(1)}, u32[]{:S(2)}, u32[]{:S(2)}) %collective-permute-start.9) | collective-permute-done | bytes 131104 | tf_op jit(solution)/shard_map/ppermute | solution.py:268
  107.7 3.8 %collective-permute-start.26 = (bf16[336,128]{1,0:T(8,128)(2,1)S(1)}, bf16[336,128]{1,0:T(8,128)(2,1)S(1)}, u32[]{:S(2)}, u32[]{:S(2)}) collective-permute-start(bf16[336,128]{1,0:T(8,128)(2,1)S(1)} %get-tuple-element.62), channel_id=1, source_target_pairs={{0,14},{2,12},{4,10},{6,8},{8,6},{10,4},{12,2},{14,0},{1,15},{3,13... | collective-permute-start | bytes 258056 | tf_op jit(solution)/shard_map/ppermute | solution.py:268
  112.5 1.6 %collective-permute-done.25.refs_6_ = bf16[336,128]{1,0:T(8,128)(2,1)S(1)} collective-permute-done((bf16[336,128]{1,0:T(8,128)(2,1)S(1)}, bf16[336,128]{1,0:T(8,128)(2,1)S(1)}, u32[]{:S(2)}, u32[]{:S(2)}) %collective-permute-start.25) | collective-permute-done | bytes 86048 | tf_op jit(solution)/shard_map/ppermute | solution.py:268
  114.0 1.8 %collective-permute-done.26.refs_7_ = bf16[336,128]{1,0:T(8,128)(2,1)S(1)} collective-permute-done((bf16[336,128]{1,0:T(8,128)(2,1)S(1)}, bf16[336,128]{1,0:T(8,128)(2,1)S(1)}, u32[]{:S(2)}, u32[]{:S(2)}) %collective-permute-start.26) | collective-permute-done | bytes 86048 | tf_op jit(solution)/shard_map/ppermute | solution.py:268
  115.8 1.5 %collective-permute-done.22.refs_3_ = bf16[592,128]{1,0:T(8,128)(2,1)S(1)} collective-permute-done((bf16[592,128]{1,0:T(8,128)(2,1)S(1)}, bf16[592,128]{1,0:T(8,128)(2,1)S(1)}, u32[]{:S(2)}, u32[]{:S(2)}) %collective-permute-start.22) | collective-permute-done | bytes 151584 | tf_op jit(solution)/shard_map/ppermute | solution.py:268
  (44 shorter events, 12.1 us)
Async XLA Ops:
  1.9 28.6 %collective-permute-start.12 = (bf16[128,2688]{1,0:T(8,128)(2,1)S(1)}, bf16[128,2688]{1,0:T(8,128)(2,1)S(1)}, u32[]{:S(2)}, u32[]{:S(2)}) collective-permute-start(bf16[128,2688]{1,0:T(8,128)(2,1)S(1)} %constant_dynamic-slice_fusion.1), channel_id=1, source_target_pairs={{0,4},{2,6},{4,0},{6,2},{8,12},{10,14},{12,8},{14,10},{1,5},{3,7},... | collective-permute-start | bytes 2064392 | tf_op jit(solution)/shard_map/ppermute | solution.py:268
  5.0 45.0 %collective-permute-start.16 = (bf16[128,2688]{1,0:T(8,128)(2,1)S(1)}, bf16[128,2688]{1,0:T(8,128)(2,1)S(1)}, u32[]{:S(2)}, u32[]{:S(2)}) collective-permute-start(bf16[128,2688]{1,0:T(8,128)(2,1)S(1)} %constant_dynamic-slice_fusion.1), channel_id=1, source_target_pairs={{0,2},{2,0},{4,6},{6,4},{8,10},{10,8},{12,14},{14,12},{1,3},{3,1},... | collective-permute-start | bytes 2064392 | tf_op jit(solution)/shard_map/ppermute | solution.py:268
  9.4 14.4 %collective-permute-start.3 = (bf16[512,128]{1,0:T(8,128)(2,1)}, bf16[512,128]{1,0:T(8,128)(2,1)S(1)}, u32[]{:S(2)}, u32[]{:S(2)}) collective-permute-start(bf16[512,128]{1,0:T(8,128)(2,1)} %get-tuple-element.38), channel_id=1, source_target_pairs={{0,8},{2,10},{4,12},{6,14},{1,9},{3,11},{5,13},{7,15},{16,24},{18,... | collective-permute-start | bytes 393224 | tf_op jit(solution)/shard_map/ppermute | solution.py:276
  14.0 12.6 %collective-permute-start.4 = (bf16[512,128]{1,0:T(8,128)(2,1)}, bf16[512,128]{1,0:T(8,128)(2,1)S(1)}, u32[]{:S(2)}, u32[]{:S(2)}) collective-permute-start(bf16[512,128]{1,0:T(8,128)(2,1)} %get-tuple-element.39), channel_id=1, source_target_pairs={{0,10},{2,8},{4,14},{6,12},{1,11},{3,9},{5,15},{7,13},{16,26},{18,... | collective-permute-start | bytes 393224 | tf_op jit(solution)/shard_map/ppermute | solution.py:276
  15.3 14.1 %collective-permute-start.5 = (bf16[512,128]{1,0:T(8,128)(2,1)}, bf16[512,128]{1,0:T(8,128)(2,1)S(1)}, u32[]{:S(2)}, u32[]{:S(2)}) collective-permute-start(bf16[512,128]{1,0:T(8,128)(2,1)} %get-tuple-element.40), channel_id=1, source_target_pairs={{0,12},{2,14},{4,8},{6,10},{1,13},{3,15},{5,9},{7,11},{16,28},{18,... | collective-permute-start | bytes 393224 | tf_op jit(solution)/shard_map/ppermute | solution.py:276
  23.8 24.7 %collective-permute-start = (bf16[1536,128]{1,0:T(8,128)(2,1)}, bf16[1536,128]{1,0:T(8,128)(2,1)S(1)}, u32[]{:S(2)}, u32[]{:S(2)}) collective-permute-start(bf16[1536,128]{1,0:T(8,128)(2,1)} %get-tuple-element.35), channel_id=1, source_target_pairs={{0,2},{2,0},{4,6},{6,4},{8,10},{10,8},{12,14},{14,12},{1,3},{3,1},... | collective-permute-start | bytes 1179656 | tf_op jit(solution)/shard_map/ppermute | solution.py:268
  26.6 23.4 %collective-permute-start.1 = (bf16[1536,128]{1,0:T(8,128)(2,1)}, bf16[1536,128]{1,0:T(8,128)(2,1)S(1)}, u32[]{:S(2)}, u32[]{:S(2)}) collective-permute-start(bf16[1536,128]{1,0:T(8,128)(2,1)} %get-tuple-element.36), channel_id=1, source_target_pairs={{0,4},{2,6},{4,0},{6,2},{8,12},{10,14},{12,8},{14,10},{1,5},{3,7},... | collective-permute-start | bytes 1179656 | tf_op jit(solution)/shard_map/ppermute | solution.py:268
  29.4 21.1 %collective-permute-start.2 = (bf16[1536,128]{1,0:T(8,128)(2,1)}, bf16[1536,128]{1,0:T(8,128)(2,1)S(1)}, u32[]{:S(2)}, u32[]{:S(2)}) collective-permute-start(bf16[1536,128]{1,0:T(8,128)(2,1)} %get-tuple-element.37), channel_id=1, source_target_pairs={{0,6},{2,4},{4,2},{6,0},{8,14},{10,12},{12,10},{14,8},{1,7},{3,5},... | collective-permute-start | bytes 1179656 | tf_op jit(solution)/shard_map/ppermute | solution.py:268
  30.6 17.9 %collective-permute-start.6 = (bf16[512,128]{1,0:T(8,128)(2,1)}, bf16[512,128]{1,0:T(8,128)(2,1)S(1)}, u32[]{:S(2)}, u32[]{:S(2)}) collective-permute-start(bf16[512,128]{1,0:T(8,128)(2,1)} %get-tuple-element.41), channel_id=1, source_target_pairs={{0,14},{2,12},{4,10},{6,8},{1,15},{3,13},{5,11},{7,9},{16,30},{18,... | collective-permute-start | bytes 393224 | tf_op jit(solution)/shard_map/ppermute | solution.py:276
  48.5 11.3 %collective-permute-start.14 = (bf16[64,2688]{1,0:T(8,128)(2,1)S(1)}, bf16[64,2688]{1,0:T(8,128)(2,1)S(1)}, u32[]{:S(2)}, u32[]{:S(2)}) collective-permute-start(bf16[64,2688]{1,0:T(8,128)(2,1)S(1)} %constant_dynamic-slice_fusion), channel_id=1, source_target_pairs={{0,6},{2,4},{4,2},{6,0},{8,14},{10,12},{12,10},{14,8},{1,7},{3,5},... | collective-permute-start | bytes 1032200 | tf_op jit(solution)/shard_map/ppermute | solution.py:268
  48.5 15.8 %collective-permute-start.18 = (bf16[64,2688]{1,0:T(8,128)(2,1)S(1)}, bf16[64,2688]{1,0:T(8,128)(2,1)S(1)}, u32[]{:S(2)}, u32[]{:S(2)}) collective-permute-start(bf16[64,2688]{1,0:T(8,128)(2,1)S(1)} %slice.8), channel_id=1, source_target_pairs={{0,2},{2,0},{4,6},{6,4},{8,10},{10,8},{12,14},{14,12},{1,3},{3,1},... | collective-permute-start | bytes 1032200 | tf_op jit(solution)/shard_map/ppermute | solution.py:268
  50.0 39.5 %collective-permute-start.13 = (bf16[128,2688]{1,0:T(8,128)(2,1)S(1)}, bf16[128,2688]{1,0:T(8,128)(2,1)S(1)}, u32[]{:S(2)}, u32[]{:S(2)}) collective-permute-start(bf16[128,2688]{1,0:T(8,128)(2,1)S(1)} %collective-permute-done.12.refs_0_), channel_id=1, source_target_pairs={{0,1},{1,0},{2,3},{3,2},{4,5},{5,4},{6,7},{7,6},{8,9},{9,8},{10,11... | collective-permute-start | bytes 2064392 | tf_op jit(solution)/shard_map/ppermute | solution.py:279
  50.0 39.5 %collective-permute-start.17 = (bf16[128,2688]{1,0:T(8,128)(2,1)S(1)}, bf16[128,2688]{1,0:T(8,128)(2,1)S(1)}, u32[]{:S(2)}, u32[]{:S(2)}) collective-permute-start(bf16[128,2688]{1,0:T(8,128)(2,1)S(1)} %collective-permute-done.16.refs_4_), channel_id=1, source_target_pairs={{0,1},{1,0},{2,3},{3,2},{4,5},{5,4},{6,7},{7,6},{8,9},{9,8},{10,11... | collective-permute-start | bytes 2064392 | tf_op jit(solution)/shard_map/ppermute | solution.py:279
  58.5 27.8 %collective-permute-start.11 = (bf16[1024,128]{1,0:T(8,128)(2,1)S(1)}, bf16[1024,128]{1,0:T(8,128)(2,1)S(1)}, u32[]{:S(2)}, u32[]{:S(2)}) collective-permute-start(bf16[1024,128]{1,0:T(8,128)(2,1)S(1)} %get-tuple-element.50), channel_id=1, source_target_pairs={{8,0},{10,2},{12,4},{14,6},{9,1},{11,3},{13,5},{15,7},{24,16},{26,... | collective-permute-start | bytes 786440 | tf_op jit(solution)/shard_map/ppermute | solution.py:276
  59.8 28.1 %collective-permute-start.15 = (bf16[64,2688]{1,0:T(8,128)(2,1)S(1)}, bf16[64,2688]{1,0:T(8,128)(2,1)S(1)}, u32[]{:S(2)}, u32[]{:S(2)}) collective-permute-start(bf16[64,2688]{1,0:T(8,128)(2,1)S(1)} %collective-permute-done.14.refs_2_), channel_id=1, source_target_pairs={{0,1},{1,0},{2,3},{3,2},{4,5},{5,4},{6,7},{7,6},{8,9},{9,8},{10,11... | collective-permute-start | bytes 1032200 | tf_op jit(solution)/shard_map/ppermute | solution.py:279
  64.3 27.2 %collective-permute-start.19 = (bf16[64,2688]{1,0:T(8,128)(2,1)S(1)}, bf16[64,2688]{1,0:T(8,128)(2,1)S(1)}, u32[]{:S(2)}, u32[]{:S(2)}) collective-permute-start(bf16[64,2688]{1,0:T(8,128)(2,1)S(1)} %collective-permute-done.18.refs_6_), channel_id=1, source_target_pairs={{0,1},{1,0},{2,3},{3,2},{4,5},{5,4},{6,7},{7,6},{8,9},{9,8},{10,11... | collective-permute-start | bytes 1032200 | tf_op jit(solution)/shard_map/ppermute | solution.py:279
  86.3 11.7 %collective-permute-start.10 = (bf16[1024,128]{1,0:T(8,128)(2,1)S(1)}, bf16[1024,128]{1,0:T(8,128)(2,1)S(1)}, u32[]{:S(2)}, u32[]{:S(2)}) collective-permute-start(bf16[1024,128]{1,0:T(8,128)(2,1)S(1)} %get-tuple-element.48), channel_id=1, source_target_pairs={{8,0},{10,2},{12,4},{14,6},{9,1},{11,3},{13,5},{15,7},{24,16},{26,... | collective-permute-start | bytes 786440 | tf_op jit(solution)/shard_map/ppermute | solution.py:276
  87.9 11.2 %collective-permute-start.7 = (bf16[512,128]{1,0:T(8,128)(2,1)S(1)}, bf16[512,128]{1,0:T(8,128)(2,1)S(1)}, u32[]{:S(2)}, u32[]{:S(2)}) collective-permute-start(bf16[512,128]{1,0:T(8,128)(2,1)S(1)} %get-tuple-element.44), channel_id=1, source_target_pairs={{0,2},{2,0},{4,6},{6,4},{8,10},{10,8},{12,14},{14,12},{1,3},{3,1},... | collective-permute-start | bytes 393224 | tf_op jit(solution)/shard_map/ppermute | solution.py:268
  89.4 12.8 %collective-permute-start.8 = (bf16[512,128]{1,0:T(8,128)(2,1)S(1)}, bf16[512,128]{1,0:T(8,128)(2,1)S(1)}, u32[]{:S(2)}, u32[]{:S(2)}) collective-permute-start(bf16[512,128]{1,0:T(8,128)(2,1)S(1)} %get-tuple-element.45), channel_id=1, source_target_pairs={{0,4},{2,6},{4,0},{6,2},{8,12},{10,14},{12,8},{14,10},{1,5},{3,7},... | collective-permute-start | bytes 393224 | tf_op jit(solution)/shard_map/ppermute | solution.py:268
  89.4 18.2 %collective-permute-start.9 = (bf16[512,128]{1,0:T(8,128)(2,1)S(1)}, bf16[512,128]{1,0:T(8,128)(2,1)S(1)}, u32[]{:S(2)}, u32[]{:S(2)}) collective-permute-start(bf16[512,128]{1,0:T(8,128)(2,1)S(1)} %get-tuple-element.46), channel_id=1, source_target_pairs={{0,6},{2,4},{4,2},{6,0},{8,14},{10,12},{12,10},{14,8},{1,7},{3,5},... | collective-permute-start | bytes 393224 | tf_op jit(solution)/shard_map/ppermute | solution.py:268
  94.4 13.3 %collective-permute-start.23 = (bf16[336,128]{1,0:T(8,128)(2,1)S(1)}, bf16[336,128]{1,0:T(8,128)(2,1)S(1)}, u32[]{:S(2)}, u32[]{:S(2)}) collective-permute-start(bf16[336,128]{1,0:T(8,128)(2,1)S(1)} %get-tuple-element.59), channel_id=1, source_target_pairs={{0,8},{2,10},{4,12},{6,14},{8,0},{10,2},{12,4},{14,6},{1,9},{3,11}... | collective-permute-start | bytes 258056 | tf_op jit(solution)/shard_map/ppermute | solution.py:268
  98.0 9.7 %collective-permute-start.24 = (bf16[336,128]{1,0:T(8,128)(2,1)S(1)}, bf16[336,128]{1,0:T(8,128)(2,1)S(1)}, u32[]{:S(2)}, u32[]{:S(2)}) collective-permute-start(bf16[336,128]{1,0:T(8,128)(2,1)S(1)} %get-tuple-element.60), channel_id=1, source_target_pairs={{0,10},{2,8},{4,14},{6,12},{8,2},{10,0},{12,6},{14,4},{1,11},{3,9}... | collective-permute-start | bytes 258056 | tf_op jit(solution)/shard_map/ppermute | solution.py:268
  99.1 16.7 %collective-permute-start.20 = (bf16[592,128]{1,0:T(8,128)(2,1)S(1)}, bf16[592,128]{1,0:T(8,128)(2,1)S(1)}, u32[]{:S(2)}, u32[]{:S(2)}) collective-permute-start(bf16[592,128]{1,0:T(8,128)(2,1)S(1)} %get-tuple-element.56), channel_id=1, source_target_pairs={{0,2},{2,0},{4,6},{6,4},{8,10},{10,8},{12,14},{14,12},{1,3},{3,1},... | collective-permute-start | bytes 454664 | tf_op jit(solution)/shard_map/ppermute | solution.py:268
  102.2 13.6 %collective-permute-start.21 = (bf16[592,128]{1,0:T(8,128)(2,1)S(1)}, bf16[592,128]{1,0:T(8,128)(2,1)S(1)}, u32[]{:S(2)}, u32[]{:S(2)}) collective-permute-start(bf16[592,128]{1,0:T(8,128)(2,1)S(1)} %get-tuple-element.57), channel_id=1, source_target_pairs={{0,4},{2,6},{4,0},{6,2},{8,12},{10,14},{12,8},{14,10},{1,5},{3,7},... | collective-permute-start | bytes 454664 | tf_op jit(solution)/shard_map/ppermute | solution.py:268
  (5 other events, 101.7 us)
